TPU v7x, 32 devices: a whole 2x2x4 slice. The times are simulated.
32 devices in a mesh: dp: 8 (over z, x), fsdp: 4 (over y, core).
Axes of the slice: x: 2, y: 2, z: 4, core: 2. Of those that a mesh axis runs over, the one named last changes fastest.
Arguments:
- tokens: bfloat16 [16384, 768], P(('dp', 'fsdp')), may hold values from -6 to 6
- cotangent: bfloat16 [16384, 768], P(('dp', 'fsdp')), may hold values from -6 to 6
- lengths: int32 [32], P(('dp', 'fsdp')), may hold values from 128 to 512
- rel_1d: int32 [32, 512, 512], P(('dp', 'fsdp')), may hold values from 0 to 31
- rel_x: int32 [32, 512, 512], P(('dp', 'fsdp')), may hold values from 0 to 63
- rel_y: int32 [32, 512, 512], P(('dp', 'fsdp')), may hold values from 0 to 63
- attn_weights: float32 [3072, 768], P(('dp', 'fsdp')), may hold values from -0.25 to 0.25
- attn_m1: float32 [3072, 768], P(('dp', 'fsdp')), may hold values from -0.00061035156 to 0.00061035156
- attn_m2: float32 [3072, 768], P(('dp', 'fsdp')), may hold values from 1.4106315e-10 to 5.642526e-10
- attn_ema: float32 [3072, 768], P(('dp', 'fsdp')), may hold values from -0.25 to 0.25
- ffn_weights: float32 [6144, 768], P(('dp', 'fsdp')), may hold values from -0.0625 to 0.0625
- ffn_m1: float32 [6144, 768], P(('dp', 'fsdp')), may hold values from -0.00061035156 to 0.00061035156
- ffn_m2: float32 [6144, 768], P(('dp', 'fsdp')), may hold values from 1.4106315e-10 to 5.642526e-10
- ffn_ema: float32 [6144, 768], P(('dp', 'fsdp')), may hold values from -0.0625 to 0.0625
- vectors: float32 [12, 768], replicated, may hold values from -0.8 to 1.5, as said below
- vec_m1: float32 [12, 768], replicated, may hold values from -0.0024414062 to 0.0024414062
- vec_m2: float32 [12, 768], replicated, may hold values from 2.2570104e-09 to 9.028041e-09
- vec_ema: float32 [12, 768], replicated, may hold values from -0.8 to 1.5, as said below
- table: float32 [160, 12], replicated, may hold values from -5 to 5
- tab_m1: float32 [160, 12], replicated, may hold values from -0.0007324219 to 0.0007324219
- tab_m2: float32 [160, 12], replicated, may hold values from 1.4106315e-10 to 5.642526e-10
- tab_ema: float32 [160, 12], replicated, may hold values from -5 to 5
Outputs:
- block_out: bfloat16 [16384, 768], P(('dp', 'fsdp'))
- grad_input: float32 [16384, 768], P(('dp', 'fsdp'))
- grad_norm: float32 [], replicated
- new_attn: float32 [3072, 768], P(('dp', 'fsdp'))
- new_attn_m1: float32 [3072, 768], P(('dp', 'fsdp'))
- new_attn_m2: float32 [3072, 768], P(('dp', 'fsdp'))
- new_attn_ema: float32 [3072, 768], P(('dp', 'fsdp'))
- new_ffn: float32 [6144, 768], P(('dp', 'fsdp'))
- new_ffn_m1: float32 [6144, 768], P(('dp', 'fsdp'))
- new_ffn_m2: float32 [6144, 768], P(('dp', 'fsdp'))
- new_ffn_ema: float32 [6144, 768], P(('dp', 'fsdp'))
- new_vectors: float32 [12, 768], replicated
- new_vec_m1: float32 [12, 768], replicated
- new_vec_m2: float32 [12, 768], replicated
- new_vec_ema: float32 [12, 768], replicated
- new_table: float32 [160, 12], replicated
- new_tab_m1: float32 [160, 12], replicated
- new_tab_m2: float32 [160, 12], replicated
- new_tab_ema: float32 [160, 12], replicated
- vec_grad: float32 [12, 768], replicated
Inputs may be any that keep to these rules, and one draw needn't show every extreme that they name: `vectors`: rows 0 and 2 lie in 0.5 to 1.5. `vec_ema`: rows 0 and 2 lie in 0.5 to 1.5.
All inputs are finite; a program needn't handle non-finite values.
Results may differ from a plain program's by a relative error of at most 0.017.
Values may be sent and summed in bfloat16 or wider, within the bound.
No kernel may reach another device: no remote copies, remote signals or barrier semaphores. Data moves between devices by JAX's collectives and lax.ppermute only.
A program may use at most 128 MiB of HBM per device.

v0:
```python
import math

import jax
import jax.numpy as jnp
from jax import lax
from jax.experimental import pallas as pl
from jax.experimental.pallas import tpu as pltpu
from jax.sharding import PartitionSpec as P

D = 768
H = 12
HD = 64
FF = 3072
B1 = 32
BX = 64
SEQ = 512
STEP = 10
BUCKETS = B1 + 2 * BX


NEG_FILL = -1e30
NORM_EPS = 1e-05
BF = jnp.bfloat16
F32 = jnp.float32
NT = (((1,), (1,)), ((), ()))
TN = (((0,), (0,)), ((), ()))
NN = (((1,), (0,)), ((), ()))
ALL = ("dp", "fsdp")
COST = 1_000_000
SPLIT = (4, 2, 2, 2)
BLOCKS = 32
A_ROWS = 4 * D // BLOCKS
F_ROWS = 2 * FF // BLOCKS
HALF = FF // 2
ANY = pl.BlockSpec(memory_space=pl.ANY)


def mm(a, b, dims):
    return lax.dot_general(a, b, dims, preferred_element_type=F32)


def adam_update(weight, moment_one, second, gradient, clip_scale, step_rate, decay_rate, average):
    clipped = gradient * clip_scale
    new_first = 0.9 * moment_one + 0.1 * clipped
    new_second = 0.999 * second + 0.001 * clipped * clipped
    first_hat = new_first / (1.0 - 0.9**STEP)
    second_hat = new_second / (1.0 - 0.999**STEP)
    new_weight = weight - step_rate * (
        first_hat / (jnp.sqrt(second_hat) + 1e-08) + decay_rate * weight
    )
    new_average = 0.8 * average + 0.2 * new_weight
    return (new_weight, new_first, new_second, new_average)


def bias_kernel(len_ref, tab_ref, one_ref, x_ref, y_ref, out_ref):
    length = len_ref[0]
    rows = one_ref.shape[1]

    def eight(i, _):
        r = pl.ds(pl.multiple_of(i * 8, 8), 8)
        for c in range(0, SEQ, 128):
            ids = [ref[0, r, c : c + 128] for ref in (one_ref, x_ref, y_ref)]
            keep = lax.broadcasted_iota(jnp.int32, (8, 128), 1) + c < length
            for h in range(H):
                total = None
                for t in range(3):
                    line = jnp.broadcast_to(tab_ref[h, t : t + 1, :], (8, 128))
                    got = jnp.take_along_axis(line, ids[t], axis=1, mode="promise_in_bounds")
                    total = got if total is None else total + got
                out_ref[h, r, c : c + 128] = jnp.where(keep, total, NEG_FILL)
        return 0

    lax.fori_loop(0, rows // 8, eight, 0)


PARTS = 2
BIAS_ROWS = ((0, 192), (192, 256), (448, 64))


def bias_lines(table):
    lines = table.T
    return jnp.stack(
        [
            jnp.pad(lines[:, :B1], ((0, 0), (0, 128 - B1))),
            jnp.pad(lines[:, B1 : B1 + BX], ((0, 0), (0, 128 - BX))),
            jnp.pad(lines[:, B1 + BX :], ((0, 0), (0, 128 - BX))),
        ],
        axis=1,
    )


def page_bias(lengths, tab, rel, part, out):
    rows = 64
    first, count = BIAS_ROWS[part][0] // rows, BIAS_ROWS[part][1] // rows
    ids = pl.BlockSpec((1, rows, SEQ), lambda i, *_: (0, first + i, 0))
    extra = [] if out is None else [out]
    return pl.pallas_call(
        lambda *refs: bias_kernel(*refs[:5], refs[-1]),
        grid_spec=pltpu.PrefetchScalarGridSpec(
            num_scalar_prefetch=1,
            grid=(count,),
            in_specs=[pl.BlockSpec((H, 3, 128), lambda i, *_: (0, 0, 0)), ids, ids, ids]
            + [ANY] * len(extra),
            out_specs=pl.BlockSpec((H, rows, SEQ), lambda i, *_: (0, first + i, 0)),
        ),
        out_shape=jax.ShapeDtypeStruct((H, SEQ, SEQ), F32),
        input_output_aliases={5: 0} if extra else {},
        cost_estimate=pl.CostEstimate(
            flops=COST, bytes_accessed=COST, transcendentals=0
        ),
        name="bias",
    )(lengths, tab, *rel, *extra)


def head_masks():
    lane = lax.broadcasted_iota(jnp.int32, (1, 2 * HD), 1)
    return (lane < HD, lane >= HD)


def attend_kernel(q_ref, k_ref, v_ref, bias_ref, ctx_ref, p_ref, *, rows):
    zero = jnp.zeros((), BF)
    masks = head_masks()
    keys = [jnp.where(m, k_ref[...], zero) for m in masks]
    vals = [jnp.where(m, v_ref[...], zero) for m in masks]
    for r in range(0, SEQ, rows):
        q = q_ref[r : r + rows, :]
        ctx = None
        for h in range(2):
            scores = mm(q, keys[h], NT) * HD ** (-0.5) + bias_ref[h, r : r + rows, :]
            top = jnp.max(scores, axis=-1, keepdims=True)
            raised = jnp.exp(scores - top)
            total = jnp.sum(raised, axis=-1, keepdims=True)
            soft = (raised * (1.0 / total)).astype(BF)
            p_ref[h, r : r + rows, :] = soft
            part = mm(soft, vals[h], NN)
            ctx = part if ctx is None else ctx + part
        ctx_ref[r : r + rows, :] = ctx.astype(BF)


def lane_block(offset):
    return pl.BlockSpec((SEQ, 2 * HD), lambda i: (0, offset + i))


PAIR_BLOCK = pl.BlockSpec((2, SEQ, SEQ), lambda i: (i, 0, 0))


def attend(qkv, bias):
    n = D // (2 * HD)
    return pl.pallas_call(
        lambda *refs: attend_kernel(*refs, rows=256),
        grid=(n,),
        in_specs=[lane_block(0), lane_block(n), lane_block(2 * n), PAIR_BLOCK],
        out_specs=[lane_block(0), PAIR_BLOCK],
        out_shape=[
            jax.ShapeDtypeStruct((SEQ, D), BF),
            jax.ShapeDtypeStruct((H, SEQ, SEQ), BF),
        ],
        cost_estimate=pl.CostEstimate(
            flops=COST, bytes_accessed=COST, transcendentals=0
        ),
        name="attend",
    )(qkv, qkv, qkv, bias)


def attend_back_kernel(
    q_ref, k_ref, v_ref, p_ref, c_ref, dc_ref, dq_ref, dk_ref, dv_ref, ds_ref, sum_ref, *, rows
):
    zero = jnp.zeros((), BF)
    masks = head_masks()
    keys = [jnp.where(m, k_ref[...], zero) for m in masks]
    vals = [jnp.where(m, v_ref[...], zero) for m in masks]
    scale = HD ** (-0.5)
    q_sum = jnp.zeros((1, 2 * HD), F32)
    for r in range(0, SEQ, rows):
        dc = dc_ref[r : r + rows, :]
        prod = dc.astype(F32) * c_ref[r : r + rows, :].astype(F32)
        dq = None
        for h in range(2):
            soft = p_ref[h, r : r + rows, :]
            inner = jnp.sum(jnp.where(masks[h], prod, 0.0), axis=-1, keepdims=True)
            d_soft = mm(dc, vals[h], NT)
            d_scores = (soft.astype(F32) * (d_soft - inner)).astype(BF)
            ds_ref[h, r : r + rows, :] = d_scores
            part = mm(d_scores, keys[h], NN)
            dq = part if dq is None else dq + part
        dq = (dq * scale).astype(BF)
        dq_ref[r : r + rows, :] = dq
        q_sum = q_sum + jnp.sum(dq.astype(F32), axis=0, keepdims=True)
    flips = (dc_ref[...].astype(F32).T.astype(BF), q_ref[...].astype(F32).T.astype(BF))
    sums = [q_sum]
    for flip, factor, pair_ref, out_ref in (
        (flips[0], 1.0, p_ref, dv_ref),
        (flips[1], scale, ds_ref, dk_ref),
    ):
        parts = [mm(flip[HD * h : HD * h + HD, :], pair_ref[h], NN) for h in range(2)]
        done = (jnp.concatenate(parts, axis=0).T * factor).astype(BF)
        out_ref[...] = done
        sums.append(jnp.sum(done.astype(F32), axis=0, keepdims=True))
    sum_ref[...] = jnp.concatenate(sums[:2] + [jnp.zeros((6, 2 * HD), F32)], axis=0)


def attend_back(qkv, soft, ctx, d_ctx):
    n = D // (2 * HD)
    return pl.pallas_call(
        lambda *refs: attend_back_kernel(*refs, rows=256),
        grid=(n,),
        in_specs=[
            lane_block(0),
            lane_block(n),
            lane_block(2 * n),
            PAIR_BLOCK,
            lane_block(0),
            lane_block(0),
        ],
        out_specs=[
            lane_block(0),
            lane_block(0),
            lane_block(0),
            PAIR_BLOCK,
            pl.BlockSpec((8, 2 * HD), lambda i: (0, i)),
        ],
        out_shape=[jax.ShapeDtypeStruct((SEQ, D), BF)] * 3
        + [jax.ShapeDtypeStruct((H, SEQ, SEQ), BF), jax.ShapeDtypeStruct((8, D), F32)],
        cost_estimate=pl.CostEstimate(
            flops=COST, bytes_accessed=COST, transcendentals=0
        ),
        name="attend_back",
    )(qkv, qkv, qkv, soft, ctx, d_ctx)


def table_kernel(one_ref, x_ref, y_ref, ds_ref, out_ref):
    @pl.when(pl.program_id(0) == 0)
    def _():
        out_ref[...] = jnp.zeros_like(out_ref)

    rows = one_ref.shape[1]
    flipped = jnp.swapaxes(ds_ref[...].astype(F32), 0, 1).astype(BF)
    total = None
    for r in range(rows):
        hot = jnp.concatenate(
            [
                (lax.broadcasted_iota(jnp.int32, (size, SEQ), 0) == ref[0, r : r + 1, :])
                .astype(F32)
                .astype(BF)
                for ref, size in ((one_ref, B1), (x_ref, BX), (y_ref, BX))
            ],
            axis=0,
        )
        part = mm(flipped[r], hot, NT)
        total = part if total is None else total + part
    out_ref[...] += total


def table_grad(rel_1d, rel_x, rel_y, d_scores, part):
    rows = 16
    count = SEQ // rows // PARTS
    first = part * count
    ids = pl.BlockSpec((1, rows, SEQ), lambda i: (0, first + i, 0))
    return pl.pallas_call(
        table_kernel,
        grid=(count,),
        in_specs=[ids, ids, ids, pl.BlockSpec((H, rows, SEQ), lambda i: (0, first + i, 0))],
        out_specs=pl.BlockSpec((H, BUCKETS), lambda i: (0, 0)),
        out_shape=jax.ShapeDtypeStruct((H, BUCKETS), F32),
        cost_estimate=pl.CostEstimate(
            flops=COST, bytes_accessed=COST, transcendentals=0
        ),
        name="table_grad",
    )(rel_1d, rel_x, rel_y, d_scores)


def spread(size, plan):
    found = []
    for whole in plan:
        at, pieces = 0, []
        for z, x, y, first, last in whole:
            rows = (last - first) * size // 2
            pieces.append((at, rows, z, x, y, first * size // 2))
            at += rows
        found.append(pieces)
    return found


def blocks(zs, x, y):
    return [(z, x, y, 0, 2) for z in zs]


ATTN_PLAN = spread(
    A_ROWS,
    [
        blocks(range(4), 0, 0),
        blocks(range(4), 1, 0),
        blocks(range(4), 0, 1),
        blocks((0, 1), 1, 1),
        blocks((2, 3), 1, 1),
    ],
)
FFN_PLAN = spread(
    F_ROWS,
    [
        blocks((0,), 0, 0),
        blocks((0,), 1, 0),
        blocks((0,), 0, 1),
        blocks((0,), 1, 1),
        blocks((1, 2, 3), 0, 0),
        blocks((1, 2, 3), 1, 0),
        blocks((1, 2, 3), 0, 1),
        [(1, 1, 1, 0, 2), (2, 1, 1, 0, 1)],
        [(2, 1, 1, 1, 2), (3, 1, 1, 0, 2)],
    ],
)
A_COPIES = 2 * sum(len(pieces) for pieces in ATTN_PLAN)
F_COPIES = 2 * sum(len(pieces) for pieces in FFN_PLAN)

ATTN_FAR, FFN_FAR = ATTN_PLAN, FFN_PLAN


def piece_list(plans, refs):
    found = []
    for core, plan in enumerate(plans):
        for pieces, ref in zip(plan, refs[len(plans[0]) * core :]):
            for start, rows, z, x, y, offset in pieces:
                found.append((core, z, x, y, offset, rows, ref.at[pl.ds(start, rows), :]))
    return found


def qkv_kernel(at_ref, tok_ref, add_ref, *refs):
    qkv_ref, all_ref, weight_ref, sems, done = refs[len(ATTN_PLAN) + len(ATTN_FAR) :]
    copies = []
    for n, (core, z, x, y, offset, rows, ref) in enumerate(piece_list((ATTN_PLAN, ATTN_FAR), refs)):
        block = (
            ((at_ref[0] ^ z) * 2 + (at_ref[1] ^ x)) * 2 + (at_ref[2] ^ y)
        ) * 2 + (at_ref[3] ^ core)
        spot = pl.ds(pl.multiple_of(block * A_ROWS + offset, 16), rows)
        copies.append(pltpu.make_async_copy(ref, weight_ref.at[spot, :], sems.at[n]))
    for copy in copies:
        copy.start()
    for copy in copies:
        copy.wait()
    store = pltpu.make_async_copy(weight_ref, all_ref, done)
    store.start()
    for t in range(3):
        part = slice(D * t, D * t + D)
        qkv_ref[:, part] = (mm(tok_ref[...], weight_ref[part, :], NN) + add_ref[:, part]).astype(BF)
    store.wait()


def project(at, tokens, add_three, pieces):
    count = tokens.shape[0]
    vmem = pl.BlockSpec(memory_space=pltpu.VMEM)
    return pl.pallas_call(
        qkv_kernel,
        in_specs=[pl.BlockSpec(memory_space=pltpu.SMEM), vmem, vmem] + [ANY] * len(pieces),
        out_specs=[vmem, ANY],
        out_shape=[
            jax.ShapeDtypeStruct((count, 3 * D), BF),
            jax.ShapeDtypeStruct((4 * D, D), BF),
        ],
        scratch_shapes=[
            pltpu.VMEM((4 * D, D), BF),
            pltpu.SemaphoreType.DMA((A_COPIES,)),
            pltpu.SemaphoreType.DMA,
        ],
        cost_estimate=pl.CostEstimate(
            flops=COST, bytes_accessed=COST, transcendentals=0
        ),
        name="project",
    )(at, tokens, add_three, *pieces)


def grad_ffn_kernel(at_ref, *refs, high):
    wide, slim, outs, (left, right, sems) = refs[:4], refs[4:8], refs[8:11], refs[11:]
    which = (at_ref[0] // 2) ^ high
    for w in range(2):

        @pl.when(which == w)
        def _():
            copies = []
            for i in range(2):
                rows = pl.ds(SEQ * i, SEQ)
                copies.append(
                    pltpu.make_async_copy(wide[2 * w + i], left.at[rows, :], sems.at[2 * i])
                )
                copies.append(
                    pltpu.make_async_copy(slim[2 * w + i], right.at[rows, :], sems.at[2 * i + 1])
                )
            for copy in copies:
                copy.start()
            for copy in copies:
                copy.wait()

    own, kept, sent = outs
    for z in range(2):
        done = mm(left[:, HALF // 2 * z : HALF // 2 * (z + 1)], right[...], TN).astype(BF)
        rows = [done[F_ROWS * q : F_ROWS * q + F_ROWS, :] for q in range(4)]
        own[z] = rows[0]
        kept[z] = rows[1 if high else 2]
        sent[z] = rows[3]
        sent[2 + z] = rows[2 if high else 1]


def grad_ffn(at, wide, slim, high):
    shape = lambda n: jax.ShapeDtypeStruct((n, F_ROWS, D), BF)
    return pl.pallas_call(
        lambda *refs: grad_ffn_kernel(*refs, high=high),
        in_specs=[pl.BlockSpec(memory_space=pltpu.SMEM)] + [ANY] * 8,
        out_specs=[pl.BlockSpec(memory_space=pltpu.VMEM)] * 3,
        out_shape=[shape(2), shape(2), shape(4)],
        scratch_shapes=[
            pltpu.VMEM((2 * SEQ, HALF), BF),
            pltpu.VMEM((2 * SEQ, D), BF),
            pltpu.SemaphoreType.DMA((4,)),
        ],
        cost_estimate=pl.CostEstimate(
            flops=COST, bytes_accessed=COST, transcendentals=0
        ),
        name="grad_ffn",
    )(at, *wide, *slim)


def grad_attn_kernel(at_ref, tok_ref, tok_far, ctx_ref, ctx_far, *refs):
    grads, outs, (flip, left, right, sems) = refs[:8], refs[8:14], refs[14:]
    copies = []
    for t in range(4):
        for i in range(2):
            spot = right.at[t, pl.ds(SEQ * i, SEQ), :]
            copies.append(pltpu.make_async_copy(grads[2 * t + i], spot, sems.at[2 * t + i]))
    for copy in copies:
        copy.start()
    for n, (near, far) in enumerate(((tok_ref, tok_far), (ctx_ref, ctx_far))):
        flip[:, :SEQ] = near[...].astype(F32).T.astype(BF)
        flip[:, SEQ:] = far[...].astype(F32).T.astype(BF)
        for q in range(4):
            block = (((at_ref[1] ^ (q // 2)) * 2 + (at_ref[2] ^ (q % 2))) * 2) + at_ref[3]
            spot = pl.ds(pl.multiple_of(block * A_ROWS, A_ROWS), A_ROWS)
            left[n, A_ROWS * q : A_ROWS * q + A_ROWS, :] = flip[spot, :]
    for copy in copies:
        copy.wait()
    for z in range(4):
        which = at_ref[0] ^ z
        done = mm(left[which // 3], right[which], NN).astype(BF)
        rows = [done[A_ROWS * q : A_ROWS * q + A_ROWS, :] for q in range(4)]
        own, kept, sent = outs[3 * (z // 2) : 3 * (z // 2) + 3]
        own[z % 2] = rows[0]
        kept[z % 2] = rows[1 if z // 2 else 2]
        sent[z % 2] = rows[3]
        sent[2 + z % 2] = rows[2 if z // 2 else 1]


def grad_attn(at, tokens, tokens_far, ctx, ctx_far, grads):
    shape = lambda n: jax.ShapeDtypeStruct((n, A_ROWS, D), BF)
    vmem = pl.BlockSpec(memory_space=pltpu.VMEM)
    return pl.pallas_call(
        grad_attn_kernel,
        in_specs=[pl.BlockSpec(memory_space=pltpu.SMEM)] + [vmem] * 4 + [ANY] * 8,
        out_specs=[vmem] * 6,
        out_shape=[shape(2), shape(2), shape(4)] * 2,
        scratch_shapes=[
            pltpu.VMEM((D, 2 * SEQ), BF),
            pltpu.VMEM((2, D // 2, 2 * SEQ), BF),
            pltpu.VMEM((4, 2 * SEQ, D), BF),
            pltpu.SemaphoreType.DMA((8,)),
        ],
        cost_estimate=pl.CostEstimate(
            flops=COST, bytes_accessed=COST, transcendentals=0
        ),
        name="grad_attn",
    )(at, tokens, tokens_far, ctx, ctx_far, *grads)


def row_mean(values):
    return jnp.mean(values, axis=-1, keepdims=True)


def normal_rows(values):
    center = values - row_mean(values)
    inv = lax.rsqrt(row_mean(center * center) + NORM_EPS)
    return center * inv, inv


def normal_back(normal, inv, grad):
    return inv * (grad - row_mean(grad) - normal * row_mean(grad * normal))


def gelu_parts(u):
    z = jnp.abs(u) * (2.0**-0.5)
    t = 1.0 / (1.0 + 0.3275911 * z)
    tail = jnp.exp(-0.5 * u * u)
    poly = t * (
        0.254829592
        + t * (-0.284496736 + t * (1.421413741 + t * (-1.453152027 + t * 1.061405429)))
    )
    half = 0.5 * poly * tail
    cdf = jnp.where(u < 0, half, 1.0 - half)
    return u * cdf, cdf + u * (tail * (1.0 / math.sqrt(2.0 * math.pi)))


def row_sum(values):
    return jnp.sum(values.astype(F32), axis=0, keepdims=True)


def block_kernel(
    at_ref,
    ctx_ref,
    tok_ref,
    cot_ref,
    vec_ref,
    b1_ref,
    wo_ref,
    *refs,
    wide,
):
    split = len(FFN_PLAN) + len(FFN_FAR)
    pieces, refs = refs[:split], refs[split:]
    out_ref, hid_ref, act_near, act_far, dff_ref, du_near, du_far = refs[:7]
    dr_ref, dab_ref, dctx_ref, sum_ref, db1_ref, slope_ref, ffn_ref, sems = refs[7:]
    copies = []
    for n, (core, z, x, y, offset, rows, ref) in enumerate(piece_list((FFN_PLAN, FFN_FAR), pieces)):
        spot = pl.ds(core * HALF + ((z % 2) * 4 + x * 2 + y) * F_ROWS + offset, rows)
        which = (at_ref[0] // 2) ^ (z // 2)
        copies.append(pltpu.make_async_copy(ref, ffn_ref.at[which, spot, :], sems.at[n]))
    w1_ref, w2_ref = ffn_ref.at[0], ffn_ref.at[1]

    @pl.when(pl.program_id(0) == 0)
    def _():
        for copy in copies:
            copy.start()
        sum_ref[...] = jnp.zeros_like(sum_ref)
        db1_ref[...] = jnp.zeros_like(db1_ref)

    vec = [vec_ref[i : i + 1, :] for i in range(8)]
    resid = tok_ref[...].astype(F32) + (mm(ctx_ref[...], wo_ref[...], NN) + vec[6])
    n_one, inv_one = normal_rows(resid)
    hidden = n_one * vec[0] + vec[1]
    hid_low = hidden.astype(BF)
    hid_ref[...] = hid_low
    total = hidden + vec[7]

    @pl.when(pl.program_id(0) == 0)
    def _():
        for copy in copies:
            copy.wait()

    for f in range(0, FF, wide):
        part = slice(f, f + wide)
        u = mm(hid_low, w1_ref[part, :], NT) + b1_ref[:, part]
        act, slope = gelu_parts(u)
        act = act.astype(BF)
        side = slice(f % HALF, f % HALF + wide)
        (act_near if f < HALF else act_far)[:, side] = act
        slope_ref[:, part] = slope
        total = total + mm(act, w2_ref[part, :], NN)
    n_two, inv_two = normal_rows(total)
    out_ref[...] = (n_two * vec[2] + vec[3]).astype(BF)
    dy = cot_ref[...].astype(F32)
    d_two = normal_back(n_two, inv_two, dy * vec[2])
    dff = d_two.astype(BF)
    dff_ref[...] = dff
    d_hid = d_two
    for f in range(0, FF, wide):
        part = slice(f, f + wide)
        du = (mm(dff, w2_ref[part, :], NT) * slope_ref[:, part]).astype(BF)
        side = slice(f % HALF, f % HALF + wide)
        (du_near if f < HALF else du_far)[:, side] = du
        db1_ref[:, part] += row_sum(du)
        d_hid = d_hid + mm(du, w1_ref[part, :], NN)
    d_one = normal_back(n_one, inv_one, d_hid * vec[0])
    dr_ref[...] = d_one
    dab = d_one.astype(BF)
    dab_ref[...] = dab
    dctx_ref[...] = mm(dab, wo_ref[...], NT).astype(BF)
    sum_ref[...] += jnp.concatenate(
        [
            row_sum(d_hid * n_one),
            row_sum(d_hid),
            row_sum(dy * n_two),
            row_sum(dy),
            jnp.zeros((2, D), F32),
            row_sum(dab),
            row_sum(dff),
        ],
        axis=0,
    )


def block_pass(at, ctx, tokens, cotangent, vectors, b_first, attn_full, pieces):
    rows = 256
    by_row = lambda width: pl.BlockSpec((rows, width), lambda i, *_: (i, 0))
    whole = lambda shape, first=0: pl.BlockSpec(
        shape, lambda i, *_: (first, 0), pipeline_mode=pl.Buffered(1)
    )
    count = tokens.shape[0]
    low = lambda width: jax.ShapeDtypeStruct((count, width), BF)
    return pl.pallas_call(
        lambda *refs: block_kernel(*refs, wide=768),
        grid_spec=pltpu.PrefetchScalarGridSpec(
            num_scalar_prefetch=1,
            grid=(count // rows,),
            in_specs=[
                by_row(D),
                by_row(D),
                by_row(D),
                whole((12, D)),
                whole((1, FF)),
                whole((D, D), 3),
            ]
            + [ANY] * len(pieces),
            out_specs=[
                by_row(D),
                by_row(D),
                by_row(HALF),
                by_row(HALF),
                by_row(D),
                by_row(HALF),
                by_row(HALF),
                by_row(D),
                by_row(D),
                by_row(D),
                pl.BlockSpec((8, D), lambda i, *_: (0, 0)),
                pl.BlockSpec((1, FF), lambda i, *_: (0, 0)),
            ],
            scratch_shapes=[
                pltpu.VMEM((rows, FF), F32),
                pltpu.VMEM((2, FF, D), BF),
                pltpu.SemaphoreType.DMA((F_COPIES,)),
            ],
        ),
        out_shape=[
            low(D),
            low(D),
            low(HALF),
            low(HALF),
            low(D),
            low(HALF),
            low(HALF),
            jax.ShapeDtypeStruct((count, D), F32),
            low(D),
            low(D),
            jax.ShapeDtypeStruct((8, D), F32),
            jax.ShapeDtypeStruct((1, FF), F32),
        ],
        cost_estimate=pl.CostEstimate(
            flops=COST, bytes_accessed=COST, transcendentals=0
        ),
        name="block_pass",
    )(at, ctx, tokens, cotangent, vectors, b_first, attn_full, *pieces)


def swap(array, mask):
    return lax.ppermute(array, ALL, [(i, i ^ mask) for i in range(BLOCKS)])


def together(*groups):
    return lax.optimization_barrier(groups)


def tie(arrays, after):
    return lax.optimization_barrier((arrays, after))[0]


def column(shard, zs):
    return jnp.concatenate([shard if z == 0 else swap(shard, 8 * z) for z in zs])


def gather_full(shard, plans):
    full = lax.all_gather(shard, ALL, axis=0, tiled=True)
    view = full.reshape(*SPLIT, full.shape[0] // BLOCKS, D)
    return tuple(
        jnp.concatenate([view[z, x, y, core, off : off + n] for _, n, z, x, y, off in pieces])
        for core, plan in enumerate(plans)
        for pieces in plan
    )


def wide(array):
    return array.astype(F32)


def scatter_first(low, high):
    return swap(low[2], 2), swap(high[2], 4)


def scatter_second(low, high, from_y, from_x):
    to_x = (wide(low[1]) + wide(from_y[:2])).astype(BF)
    to_y = (wide(high[1]) + wide(from_x[:2])).astype(BF)
    return swap(to_x, 4), swap(to_y, 2)


def scatter_third(low, high, from_y, from_x, last_x, last_y):
    low = wide(low[0]) + wide(from_y[2:]) + wide(last_x)
    high = wide(high[0]) + wide(from_x[2:]) + wide(last_y)
    send = (low[1].astype(BF), high[0].astype(BF), high[1].astype(BF))
    return low[0], tuple(swap(a, 8 * z) for z, a in zip((1, 2, 3), send))


def scatter_full(sides):
    cores = []
    for low, high in sides:
        rows = [(low[0], high[0]), (low[2][2:], high[1]), (low[1], high[2][2:])]
        rows.append((low[2][:2], high[2][:2]))
        cores.append(jnp.stack([jnp.concatenate(pair) for pair in rows], axis=1))
    full = jnp.stack(cores, axis=2).reshape(-1, D)
    return lax.psum_scatter(full, ALL, scatter_dimension=0, tiled=True).astype(F32)


def flip_bits(array, at):
    for axis, bit in enumerate((at[0] % 2, at[1], at[2], at[3])):
        array = jnp.where(bit == 1, jnp.flip(array, axis), array)
    return array


LANES = 256


def pack_table(grad):
    return jnp.pad(grad, ((0, 0), (0, LANES - BUCKETS))).reshape(H * LANES // D, D)


def update_kernel(total_ref, attn_sum, ffn_sum, *refs):
    states, outs = [refs[4 * i : 4 * i + 4] for i in range(4)], refs[16:]
    per = D // LANES
    vec_total = total_ref[:H, :]
    heads = jnp.concatenate(
        [
            total_ref[H + h // per : H + h // per + 1, LANES * (h % per) : LANES * (h % per + 1)]
            for h in range(H)
        ],
        axis=0,
    )
    square = total_ref[H : H + 1, LANES - 1 : LANES]
    lane = lax.broadcasted_iota(jnp.int32, heads.shape, 1)
    tab_total = jnp.where(lane < BUCKETS, heads, 0.0)
    rows = jnp.sum(tab_total * tab_total, axis=0, keepdims=True)
    square = square + jnp.sum(rows, axis=1, keepdims=True)
    rows = jnp.sum(vec_total * vec_total, axis=0, keepdims=True)
    norm = jnp.sqrt(square + jnp.sum(rows, axis=1, keepdims=True))
    scale = 1.0 / jnp.maximum(norm, 1.0)
    outs[0][...] = norm
    outs[1][...] = vec_total * scale
    totals = (attn_sum[...], ffn_sum[...], vec_total, heads[:H, :BUCKETS])
    for i, (state, total) in enumerate(zip(states, totals)):
        rate, decay = (0.06, 0.01) if i < 2 else (0.6, 0.0)
        weight, first, second, average = (ref[...] for ref in state)
        new = adam_update(weight, first, second, total, scale, rate, decay, average)
        for out, value in zip(outs[2 + 4 * i :], new):
            out[...] = value


def update(total, attn_sum, ffn_sum, states):
    vmem = pl.BlockSpec(memory_space=pltpu.VMEM)
    like = lambda a: jax.ShapeDtypeStruct(a.shape, F32)
    one = jax.ShapeDtypeStruct((1, 1), F32)
    return pl.pallas_call(
        update_kernel,
        in_specs=[vmem] * 19,
        out_specs=[vmem] * 18,
        out_shape=[one, like(states[8])] + [like(a) for a in states],
        name="update",
    )(total, attn_sum, ffn_sum, *states)


def input_grad(start, d_three, attn_full):
    for t in range(3):
        start = start + mm(d_three[t], attn_full[D * t : D * t + D], NT)
    return start


def shards(
    tokens,
    cotangent,
    lengths,
    rel_1d,
    rel_x,
    rel_y,
    attn_weights,
    attn_m1,
    attn_m2,
    attn_ema,
    ffn_weights,
    ffn_m1,
    ffn_m2,
    ffn_ema,
    vectors,
    vec_m1,
    vec_m2,
    vec_ema,
    table,
    tab_m1,
    tab_m2,
    tab_ema,
    *,
    direct,
):
    attn_low, ffn_low = attn_weights.astype(BF), ffn_weights.astype(BF)
    rel = (rel_1d, rel_x, rel_y)
    tab = bias_lines(table)
    add_three = jnp.concatenate([vectors[4], jnp.zeros((D,), F32), vectors[5]]).reshape(1, 3 * D)
    if direct:
        dp, fsdp = lax.axis_index("dp"), lax.axis_index("fsdp")
        at = jnp.stack([dp // 2, dp % 2, fsdp // 2, fsdp % 2]).astype(jnp.int32)
        far = lambda a: swap(a, 1)
        attn_column = column(attn_low, range(4))
        ffn_x, ffn_y = swap(ffn_low, 4), swap(ffn_low, 2)
        bias = page_bias(lengths, tab, rel, 0, None)
        attn_column, ffn_x, ffn_y, later, bias = together(
            attn_column, ffn_x, ffn_y, ffn_low, bias
        )
        beside, above = swap(attn_column, 4), swap(attn_column, 2)
        ffn_column = column(later, (1, 2, 3))
        bias = page_bias(lengths, tab, rel, 1, bias)
        beside, above, bias = together(beside, above, bias)
        side = 2 * A_ROWS
        low, high = swap(beside[:side], 2), swap(above[side:], 4)
        near, ffn_column, bias = together((attn_column, beside, above), ffn_column, bias)
        away = tuple(swap(piece, 1) for piece in near)
        bias = page_bias(lengths, tab, rel, 2, bias)
        last, ffn_column, ffn_x, away, bias = together((low, high), ffn_column, ffn_x, away, bias)
        attn_pieces = near + last + away + tuple(swap(piece, 1) for piece in last)
        ffn_low = tie(ffn_low, ffn_column)
        beside, above, corner = swap(ffn_column, 4), swap(ffn_column, 2), swap(ffn_x, 2)
        qkv, attn_full = project(at, tokens, add_three, attn_pieces)
        ctx, soft = attend(qkv, bias)
        near = (ffn_low, ffn_x, ffn_y, corner, ffn_column, beside, above)
        first = (swap(ffn_low, 1), swap(ffn_x, 1))
        near, first, ctx = together(near, first, ctx)
        side = 3 * F_ROWS // 2
        last = (swap(near[5][:side], 2), swap(near[6][side:], 4))
        away = first + tuple(swap(piece, 1) for piece in near[2:])
        last, away = together(last, away)
        ffn_pieces = near + last + away + tuple(swap(piece, 1) for piece in last)
    else:
        at = jnp.zeros((4,), jnp.int32)
        far = jnp.zeros_like
        bias = None
        for part in range(len(BIAS_ROWS)):
            bias = page_bias(lengths, tab, rel, part, bias)
        attn_pieces = gather_full(attn_low, (ATTN_PLAN, ATTN_FAR))
        ffn_pieces = gather_full(ffn_low, (FFN_PLAN, FFN_FAR))
        qkv, attn_full = project(at, tokens, add_three, attn_pieces)
        ctx, soft = attend(qkv, bias)
        tokens_far, ctx_far = far(tokens), far(ctx)
    b_first = flip_bits(vectors[8:].reshape(2, 2, 2, 2, F_ROWS), at)
    b_first = b_first.transpose(3, 0, 1, 2, 4).reshape(1, FF)
    (
        block_out,
        hid,
        act_near,
        act_away,
        d_ffn,
        du_near,
        du_away,
        d_resid_one,
        d_attn,
        d_context,
        sums,
        grad_bias_first,
    ) = block_pass(at, ctx, tokens, cotangent, vectors, b_first, attn_full, ffn_pieces)
    away = (far(du_away), far(act_away), far(hid), far(d_ffn), far(d_attn))
    dq, dk, dv, d_scores, qv_sums = attend_back(qkv, soft, ctx, d_context)
    d_three = (dq, dk, dv)
    if direct:
        away, d_three, d_scores, rows = together(away, d_three, d_scores, (tokens, ctx))
        du_far, act_far, hid_far, d_ffn_far, d_attn_far = away
        wide_ones, slim = (du_near, du_far, act_near, act_far), (hid, hid_far, d_ffn, d_ffn_far)
        low = grad_ffn(at, wide_ones, slim, 0)
        three_far = tuple(far(d) for d in d_three + rows)
        low, three_far, wide_ones = together(low, three_far, wide_ones)
        high = grad_ffn(at, wide_ones, slim, 1)
        grads = [g for pair in zip(d_three, three_far[:3]) for g in pair] + [d_attn, d_attn_far]
        high, grads = together(high, grads)
        ffn_first = scatter_first(low, high)
        parts = grad_attn(at, tokens, three_far[3], ctx, three_far[4], grads)
        parts, d_scores = together(parts, d_scores)
        attn_first = scatter_first(parts[:3], parts[3:])
        tables = [table_grad(*rel, d_scores, 0)]
        ffn_first, d_scores, tables[0] = together(ffn_first, d_scores, tables[0])
        ffn_second = scatter_second(low, high, *ffn_first)
        tables.append(table_grad(*rel, d_scores, 1))
        attn_first, ffn_second, d_three, tables[1] = together(
            attn_first, ffn_second, d_three, tables[1]
        )
        ffn_own, ffn_three = scatter_third(low, high, *ffn_first, *ffn_second)
        attn_second = scatter_second(parts[:3], parts[3:], *attn_first)
        grad_input = input_grad(d_resid_one, d_three, attn_full)
        attn_second, grad_input = together(attn_second, grad_input)
        attn_own, attn_three = scatter_third(parts[:3], parts[3:], *attn_first, *attn_second)
        ffn_shard = sum((wide(a) for a in ffn_three), ffn_own)
        attn_shard = sum((wide(a) for a in attn_three), attn_own)
    else:
        sides, attn_sides = [], []
        grads = [g for d in (*d_three, d_attn) for g in (d, far(d))]
        slim = (hid, far(hid), d_ffn, far(d_ffn))
        for core, (du, act) in enumerate(((du_near, act_near), (du_away, act_away))):
            wide_ones = (du, far(du), act, far(act))
            sides.append([grad_ffn(at, wide_ones, slim, side) for side in range(2)])
            spot = at.at[3].set(core)
            parts = grad_attn(spot, tokens, tokens_far, ctx, ctx_far, grads)
            attn_sides.append((parts[:3], parts[3:]))
        ffn_shard, attn_shard = scatter_full(sides), scatter_full(attn_sides)
        tables = [table_grad(*rel, d_scores, part) for part in range(PARTS)]
        grad_input = input_grad(d_resid_one, d_three, attn_full)
    grad_table = pack_table(sum(tables[1:], tables[0]))
    grad_bias_first = grad_bias_first.reshape(2, 2, 2, 2, F_ROWS).transpose(1, 2, 3, 0, 4)
    grad_bias_first = flip_bits(grad_bias_first, at).reshape(FF // D, D)
    small = jnp.concatenate([sums[:4], qv_sums[:2], sums[6:], grad_bias_first, grad_table], axis=0)
    squares = jnp.sum(attn_shard * attn_shard) + jnp.sum(ffn_shard * ffn_shard)
    row = lax.broadcasted_iota(jnp.int32, small.shape, 0)
    lane = lax.broadcasted_iota(jnp.int32, small.shape, 1)
    small = jnp.where((row == H) & (lane == LANES - 1), squares, small)
    if direct:
        for mask in (1, 2, 4, 8, 16):
            small = small + swap(small, mask)
    else:
        small = lax.psum(small, ALL)
    states = (attn_weights, attn_m1, attn_m2, attn_ema, ffn_weights, ffn_m1, ffn_m2, ffn_ema)
    states += (vectors, vec_m1, vec_m2, vec_ema, table.T, tab_m1.T, tab_m2.T, tab_ema.T)
    grad_norm, vec_grad, *new = update(small, attn_shard, ffn_shard, states)
    new = new[:12] + [array.T for array in new[12:]]
    return (block_out, grad_input, grad_norm.reshape(()), *new, vec_grad)


def solution(mesh):
    direct = mesh.shape["dp"] == SPLIT[0] * SPLIT[1] and mesh.shape["fsdp"] == SPLIT[2] * SPLIT[3]
    return jax.shard_map(
        lambda *arrays: shards(*arrays, direct=direct),
        mesh=mesh,
        in_specs=(
            P(("dp", "fsdp"), None),
            P(("dp", "fsdp"), None),
            P(("dp", "fsdp")),
            P(("dp", "fsdp"), None, None),
            P(("dp", "fsdp"), None, None),
            P(("dp", "fsdp"), None, None),
            P(("dp", "fsdp"), None),
            P(("dp", "fsdp"), None),
            P(("dp", "fsdp"), None),
            P(("dp", "fsdp"), None),
            P(("dp", "fsdp"), None),
            P(("dp", "fsdp"), None),
            P(("dp", "fsdp"), None),
            P(("dp", "fsdp"), None),
            P(),
            P(),
            P(),
            P(),
            P(),
            P(),
            P(),
            P(),
        ),
        out_specs=(
            P(("dp", "fsdp"), None),
            P(("dp", "fsdp"), None),
            P(),
            P(("dp", "fsdp"), None),
            P(("dp", "fsdp"), None),
            P(("dp", "fsdp"), None),
            P(("dp", "fsdp"), None),
            P(("dp", "fsdp"), None),
            P(("dp", "fsdp"), None),
            P(("dp", "fsdp"), None),
            P(("dp", "fsdp"), None),
            P(),
            P(),
            P(),
            P(),
            P(),
            P(),
            P(),
            P(),
            P(),
        ),
        check_vma=False,
    )
```

profile of v0, /device:TPU:0, one launch (start us, length us, event | category | flops | bytes accessed | tf_op | source)
XLA Modules:
  0.0 302.3 jit_solution(8187089809788927199)
XLA Ops:
  1.7 5.1 %collective-permute-start.2 = (bf16[96,768]{1,0:T(8,128)(2,1)S(1)}, bf16[96,768]{1,0:T(8,128)(2,1)S(1)}, u32[]{:S(2)}, u32[]{:S(2)}) collective-permute-start(bf16[96,768]{1,0:T(8,128)(2,1)S(1)} %convert_element_type.128), channel_id=1, source_target_pairs={{0,24},{1,25},{2,26},{3,27},{4,28},{5,29},{6,30},{7,31},{8,16},{9,... | collective-permute-start | bytes 442376 | tf_op jit(solution)/shard_map/ppermute | solution.py:650
  13.2 12.3 %bias.3.refs_5_ = f32[12,512,512]{2,1,0:T(8,128)} custom-call(s32[1]{0:T(128)S(6)} %copy.53.refs_0_, f32[12,3,128]{2,1,0:T(4,128)} %copy.44.refs_1_, s32[1,512,512]{2,1,0:T(8,128)} %one_ref.3, s32[1,512,512]{2,1,0:T(8,128)} %x_ref.3, s32[1,512,512]{2,1,0:T(8,128)} %y_ref.3), custom_call_target="tpu_custom_call" | custom-call | flops 1000000 | bytes 1000000 | tf_op jit(solution)/shard_map/bias/pallas_call | solution.py:97
  26.5 3.7 %collective-permute-start.11 = (bf16[192,768]{1,0:T(8,128)(2,1)S(1)}, bf16[192,768]{1,0:T(8,128)(2,1)S(1)}, u32[]{:S(2)}, u32[]{:S(2)}) collective-permute-start(bf16[192,768]{1,0:T(8,128)(2,1)S(1)} %convert_element_type.127.refs_7_), channel_id=1, source_target_pairs={{0,24},{1,25},{2,26},{3,27},{4,28},{5,29},{6,30},{7,31},{8,16},{9,... | collective-permute-start | bytes 884744 | tf_op jit(solution)/shard_map/ppermute | solution.py:650
  30.9 15.6 %bias.4.refs_5_ = f32[12,512,512]{2,1,0:T(8,128)} custom-call(s32[1]{0:T(128)S(6)} %copy.53.refs_0_, f32[12,3,128]{2,1,0:T(4,128)} %copy.44.refs_1_, s32[1,512,512]{2,1,0:T(8,128)} %one_ref.3, s32[1,512,512]{2,1,0:T(8,128)} %x_ref.3, s32[1,512,512]{2,1,0:T(8,128)} %y_ref.3, f32[12,512,512]{2,1,0:T(8,128)} %bias.3.refs_5_), custom_call_target="tpu_custom_call", output_to_operand_aliasing={{}: (5, {})} | custom-call | flops 1000000 | bytes 1000000 | tf_op jit(solution)/shard_map/bias/pallas_call | solution.py:97
  46.6 6.8 %collective-permute-done.10 = bf16[192,768]{1,0:T(8,128)(2,1)S(1)} collective-permute-done((bf16[192,768]{1,0:T(8,128)(2,1)S(1)}, bf16[192,768]{1,0:T(8,128)(2,1)S(1)}, u32[]{:S(2)}, u32[]{:S(2)}) %collective-permute-start.10) | collective-permute-done | bytes 294944 | tf_op jit(solution)/shard_map/ppermute | solution.py:650
  59.6 5.5 %bias.5.refs_3_ = f32[12,512,512]{2,1,0:T(8,128)} custom-call(s32[1]{0:T(128)S(6)} %copy.53.refs_0_, f32[12,3,128]{2,1,0:T(4,128)} %copy.44.refs_1_, s32[1,512,512]{2,1,0:T(8,128)} %one_ref.3, s32[1,512,512]{2,1,0:T(8,128)} %x_ref.3, s32[1,512,512]{2,1,0:T(8,128)} %y_ref.3, f32[12,512,512]{2,1,0:T(8,128)} %bias.4.refs_5_), custom_call_target="tpu_custom_call", output_to_operand_aliasing={{}: (5, {})} | custom-call | flops 1000000 | bytes 1000000 | tf_op jit(solution)/shard_map/bias/pallas_call | solution.py:97
  74.8 7.5 %project.1 = (bf16[512,2304]{1,0:T(8,128)(2,1)}, bf16[3072,768]{1,0:T(8,128)(2,1)}) custom-call(s32[4]{0:T(128)} %pad_add_fusion.at_ref.refs_0_, bf16[512,768]{1,0:T(8,128)(2,1)} %tok_ref.3, f32[1,2304]{1,0:T(1,128)} %reshape.67.add_ref, bf16[384,768]{1,0:T(8,128)(2,1)} %copy-done.5, bf16[384,768]{1,0:T(8,128)(2,1)} %copy-done.10, ...), custom_call_target="tpu_custom_call" | custom-call | flops 1000000 | bytes 1000000 | tf_op jit(solution)/shard_map/project/pallas_call | solution.py:351
  82.3 12.9 %attend.1 = (bf16[512,768]{1,0:T(8,128)(2,1)}, bf16[12,512,512]{2,1,0:T(8,128)(2,1)}) custom-call(bf16[512,2304]{1,0:T(8,128)(2,1)} %get-tuple-element.189.refs_0_.refs_1_.refs_2_, bf16[512,2304]{1,0:T(8,128)(2,1)} %get-tuple-element.189.refs_0_.refs_1_.refs_2_, bf16[512,2304]{1,0:T(8,128)(2,1)} %get-tuple-element.189.refs_0_.refs_1_.refs_2_, ...), custom_call_target="tpu_custom_call" | custom-call | flops 1000000 | bytes 1000000 | tf_op jit(solution)/shard_map/attend/pallas_call | solution.py:149
  97.6 3.5 %collective-permute-done.24.refs_18_ = bf16[192,768]{1,0:T(8,128)(2,1)} collective-permute-done((bf16[192,768]{1,0:T(8,128)(2,1)}, bf16[192,768]{1,0:T(8,128)(2,1)}, u32[]{:S(2)}, u32[]{:S(2)}) %collective-permute-start.24) | collective-permute-done | bytes 294944 | tf_op jit(solution)/shard_map/ppermute | solution.py:650
  104.0 9.5 %collective-permute-done.23.refs_15_ = bf16[288,768]{1,0:T(8,128)(2,1)} collective-permute-done((bf16[288,768]{1,0:T(8,128)(2,1)S(1)}, bf16[288,768]{1,0:T(8,128)(2,1)}, u32[]{:S(2)}, u32[]{:S(2)}) %collective-permute-start.23) | collective-permute-done | bytes 442400 | tf_op jit(solution)/shard_map/ppermute | solution.py:650
  118.9 25.4 %block_pass.1 = (bf16[512,768]{1,0:T(8,128)(2,1)}, bf16[512,768]{1,0:T(8,128)(2,1)}, bf16[512,1536]{1,0:T(8,128)(2,1)}, bf16[512,1536]{1,0:T(8,128)(2,1)}, bf16[...) custom-call(s32[4]{0:T(128)} %pad_add_fusion.at_ref.refs_0_, ...), custom_call_target="tpu_custom_call" | custom-call | flops 1000000 | bytes 1000000 | tf_op jit(solution)/shard_map/block_pass/pallas_call | solution.py:594
  146.2 10.8 %attend_back.1 = (bf16[512,768]{1,0:T(8,128)(2,1)}, bf16[512,768]{1,0:T(8,128)(2,1)}, bf16[512,768]{1,0:T(8,128)(2,1)}, bf16[12,512,512]{2,1,0:T(8,128)(2,1)}, f32[8,768]{1,0:T(8,128)}) custom-call(bf16[512,2304]{1,0:T(8,128)(2,1)} %get-tuple-element.189.refs_0_.refs_1_.refs_2_, bf16[512,2304]{1,0:T(8,128)(2,1)} %get-tuple-element.189.refs_0_.refs_1_.refs_2_, ...), custom_call_target="tpu_custom_call" | custom-call | flops 1000000 | bytes 1000000 | tf_op jit(solution)/shard_map/attend_back/pallas_call | solution.py:204
  158.3 6.9 %grad_ffn.2 = (bf16[2,192,768]{2,1,0:T(8,128)(2,1)}, bf16[2,192,768]{2,1,0:T(8,128)(2,1)}, bf16[4,192,768]{2,1,0:T(8,128)(2,1)}) custom-call(s32[4]{0:T(128)} %pad_add_fusion.at_ref.refs_0_, bf16[512,1536]{1,0:T(8,128)(2,1)} %get-tuple-element.240.refs_1_, bf16[512,1536]{1,0:T(8,128)(2,1)} %copy-done.2, bf16[512,1536]{1,0:T(8,128)(2,1)} %get-tuple-element.242.refs_3_, ...), custom_call_target="tpu_custom_call" | custom-call | flops 1000000 | bytes 1000000 | tf_op jit(solution)/shard_map/grad_ffn/pallas_call | solution.py:404
  165.3 7.1 %grad_ffn.3 = (bf16[2,192,768]{2,1,0:T(8,128)(2,1)}, bf16[2,192,768]{2,1,0:T(8,128)(2,1)}, bf16[4,192,768]{2,1,0:T(8,128)(2,1)}) custom-call(s32[4]{0:T(128)} %pad_add_fusion.at_ref.refs_0_, bf16[512,1536]{1,0:T(8,128)(2,1)} %get-tuple-element.240.refs_1_, bf16[512,1536]{1,0:T(8,128)(2,1)} %copy-done.2, bf16[512,1536]{1,0:T(8,128)(2,1)} %get-tuple-element.242.refs_3_, ...), custom_call_target="tpu_custom_call" | custom-call | flops 1000000 | bytes 1000000 | tf_op jit(solution)/shard_map/grad_ffn/pallas_call | solution.py:404
  178.9 8.4 %grad_attn.1 = (bf16[2,96,768]{2,1,0:T(8,128)(2,1)}, bf16[2,96,768]{2,1,0:T(8,128)(2,1)}, bf16[4,96,768]{2,1,0:T(8,128)(2,1)}, bf16[2,96,768]{2,1,0:T(8,128)(2,1...) custom-call(s32[4]{0:T(128)} %pad_add_fusion.at_ref.refs_0_, bf16[512,768]{1,0:T(8,128)(2,1)} %tok_ref.3, ...), custom_call_target="tpu_custom_call" | custom-call | flops 1000000 | bytes 1000000 | tf_op jit(solution)/shard_map/grad_attn/pallas_call | solution.py:453
  189.2 15.8 %table_grad.2 = f32[12,160]{1,0:T(8,128)} custom-call(s32[1,512,512]{2,1,0:T(8,128)} %one_ref.3, s32[1,512,512]{2,1,0:T(8,128)} %x_ref.3, s32[1,512,512]{2,1,0:T(8,128)} %y_ref.3, bf16[12,512,512]{2,1,0:T(8,128)(2,1)} %get-tuple-element.276.ds_ref), custom_call_target="tpu_custom_call" | custom-call | flops 1000000 | bytes 1000000 | tf_op jit(solution)/shard_map/table_grad/pallas_call | solution.py:259
  213.1 15.8 %table_grad.3 = f32[12,160]{1,0:T(8,128)} custom-call(s32[1,512,512]{2,1,0:T(8,128)} %one_ref.3, s32[1,512,512]{2,1,0:T(8,128)} %x_ref.3, s32[1,512,512]{2,1,0:T(8,128)} %y_ref.3, bf16[12,512,512]{2,1,0:T(8,128)(2,1)} %get-tuple-element.276.ds_ref), custom_call_target="tpu_custom_call" | custom-call | flops 1000000 | bytes 1000000 | tf_op jit(solution)/shard_map/table_grad/pallas_call | solution.py:259
  234.8 2.9 collective-permute-start.53
  244.8 3.2 %fusion.6 = f32[512,768]{1,0:T(8,128)} fusion(bf16[512,768]{1,0:T(8,128)(2,1)S(1)} %copy-done.14, bf16[3072,768]{1,0:T(8,128)(2,1)} %get-tuple-element.193.refs_6_), kind=kOutput, calls=%fused_computation.7 | convolution fusion | flops 603979776 | bytes 3538944 | tf_op jit(solution)/shard_map/dot_general | solution.py:39
  248.1 3.4 %fusion.4 = f32[512,768]{1,0:T(8,128)} fusion(bf16[512,768]{1,0:T(8,128)(2,1)S(1)} %copy-done.13, bf16[3072,768]{1,0:T(8,128)(2,1)} %get-tuple-element.193.refs_6_), kind=kOutput, calls=%fused_computation.5 | convolution fusion | flops 603979776 | bytes 3538944 | tf_op jit(solution)/shard_map/dot_general | solution.py:39
  251.4 2.7 concatenate.15
  254.1 4.2 %add_add_fusion = f32[512,768]{1,0:T(8,128)} fusion(f32[512,768]{1,0:T(8,128)} %fusion.4, f32[512,768]{1,0:T(8,128)S(1)} %copy-done.8, f32[512,768]{1,0:T(8,128)} %fusion.6, bf16[512,768]{1,0:T(8,128)(2,1)S(1)} %copy-done.4, bf16[3072,768]{1,0:T(8,128)(2,1)} %get-tuple-element.193.refs_6_), kind=kOutput, calls=%fused_computation | convolution fusion | flops 605159424 | bytes 8257536 | tf_op jit(solution)/shard_map/dot_general | solution.py:39
  260.9 3.0 collective-permute-start.50
  265.4 2.7 multiply_reduce_fusion
  268.1 6.0 %collective-permute-done.50 = bf16[96,768]{1,0:T(8,128)(2,1)S(1)} collective-permute-done((bf16[96,768]{1,0:T(8,128)(2,1)S(1)}, bf16[96,768]{1,0:T(8,128)(2,1)S(1)}, u32[]{:S(2)}, u32[]{:S(2)}) %collective-permute-start.50) | collective-permute-done | bytes 147488 | tf_op jit(solution)/shard_map/ppermute | solution.py:650
  279.4 3.0 collective-permute-done.56
  283.5 3.1 %collective-permute-done.57 = f32[16,768]{1,0:T(8,128)S(1)} collective-permute-done((f32[16,768]{1,0:T(8,128)S(1)}, f32[16,768]{1,0:T(8,128)S(1)}, u32[]{:S(2)}, u32[]{:S(2)}) %collective-permute-start.57) | collective-permute-done | bytes 49184 | tf_op jit(solution)/shard_map/ppermute | solution.py:650
  286.6 2.4 collective-permute-start.58
  288.9 2.1 collective-permute-done.58
  291.0 3.4 %collective-permute-start.59 = (f32[16,768]{1,0:T(8,128)S(1)}, f32[16,768]{1,0:T(8,128)S(1)}, u32[]{:S(2)}, u32[]{:S(2)}) collective-permute-start(f32[16,768]{1,0:T(8,128)S(1)} %add.132), channel_id=1, source_target_pairs={{0,16},{1,17},{2,18},{3,19},{4,20},{5,21},{6,22},{7,23},{8,24},{9,... | collective-permute-start | bytes 147464 | tf_op jit(solution)/shard_map/ppermute | solution.py:650
  294.4 2.1 collective-permute-done.59
  297.1 5.0 %update.1 = (f32[1,1]{1,0:T(1,128)}, f32[12,768]{1,0:T(8,128)}, f32[96,768]{1,0:T(8,128)}, f32[96,768]{1,0:T(8,128)}, f32[96,768]{1,0:T(8,128)}, /*index=5*/f32[...) custom-call(f32[16,768]{1,0:T(8,128)} %add.133.total_ref, ...), custom_call_target="tpu_custom_call" | custom-call | tf_op jit(solution)/shard_map/update/pallas_call | solution.py:753
  (251 shorter events, 76.7 us)
Async XLA Ops:
  1.7 23.8 %collective-permute-start.2 = (bf16[96,768]{1,0:T(8,128)(2,1)S(1)}, bf16[96,768]{1,0:T(8,128)(2,1)S(1)}, u32[]{:S(2)}, u32[]{:S(2)}) collective-permute-start(bf16[96,768]{1,0:T(8,128)(2,1)S(1)} %convert_element_type.128), channel_id=1, source_target_pairs={{0,24},{1,25},{2,26},{3,27},{4,28},{5,29},{6,30},{7,31},{8,16},{9,... | collective-permute-start | bytes 442376 | tf_op jit(solution)/shard_map/ppermute | solution.py:650
  6.8 18.6 %collective-permute-start.1 = (bf16[96,768]{1,0:T(8,128)(2,1)S(1)}, bf16[96,768]{1,0:T(8,128)(2,1)S(1)}, u32[]{:S(2)}, u32[]{:S(2)}) collective-permute-start(bf16[96,768]{1,0:T(8,128)(2,1)S(1)} %convert_element_type.128), channel_id=1, source_target_pairs={{0,16},{1,17},{2,18},{3,19},{4,20},{5,21},{6,22},{7,23},{8,24},{9,... | collective-permute-start | bytes 442376 | tf_op jit(solution)/shard_map/ppermute | solution.py:650
  6.8 18.6 %collective-permute-start = (bf16[96,768]{1,0:T(8,128)(2,1)S(1)}, bf16[96,768]{1,0:T(8,128)(2,1)S(1)}, u32[]{:S(2)}, u32[]{:S(2)}) collective-permute-start(bf16[96,768]{1,0:T(8,128)(2,1)S(1)} %convert_element_type.128), channel_id=1, source_target_pairs={{0,8},{1,9},{2,10},{3,11},{4,12},{5,13},{6,14},{7,15},{8,0},{9,1},... | collective-permute-start | bytes 442376 | tf_op jit(solution)/shard_map/ppermute | solution.py:650
  8.6 16.9 %collective-permute-start.4 = (bf16[192,768]{1,0:T(8,128)(2,1)S(1)}, bf16[192,768]{1,0:T(8,128)(2,1)S(1)}, u32[]{:S(2)}, u32[]{:S(2)}) collective-permute-start(bf16[192,768]{1,0:T(8,128)(2,1)S(1)} %convert_element_type.127.refs_7_), channel_id=1, source_target_pairs={{0,2},{1,3},{2,0},{3,1},{4,6},{5,7},{6,4},{7,5},{8,10},{9,11},{10,... | collective-permute-start | bytes 884744 | tf_op jit(solution)/shard_map/ppermute | solution.py:650
  10.3 15.2 %collective-permute-start.3 = (bf16[192,768]{1,0:T(8,128)(2,1)S(1)}, bf16[192,768]{1,0:T(8,128)(2,1)S(1)}, u32[]{:S(2)}, u32[]{:S(2)}) collective-permute-start(bf16[192,768]{1,0:T(8,128)(2,1)S(1)} %convert_element_type.127.refs_7_), channel_id=1, source_target_pairs={{0,4},{1,5},{2,6},{3,7},{4,0},{5,1},{6,2},{7,3},{8,12},{9,13},{10,... | collective-permute-start | bytes 884744 | tf_op jit(solution)/shard_map/ppermute | solution.py:650
  25.6 28.9 %collective-permute-start.6 = (bf16[384,768]{1,0:T(8,128)(2,1)S(1)}, bf16[384,768]{1,0:T(8,128)(2,1)S(1)}, u32[]{:S(2)}, u32[]{:S(2)}) collective-permute-start(bf16[384,768]{1,0:T(8,128)(2,1)S(1)} %pad_maximum_fusion.1.refs_0_), channel_id=1, source_target_pairs={{0,2},{1,3},{2,0},{3,1},{4,6},{5,7},{6,4},{7,5},{8,10},{9,11},{10,... | collective-permute-start | bytes 1769480 | tf_op jit(solution)/shard_map/ppermute | solution.py:650
  26.1 28.3 %collective-permute-start.5 = (bf16[384,768]{1,0:T(8,128)(2,1)S(1)}, bf16[384,768]{1,0:T(8,128)(2,1)S(1)}, u32[]{:S(2)}, u32[]{:S(2)}) collective-permute-start(bf16[384,768]{1,0:T(8,128)(2,1)S(1)} %pad_maximum_fusion.1.refs_0_), channel_id=1, source_target_pairs={{0,4},{1,5},{2,6},{3,7},{4,0},{5,1},{6,2},{7,3},{8,12},{9,13},{10,... | collective-permute-start | bytes 1769480 | tf_op jit(solution)/shard_map/ppermute | solution.py:650
  26.5 20.0 %collective-permute-start.11 = (bf16[192,768]{1,0:T(8,128)(2,1)S(1)}, bf16[192,768]{1,0:T(8,128)(2,1)S(1)}, u32[]{:S(2)}, u32[]{:S(2)}) collective-permute-start(bf16[192,768]{1,0:T(8,128)(2,1)S(1)} %convert_element_type.127.refs_7_), channel_id=1, source_target_pairs={{0,24},{1,25},{2,26},{3,27},{4,28},{5,29},{6,30},{7,31},{8,16},{9,... | collective-permute-start | bytes 884744 | tf_op jit(solution)/shard_map/ppermute | solution.py:650
  30.3 23.1 %collective-permute-start.10 = (bf16[192,768]{1,0:T(8,128)(2,1)S(1)}, bf16[192,768]{1,0:T(8,128)(2,1)S(1)}, u32[]{:S(2)}, u32[]{:S(2)}) collective-permute-start(bf16[192,768]{1,0:T(8,128)(2,1)S(1)} %convert_element_type.127.refs_7_), channel_id=1, source_target_pairs={{0,16},{1,17},{2,18},{3,19},{4,20},{5,21},{6,22},{7,23},{8,24},{9,... | collective-permute-start | bytes 884744 | tf_op jit(solution)/shard_map/ppermute | solution.py:650
  30.3 23.1 %collective-permute-start.9 = (bf16[192,768]{1,0:T(8,128)(2,1)S(1)}, bf16[192,768]{1,0:T(8,128)(2,1)}, u32[]{:S(2)}, u32[]{:S(2)}) collective-permute-start(bf16[192,768]{1,0:T(8,128)(2,1)S(1)} %convert_element_type.127.refs_7_), channel_id=1, source_target_pairs={{0,8},{1,9},{2,10},{3,11},{4,12},{5,13},{6,14},{7,15},{8,0},{9,1},... | collective-permute-start | bytes 884744 | tf_op jit(solution)/shard_map/ppermute | solution.py:650
  54.5 13.0 %collective-permute-start.12 = (bf16[384,768]{1,0:T(8,128)(2,1)S(1)}, bf16[384,768]{1,0:T(8,128)(2,1)S(1)}, u32[]{:S(2)}, u32[]{:S(2)}) collective-permute-start(bf16[384,768]{1,0:T(8,128)(2,1)S(1)} %pad_maximum_fusion.1.refs_0_), channel_id=1, source_target_pairs={{0,1},{1,0},{2,3},{3,2},{4,5},{5,4},{6,7},{7,6},{8,9},{9,8},{10,11... | collective-permute-start | bytes 1769480 | tf_op jit(solution)/shard_map/ppermute | solution.py:650
  54.5 12.9 %collective-permute-start.13 = (bf16[384,768]{1,0:T(8,128)(2,1)S(1)}, bf16[384,768]{1,0:T(8,128)(2,1)}, u32[]{:S(2)}, u32[]{:S(2)}) collective-permute-start(bf16[384,768]{1,0:T(8,128)(2,1)S(1)} %collective-permute-done.5.refs_1_), channel_id=1, source_target_pairs={{0,1},{1,0},{2,3},{3,2},{4,5},{5,4},{6,7},{7,6},{8,9},{9,8},{10,11... | collective-permute-start | bytes 1769480 | tf_op jit(solution)/shard_map/ppermute | solution.py:650
  68.3 27.3 %collective-permute-start.17 = (bf16[576,768]{1,0:T(8,128)(2,1)S(1)}, bf16[576,768]{1,0:T(8,128)(2,1)S(1)}, u32[]{:S(2)}, u32[]{:S(2)}) collective-permute-start(bf16[576,768]{1,0:T(8,128)(2,1)S(1)} %pad_maximum_fusion.refs_11_), channel_id=1, source_target_pairs={{0,2},{1,3},{2,0},{3,1},{4,6},{5,7},{6,4},{7,5},{8,10},{9,11},{10,... | collective-permute-start | bytes 2654216 | tf_op jit(solution)/shard_map/ppermute | solution.py:650
  69.8 25.8 %collective-permute-start.16 = (bf16[576,768]{1,0:T(8,128)(2,1)S(1)}, bf16[576,768]{1,0:T(8,128)(2,1)S(1)}, u32[]{:S(2)}, u32[]{:S(2)}) collective-permute-start(bf16[576,768]{1,0:T(8,128)(2,1)S(1)} %pad_maximum_fusion.refs_11_), channel_id=1, source_target_pairs={{0,4},{1,5},{2,6},{3,7},{4,0},{5,1},{6,2},{7,3},{8,12},{9,13},{10,... | collective-permute-start | bytes 2654216 | tf_op jit(solution)/shard_map/ppermute | solution.py:650
  70.8 24.4 %collective-permute-start.19 = (bf16[192,768]{1,0:T(8,128)(2,1)}, bf16[192,768]{1,0:T(8,128)(2,1)}, u32[]{:S(2)}, u32[]{:S(2)}) collective-permute-start(bf16[192,768]{1,0:T(8,128)(2,1)} %copy-done.29), channel_id=1, source_target_pairs={{0,1},{1,0},{2,3},{3,2},{4,5},{5,4},{6,7},{7,6},{8,9},{9,8},{10,11... | collective-permute-start | bytes 884744 | tf_op jit(solution)/shard_map/ppermute | solution.py:650
  72.1 23.4 %collective-permute-start.15 = (bf16[192,768]{1,0:T(8,128)(2,1)}, bf16[192,768]{1,0:T(8,128)(2,1)}, u32[]{:S(2)}, u32[]{:S(2)}) collective-permute-start(bf16[192,768]{1,0:T(8,128)(2,1)} %copy-done.29), channel_id=1, source_target_pairs={{0,2},{1,3},{2,0},{3,1},{4,6},{5,7},{6,4},{7,5},{8,10},{9,11},{10,... | collective-permute-start | bytes 884744 | tf_op jit(solution)/shard_map/ppermute | solution.py:650
  72.6 22.6 %collective-permute-start.18 = (bf16[192,768]{1,0:T(8,128)(2,1)S(1)}, bf16[192,768]{1,0:T(8,128)(2,1)}, u32[]{:S(2)}, u32[]{:S(2)}) collective-permute-start(bf16[192,768]{1,0:T(8,128)(2,1)S(1)} %convert_element_type.127.refs_7_), channel_id=1, source_target_pairs={{0,1},{1,0},{2,3},{3,2},{4,5},{5,4},{6,7},{7,6},{8,9},{9,8},{10,11... | collective-permute-start | bytes 884744 | tf_op jit(solution)/shard_map/ppermute | solution.py:650
  95.6 19.2 %collective-permute-start.26 = (bf16[576,768]{1,0:T(8,128)(2,1)S(1)}, bf16[576,768]{1,0:T(8,128)(2,1)S(1)}, u32[]{:S(2)}, u32[]{:S(2)}) collective-permute-start(bf16[576,768]{1,0:T(8,128)(2,1)S(1)} %pad_maximum_fusion.refs_11_), channel_id=1, source_target_pairs={{0,1},{1,0},{2,3},{3,2},{4,5},{5,4},{6,7},{7,6},{8,9},{9,8},{10,11... | collective-permute-start | bytes 2654216 | tf_op jit(solution)/shard_map/ppermute | solution.py:650
  95.8 18.9 %collective-permute-start.27 = (bf16[576,768]{1,0:T(8,128)(2,1)S(1)}, bf16[576,768]{1,0:T(8,128)(2,1)}, u32[]{:S(2)}, u32[]{:S(2)}) collective-permute-start(bf16[576,768]{1,0:T(8,128)(2,1)S(1)} %collective-permute-done.16.refs_12_), channel_id=1, source_target_pairs={{0,1},{1,0},{2,3},{3,2},{4,5},{5,4},{6,7},{7,6},{8,9},{9,8},{10,11... | collective-permute-start | bytes 2654216 | tf_op jit(solution)/shard_map/ppermute | solution.py:650
  96.2 18.6 %collective-permute-start.28 = (bf16[576,768]{1,0:T(8,128)(2,1)S(1)}, bf16[576,768]{1,0:T(8,128)(2,1)}, u32[]{:S(2)}, u32[]{:S(2)}) collective-permute-start(bf16[576,768]{1,0:T(8,128)(2,1)S(1)} %collective-permute-done.17.refs_13_), channel_id=1, source_target_pairs={{0,1},{1,0},{2,3},{3,2},{4,5},{5,4},{6,7},{7,6},{8,9},{9,8},{10,11... | collective-permute-start | bytes 2654216 | tf_op jit(solution)/shard_map/ppermute | solution.py:650
  172.4 32.6 %collective-permute-start.44 = (bf16[4,192,768]{2,1,0:T(8,128)(2,1)}, bf16[4,192,768]{2,1,0:T(8,128)(2,1)S(1)}, u32[]{:S(2)}, u32[]{:S(2)}) collective-permute-start(bf16[4,192,768]{2,1,0:T(8,128)(2,1)} %get-tuple-element.271), channel_id=1, source_target_pairs={{0,4},{1,5},{2,6},{3,7},{4,0},{5,1},{6,2},{7,3},{8,12},{9,13},{10,... | collective-permute-start | bytes 3538952 | tf_op jit(solution)/shard_map/ppermute | solution.py:650
  173.2 31.9 %collective-permute-start.43 = (bf16[4,192,768]{2,1,0:T(8,128)(2,1)}, bf16[4,192,768]{2,1,0:T(8,128)(2,1)S(1)}, u32[]{:S(2)}, u32[]{:S(2)}) collective-permute-start(bf16[4,192,768]{2,1,0:T(8,128)(2,1)} %get-tuple-element.270), channel_id=1, source_target_pairs={{0,2},{1,3},{2,0},{3,1},{4,6},{5,7},{6,4},{7,5},{8,10},{9,11},{10,... | collective-permute-start | bytes 3538952 | tf_op jit(solution)/shard_map/ppermute | solution.py:650
  187.3 41.6 %collective-permute-start.41 = (bf16[4,96,768]{2,1,0:T(8,128)(2,1)}, bf16[4,96,768]{2,1,0:T(8,128)(2,1)}, u32[]{:S(2)}, u32[]{:S(2)}) collective-permute-start(bf16[4,96,768]{2,1,0:T(8,128)(2,1)} %get-tuple-element.267), channel_id=1, source_target_pairs={{0,2},{1,3},{2,0},{3,1},{4,6},{5,7},{6,4},{7,5},{8,10},{9,11},{10,... | collective-permute-start | bytes 1769480 | tf_op jit(solution)/shard_map/ppermute | solution.py:650
  187.9 41.0 %collective-permute-start.42 = (bf16[4,96,768]{2,1,0:T(8,128)(2,1)}, bf16[4,96,768]{2,1,0:T(8,128)(2,1)}, u32[]{:S(2)}, u32[]{:S(2)}) collective-permute-start(bf16[4,96,768]{2,1,0:T(8,128)(2,1)} %get-tuple-element.268), channel_id=1, source_target_pairs={{0,4},{1,5},{2,6},{3,7},{4,0},{5,1},{6,2},{7,3},{8,12},{9,13},{10,... | collective-permute-start | bytes 1769480 | tf_op jit(solution)/shard_map/ppermute | solution.py:650
  205.3 23.7 %collective-permute-start.46 = (bf16[2,192,768]{2,1,0:T(8,128)(2,1)S(1)}, bf16[2,192,768]{2,1,0:T(8,128)(2,1)}, u32[]{:S(2)}, u32[]{:S(2)}) collective-permute-start(bf16[2,192,768]{2,1,0:T(8,128)(2,1)S(1)} %add_convert_fusion.1), channel_id=1, source_target_pairs={{0,2},{1,3},{2,0},{3,1},{4,6},{5,7},{6,4},{7,5},{8,10},{9,11},{10,... | collective-permute-start | bytes 1769480 | tf_op jit(solution)/shard_map/ppermute | solution.py:650
  207.0 22.0 %collective-permute-start.45 = (bf16[2,192,768]{2,1,0:T(8,128)(2,1)S(1)}, bf16[2,192,768]{2,1,0:T(8,128)(2,1)}, u32[]{:S(2)}, u32[]{:S(2)}) collective-permute-start(bf16[2,192,768]{2,1,0:T(8,128)(2,1)S(1)} %add_convert_fusion.2), channel_id=1, source_target_pairs={{0,4},{1,5},{2,6},{3,7},{4,0},{5,1},{6,2},{7,3},{8,12},{9,13},{10,... | collective-permute-start | bytes 1769480 | tf_op jit(solution)/shard_map/ppermute | solution.py:650
  234.8 29.1 %collective-permute-start.52 = (bf16[192,768]{1,0:T(8,128)(2,1)}, bf16[192,768]{1,0:T(8,128)(2,1)}, u32[]{:S(2)}, u32[]{:S(2)}) collective-permute-start(bf16[192,768]{1,0:T(8,128)(2,1)} %fusion.11), channel_id=1, source_target_pairs={{0,8},{1,9},{2,10},{3,11},{4,12},{5,13},{6,14},{7,15},{8,0},{9,1},... | collective-permute-start | bytes 884744 | tf_op jit(solution)/shard_map/ppermute | solution.py:650
  234.8 30.6 %collective-permute-start.53 = (bf16[192,768]{1,0:T(8,128)(2,1)}, bf16[192,768]{1,0:T(8,128)(2,1)}, u32[]{:S(2)}, u32[]{:S(2)}) collective-permute-start(bf16[192,768]{1,0:T(8,128)(2,1)} %get-tuple-element.322), channel_id=1, source_target_pairs={{0,16},{1,17},{2,18},{3,19},{4,20},{5,21},{6,22},{7,23},{8,24},{9,... | collective-permute-start | bytes 884744 | tf_op jit(solution)/shard_map/ppermute | solution.py:650
  237.7 27.7 %collective-permute-start.54 = (bf16[192,768]{1,0:T(8,128)(2,1)}, bf16[192,768]{1,0:T(8,128)(2,1)}, u32[]{:S(2)}, u32[]{:S(2)}) collective-permute-start(bf16[192,768]{1,0:T(8,128)(2,1)} %get-tuple-element.323), channel_id=1, source_target_pairs={{0,24},{1,25},{2,26},{3,27},{4,28},{5,29},{6,30},{7,31},{8,16},{9,... | collective-permute-start | bytes 884744 | tf_op jit(solution)/shard_map/ppermute | solution.py:650
  240.9 17.5 %collective-permute-start.48 = (bf16[2,96,768]{2,1,0:T(8,128)(2,1)}, bf16[2,96,768]{2,1,0:T(8,128)(2,1)}, u32[]{:S(2)}, u32[]{:S(2)}) collective-permute-start(bf16[2,96,768]{2,1,0:T(8,128)(2,1)} %add_convert_fusion.4), channel_id=1, source_target_pairs={{0,2},{1,3},{2,0},{3,1},{4,6},{5,7},{6,4},{7,5},{8,10},{9,11},{10,... | collective-permute-start | bytes 884744 | tf_op jit(solution)/shard_map/ppermute | solution.py:650
  243.5 14.9 %collective-permute-start.47 = (bf16[2,96,768]{2,1,0:T(8,128)(2,1)}, bf16[2,96,768]{2,1,0:T(8,128)(2,1)}, u32[]{:S(2)}, u32[]{:S(2)}) collective-permute-start(bf16[2,96,768]{2,1,0:T(8,128)(2,1)} %add_convert_fusion.5), channel_id=1, source_target_pairs={{0,4},{1,5},{2,6},{3,7},{4,0},{5,1},{6,2},{7,3},{8,12},{9,13},{10,... | collective-permute-start | bytes 884744 | tf_op jit(solution)/shard_map/ppermute | solution.py:650
  260.9 13.3 %collective-permute-start.50 = (bf16[96,768]{1,0:T(8,128)(2,1)S(1)}, bf16[96,768]{1,0:T(8,128)(2,1)S(1)}, u32[]{:S(2)}, u32[]{:S(2)}) collective-permute-start(bf16[96,768]{1,0:T(8,128)(2,1)S(1)} %get-tuple-element.324), channel_id=1, source_target_pairs={{0,16},{1,17},{2,18},{3,19},{4,20},{5,21},{6,22},{7,23},{8,24},{9,... | collective-permute-start | bytes 442376 | tf_op jit(solution)/shard_map/ppermute | solution.py:650
  (69 other events, 685.2 us)
where the time goes:
time: 304 us; the launch traced here: 302 us
  Pallas kernels  149 us (49%)
  starting transfers between devices  54.5 us (18%)
  waiting for transfers between devices  42.6 us (14%)
  other arithmetic  22.6 us (7%)
  local copies, waits for them, and re-layouts  19.1 us (6%)
  matrix products  10.8 us (4%)
  between operations  3.57 us (1%)
    ppermute x60, starting transfers between devices, swap(): return lax.ppermute(array, ALL, [(i, i ^ mask) for i in range(BLOCKS)])  54.5 us
    ppermute x60, waiting for transfers between devices, swap(): return lax.ppermute(array, ALL, [(i, i ^ mask) for i in range(BLOCKS)])  42.6 us
    pallas_call x3, Pallas kernels, page_bias(): pl.pallas_call(lambda *refs: bias_kernel(*refs[:5], refs[-1]), grid_spec=...  33.4 us
    pallas_call x2, Pallas kernels, table_grad(): pl.pallas_call(table_kernel, grid=(count,), in_specs=[ids, ids, ids, pl.B...  31.7 us
    pallas_call x1, Pallas kernels, block_pass(): pl.pallas_call(lambda *refs: block_kernel(*refs, wide=768), grid_spec=plt...  25.4 us
    pallas_call x2, Pallas kernels, grad_ffn(): pl.pallas_call(lambda *refs: grad_ffn_kernel(*refs, high=high), in_specs=...  14 us
    pallas_call x1, Pallas kernels, attend(): pl.pallas_call(lambda *refs: attend_kernel(*refs, rows=256), grid=(n,), i...  12.9 us
    dot_general x3, matrix products, mm(): return lax.dot_general(a, b, dims, preferred_element_type=F32)  10.8 us
  transfers between devices with their start and end apart: 60, of which 14 were waited for; matrix products, arithmetic and copies ran while one was open for 14% of the time, Pallas kernels for 37%

commit v1 on v0

--- a/solution.py
+++ b/solution.py
@@ -74,7 +74,7 @@
 
 
 PARTS = 2
-BIAS_ROWS = ((0, 192), (192, 256), (448, 64))
+BIAS_ROWS = ((0, 128), (128, 320), (448, 64))
 
 
 def bias_lines(table):
@@ -301,18 +301,26 @@
         blocks((0,), 0, 0),
         blocks((0,), 1, 0),
         blocks((0,), 0, 1),
-        blocks((0,), 1, 1),
         blocks((1, 2, 3), 0, 0),
         blocks((1, 2, 3), 1, 0),
         blocks((1, 2, 3), 0, 1),
-        [(1, 1, 1, 0, 2), (2, 1, 1, 0, 1)],
-        [(2, 1, 1, 1, 2), (3, 1, 1, 0, 2)],
+        blocks((0, 1), 1, 1),
+        blocks((2, 3), 1, 1),
     ],
 )
 A_COPIES = 2 * sum(len(pieces) for pieces in ATTN_PLAN)
 F_COPIES = 2 * sum(len(pieces) for pieces in FFN_PLAN)
 
-ATTN_FAR, FFN_FAR = ATTN_PLAN, FFN_PLAN
+
+def joined(plan):
+    start, found = 0, []
+    for pieces in plan:
+        found += [(start + first, *rest) for first, *rest in pieces]
+        start += sum(piece[1] for piece in pieces)
+    return [found]
+
+
+ATTN_FAR, FFN_FAR = joined(ATTN_PLAN[:3]) + ATTN_PLAN[3:], FFN_PLAN
 
 
 def piece_list(plans, refs):
@@ -680,9 +688,13 @@
     return swap(low[2], 2), swap(high[2], 4)
 
 
-def scatter_second(low, high, from_y, from_x):
+def scatter_sums(low, high, from_y, from_x):
     to_x = (wide(low[1]) + wide(from_y[:2])).astype(BF)
     to_y = (wide(high[1]) + wide(from_x[:2])).astype(BF)
+    return to_x, to_y
+
+
+def scatter_second(to_x, to_y):
     return swap(to_x, 4), swap(to_y, 2)
 
 
@@ -747,20 +759,29 @@
 
 
 def update(total, attn_sum, ffn_sum, states):
-    vmem = pl.BlockSpec(memory_space=pltpu.VMEM)
     like = lambda a: jax.ShapeDtypeStruct(a.shape, F32)
     one = jax.ShapeDtypeStruct((1, 1), F32)
+    steps = 4 if attn_sum.shape[0] % 32 == 0 else 1
+    whole = lambda shape: pl.BlockSpec(shape, lambda i: (0, 0))
+    part = lambda a: pl.BlockSpec((a.shape[0] // steps, D), lambda i: (i, 0))
+    states_specs = [part(a) for a in states[:8]] + [whole(a.shape) for a in states[8:]]
     return pl.pallas_call(
         update_kernel,
-        in_specs=[vmem] * 19,
-        out_specs=[vmem] * 18,
+        grid=(steps,),
+        in_specs=[whole(total.shape), part(attn_sum), part(ffn_sum)] + states_specs,
+        out_specs=[whole((1, 1)), whole(states[8].shape)] + states_specs,
         out_shape=[one, like(states[8])] + [like(a) for a in states],
         name="update",
     )(total, attn_sum, ffn_sum, *states)
 
 
-def input_grad(start, d_three, attn_full):
-    for t in range(3):
+def hidden_bias(vectors, at):
+    flipped = flip_bits(vectors[8:].reshape(2, 2, 2, 2, F_ROWS), at)
+    return flipped.transpose(3, 0, 1, 2, 4).reshape(1, FF)
+
+
+def input_grad(start, d_three, attn_full, which=(0, 1, 2)):
+    for t in which:
         start = start + mm(d_three[t], attn_full[D * t : D * t + D], NT)
     return start
 
@@ -799,37 +820,38 @@
         dp, fsdp = lax.axis_index("dp"), lax.axis_index("fsdp")
         at = jnp.stack([dp // 2, dp % 2, fsdp // 2, fsdp % 2]).astype(jnp.int32)
         far = lambda a: swap(a, 1)
+        b_first = hidden_bias(vectors, at)
         attn_column = column(attn_low, range(4))
         ffn_x, ffn_y = swap(ffn_low, 4), swap(ffn_low, 2)
         bias = page_bias(lengths, tab, rel, 0, None)
-        attn_column, ffn_x, ffn_y, later, bias = together(
-            attn_column, ffn_x, ffn_y, ffn_low, bias
+        attn_column, ffn_x, ffn_y, later, bias, at, b_first, add_three = together(
+            attn_column, ffn_x, ffn_y, ffn_low, bias, at, b_first, add_three
         )
         beside, above = swap(attn_column, 4), swap(attn_column, 2)
         ffn_column = column(later, (1, 2, 3))
         bias = page_bias(lengths, tab, rel, 1, bias)
         beside, above, bias = together(beside, above, bias)
+        near, ffn_column, bias = together((attn_column, beside, above), ffn_column, bias)
         side = 2 * A_ROWS
-        low, high = swap(beside[:side], 2), swap(above[side:], 4)
-        near, ffn_column, bias = together((attn_column, beside, above), ffn_column, bias)
-        away = tuple(swap(piece, 1) for piece in near)
+        low, high = swap(near[1][:side], 2), swap(near[2][side:], 4)
+        beside, above = swap(ffn_column, 4), swap(ffn_column, 2)
+        away = swap(jnp.concatenate(near), 1)
         bias = page_bias(lengths, tab, rel, 2, bias)
-        last, ffn_column, ffn_x, away, bias = together((low, high), ffn_column, ffn_x, away, bias)
-        attn_pieces = near + last + away + tuple(swap(piece, 1) for piece in last)
-        ffn_low = tie(ffn_low, ffn_column)
-        beside, above, corner = swap(ffn_column, 4), swap(ffn_column, 2), swap(ffn_x, 2)
+        last, away, bias, start = together((low, high), away, bias, (ffn_low, ffn_x, ffn_y))
+        attn_pieces = near + last + (away,) + tuple(swap(piece, 1) for piece in last)
+        first = tuple(swap(piece, 1) for piece in start)
         qkv, attn_full = project(at, tokens, add_three, attn_pieces)
+        first, beside, above, qkv = together(first, beside, above, qkv)
+        low = swap(jnp.concatenate([start[1], beside[:F_ROWS]]), 2)
+        high = swap(above[F_ROWS:], 4)
+        middle = (ffn_column, beside, above)
+        away = tuple(swap(piece, 1) for piece in middle)
         ctx, soft = attend(qkv, bias)
-        near = (ffn_low, ffn_x, ffn_y, corner, ffn_column, beside, above)
-        first = (swap(ffn_low, 1), swap(ffn_x, 1))
-        near, first, ctx = together(near, first, ctx)
-        side = 3 * F_ROWS // 2
-        last = (swap(near[5][:side], 2), swap(near[6][side:], 4))
-        away = first + tuple(swap(piece, 1) for piece in near[2:])
-        last, away = together(last, away)
-        ffn_pieces = near + last + away + tuple(swap(piece, 1) for piece in last)
+        last, away, ctx = together((low, high), away, ctx)
+        ffn_pieces = start + middle + last + first + away + tuple(swap(a, 1) for a in last)
     else:
         at = jnp.zeros((4,), jnp.int32)
+        b_first = hidden_bias(vectors, at)
         far = jnp.zeros_like
         bias = None
         for part in range(len(BIAS_ROWS)):
@@ -839,8 +861,6 @@
         qkv, attn_full = project(at, tokens, add_three, attn_pieces)
         ctx, soft = attend(qkv, bias)
         tokens_far, ctx_far = far(tokens), far(ctx)
-    b_first = flip_bits(vectors[8:].reshape(2, 2, 2, 2, F_ROWS), at)
-    b_first = b_first.transpose(3, 0, 1, 2, 4).reshape(1, FF)
     (
         block_out,
         hid,
@@ -874,15 +894,19 @@
         attn_first = scatter_first(parts[:3], parts[3:])
         tables = [table_grad(*rel, d_scores, 0)]
         ffn_first, d_scores, tables[0] = together(ffn_first, d_scores, tables[0])
-        ffn_second = scatter_second(low, high, *ffn_first)
+        ffn_second = scatter_second(*scatter_sums(low, high, *ffn_first))
         tables.append(table_grad(*rel, d_scores, 1))
         attn_first, ffn_second, d_three, tables[1] = together(
             attn_first, ffn_second, d_three, tables[1]
         )
         ffn_own, ffn_three = scatter_third(low, high, *ffn_first, *ffn_second)
-        attn_second = scatter_second(parts[:3], parts[3:], *attn_first)
-        grad_input = input_grad(d_resid_one, d_three, attn_full)
-        attn_second, grad_input = together(attn_second, grad_input)
+        sent, d_three = together(scatter_sums(parts[:3], parts[3:], *attn_first), d_three)
+        attn_second = scatter_second(*sent)
+        grad_input = input_grad(d_resid_one, d_three, attn_full, (0, 1))
+        late = (sums, qv_sums, grad_bias_first, tables, d_three[2])
+        attn_second, grad_input, late = together(attn_second, grad_input, late)
+        sums, qv_sums, grad_bias_first, tables, last_grad = late
+        grad_input = input_grad(grad_input, (last_grad,), attn_full[2 * D :], (0,))
         attn_own, attn_three = scatter_third(parts[:3], parts[3:], *attn_first, *attn_second)
         ffn_shard = sum((wide(a) for a in ffn_three), ffn_own)
         attn_shard = sum((wide(a) for a in attn_three), attn_own)

time: 304 us -> 297 us (0.977)
  waiting for transfers between devices: 42.6 us -> 37.3 us
  matrix products: 10.8 us -> 6.69 us
  between operations: 3.57 us -> 7.5 us
    ppermute x60 -> x56, waiting for transfers between devices: 42.6 us -> 37.3 us  [swap(): return lax.ppermute(array, ALL, [(i, i ^ mask) for i in range(BLOCKS)])]
    dot_general x3, matrix products: 10.8 us -> 6.69 us  [mm(): return lax.dot_general(a, b, dims, preferred_element_type=F32)]
    ppermute x60 -> x56, starting transfers between devices: 54.5 us -> 51.7 us  [swap(): return lax.ppermute(array, ALL, [(i, i ^ mask) for i in range(BLOCKS)])]
  transfers between devices with their start and end apart: 60 -> 56, of which waited for: 14 -> 19; matrix products, arithmetic and copies ran while one was open for 14% -> 13% of each run, Pallas kernels for 37% -> 38%
where the time goes in v1:
time: 297 us; the launch traced here: 295 us
  Pallas kernels  150 us (51%)
  starting transfers between devices  51.7 us (17%)
  waiting for transfers between devices  37.3 us (13%)
  other arithmetic  22.7 us (8%)
  local copies, waits for them, and re-layouts  19 us (6%)
  between operations  7.5 us (3%)
  matrix products  6.69 us (2%)
    ppermute x56, starting transfers between devices, swap(): return lax.ppermute(array, ALL, [(i, i ^ mask) for i in range(BLOCKS)])  51.7 us
    ppermute x56, waiting for transfers between devices, swap(): return lax.ppermute(array, ALL, [(i, i ^ mask) for i in range(BLOCKS)])  37.3 us
    pallas_call x3, Pallas kernels, page_bias(): pl.pallas_call(lambda *refs: bias_kernel(*refs[:5], refs[-1]), grid_spec=...  33.4 us
    pallas_call x2, Pallas kernels, table_grad(): pl.pallas_call(table_kernel, grid=(count,), in_specs=[ids, ids, ids, pl.B...  31.7 us
    pallas_call x1, Pallas kernels, block_pass(): pl.pallas_call(lambda *refs: block_kernel(*refs, wide=768), grid_spec=plt...  25.7 us
    pallas_call x2, Pallas kernels, grad_ffn(): pl.pallas_call(lambda *refs: grad_ffn_kernel(*refs, high=high), in_specs=...  13.8 us
    pallas_call x1, Pallas kernels, attend(): pl.pallas_call(lambda *refs: attend_kernel(*refs, rows=256), grid=(n,), i...  12.9 us
    pallas_call x1, Pallas kernels, attend_back(): pl.pallas_call(lambda *refs: attend_back_kernel(*refs, rows=256), grid=(n...  10.9 us
  transfers between devices with their start and end apart: 56, of which 19 were waited for; matrix products, arithmetic and copies ran while one was open for 13% of the time, Pallas kernels for 38%

profile of v1, /device:TPU:0, one launch (start us, length us, event | category | flops | bytes accessed | tf_op | source)
XLA Modules:
  0.0 295.0 jit_solution(8782336705199301555)
XLA Ops:
  1.7 3.1 %collective-permute-start = (bf16[96,768]{1,0:T(8,128)(2,1)S(1)}, bf16[96,768]{1,0:T(8,128)(2,1)S(1)}, u32[]{:S(2)}, u32[]{:S(2)}) collective-permute-start(bf16[96,768]{1,0:T(8,128)(2,1)S(1)} %convert_element_type.127), channel_id=1, source_target_pairs={{0,8},{1,9},{2,10},{3,11},{4,12},{5,13},{6,14},{7,15},{8,0},{9,1},... | collective-permute-start | bytes 442376 | tf_op jit(solution)/shard_map/ppermute | solution.py:658
  4.8 2.6 collective-permute-start.1
  8.5 1.8 collective-permute-start.3
  16.4 8.9 %bias.3.refs_5_ = f32[12,512,512]{2,1,0:T(8,128)} custom-call(s32[1]{0:T(128)S(6)} %copy.54.refs_0_, f32[12,3,128]{2,1,0:T(4,128)} %copy.44.refs_1_, s32[1,512,512]{2,1,0:T(8,128)} %one_ref.3, s32[1,512,512]{2,1,0:T(8,128)} %x_ref.3, s32[1,512,512]{2,1,0:T(8,128)} %y_ref.3), custom_call_target="tpu_custom_call" | custom-call | flops 1000000 | bytes 1000000 | tf_op jit(solution)/shard_map/bias/pallas_call | solution.py:97
  27.8 3.5 %collective-permute-start.8 = (bf16[192,768]{1,0:T(8,128)(2,1)S(1)}, bf16[192,768]{1,0:T(8,128)(2,1)S(1)}, u32[]{:S(2)}, u32[]{:S(2)}) collective-permute-start(bf16[192,768]{1,0:T(8,128)(2,1)S(1)} %convert_element_type.128.refs_7_), channel_id=1, source_target_pairs={{0,16},{1,17},{2,18},{3,19},{4,20},{5,21},{6,22},{7,23},{8,24},{9,... | collective-permute-start | bytes 884744 | tf_op jit(solution)/shard_map/ppermute | solution.py:658
  31.3 19.0 %bias.4.refs_5_ = f32[12,512,512]{2,1,0:T(8,128)} custom-call(s32[1]{0:T(128)S(6)} %copy.54.refs_0_, f32[12,3,128]{2,1,0:T(4,128)} %copy.44.refs_1_, s32[1,512,512]{2,1,0:T(8,128)} %one_ref.3, s32[1,512,512]{2,1,0:T(8,128)} %x_ref.3, s32[1,512,512]{2,1,0:T(8,128)} %y_ref.3, f32[12,512,512]{2,1,0:T(8,128)} %bias.3.refs_5_), custom_call_target="tpu_custom_call", output_to_operand_aliasing={{}: (5, {})} | custom-call | flops 1000000 | bytes 1000000 | tf_op jit(solution)/shard_map/bias/pallas_call | solution.py:97
  60.7 5.6 %bias.5.refs_3_ = f32[12,512,512]{2,1,0:T(8,128)} custom-call(s32[1]{0:T(128)S(6)} %copy.54.refs_0_, f32[12,3,128]{2,1,0:T(4,128)} %copy.44.refs_1_, s32[1,512,512]{2,1,0:T(8,128)} %one_ref.3, s32[1,512,512]{2,1,0:T(8,128)} %x_ref.3, s32[1,512,512]{2,1,0:T(8,128)} %y_ref.3, f32[12,512,512]{2,1,0:T(8,128)} %bias.4.refs_5_), custom_call_target="tpu_custom_call", output_to_operand_aliasing={{}: (5, {})} | custom-call | flops 1000000 | bytes 1000000 | tf_op jit(solution)/shard_map/bias/pallas_call | solution.py:97
  71.2 7.5 %project.1 = (bf16[512,2304]{1,0:T(8,128)(2,1)}, bf16[3072,768]{1,0:T(8,128)(2,1)}) custom-call(s32[4]{0:T(128)} %pad_add_fusion.at_ref.refs_0_, bf16[512,768]{1,0:T(8,128)(2,1)} %tok_ref.3, f32[1,2304]{1,0:T(1,128)} %reshape.75.add_ref, bf16[384,768]{1,0:T(8,128)(2,1)} %copy-done.3, bf16[384,768]{1,0:T(8,128)(2,1)} %copy-done.4, ...), custom_call_target="tpu_custom_call" | custom-call | flops 1000000 | bytes 1000000 | tf_op jit(solution)/shard_map/project/pallas_call | solution.py:359
  78.7 7.8 %collective-permute-done.16.refs_11_ = bf16[576,768]{1,0:T(8,128)(2,1)S(1)} collective-permute-done((bf16[576,768]{1,0:T(8,128)(2,1)S(1)}, bf16[576,768]{1,0:T(8,128)(2,1)S(1)}, u32[]{:S(2)}, u32[]{:S(2)}) %collective-permute-start.16) | collective-permute-done | bytes 884768 | tf_op jit(solution)/shard_map/ppermute | solution.py:658
  90.9 12.9 %attend.1 = (bf16[512,768]{1,0:T(8,128)(2,1)}, bf16[12,512,512]{2,1,0:T(8,128)(2,1)}) custom-call(bf16[512,2304]{1,0:T(8,128)(2,1)} %get-tuple-element.197.refs_0_.refs_1_.refs_2_, bf16[512,2304]{1,0:T(8,128)(2,1)} %get-tuple-element.197.refs_0_.refs_1_.refs_2_, bf16[512,2304]{1,0:T(8,128)(2,1)} %get-tuple-element.197.refs_0_.refs_1_.refs_2_, ...), custom_call_target="tpu_custom_call" | custom-call | flops 1000000 | bytes 1000000 | tf_op jit(solution)/shard_map/attend/pallas_call | solution.py:149
  108.8 25.7 %block_pass.1 = (bf16[512,768]{1,0:T(8,128)(2,1)}, bf16[512,768]{1,0:T(8,128)(2,1)}, bf16[512,1536]{1,0:T(8,128)(2,1)}, bf16[512,1536]{1,0:T(8,128)(2,1)}, bf16[...) custom-call(s32[4]{0:T(128)} %pad_add_fusion.at_ref.refs_0_, ...), custom_call_target="tpu_custom_call" | custom-call | flops 1000000 | bytes 1000000 | tf_op jit(solution)/shard_map/block_pass/pallas_call | solution.py:602
  135.8 10.9 %attend_back.1 = (bf16[512,768]{1,0:T(8,128)(2,1)}, bf16[512,768]{1,0:T(8,128)(2,1)}, bf16[512,768]{1,0:T(8,128)(2,1)}, bf16[12,512,512]{2,1,0:T(8,128)(2,1)}, f32[8,768]{1,0:T(8,128)}) custom-call(bf16[512,2304]{1,0:T(8,128)(2,1)} %get-tuple-element.197.refs_0_.refs_1_.refs_2_, bf16[512,2304]{1,0:T(8,128)(2,1)} %get-tuple-element.197.refs_0_.refs_1_.refs_2_, ...), custom_call_target="tpu_custom_call" | custom-call | flops 1000000 | bytes 1000000 | tf_op jit(solution)/shard_map/attend_back/pallas_call | solution.py:204
  148.2 6.9 %grad_ffn.2 = (bf16[2,192,768]{2,1,0:T(8,128)(2,1)}, bf16[2,192,768]{2,1,0:T(8,128)(2,1)}, bf16[4,192,768]{2,1,0:T(8,128)(2,1)}) custom-call(s32[4]{0:T(128)} %pad_add_fusion.at_ref.refs_0_, bf16[512,1536]{1,0:T(8,128)(2,1)} %get-tuple-element.239.refs_1_, bf16[512,1536]{1,0:T(8,128)(2,1)} %copy-done.2, bf16[512,1536]{1,0:T(8,128)(2,1)} %get-tuple-element.241.refs_3_, ...), custom_call_target="tpu_custom_call" | custom-call | flops 1000000 | bytes 1000000 | tf_op jit(solution)/shard_map/grad_ffn/pallas_call | solution.py:412
  155.1 7.0 %grad_ffn.3 = (bf16[2,192,768]{2,1,0:T(8,128)(2,1)}, bf16[2,192,768]{2,1,0:T(8,128)(2,1)}, bf16[4,192,768]{2,1,0:T(8,128)(2,1)}) custom-call(s32[4]{0:T(128)} %pad_add_fusion.at_ref.refs_0_, bf16[512,1536]{1,0:T(8,128)(2,1)} %get-tuple-element.239.refs_1_, bf16[512,1536]{1,0:T(8,128)(2,1)} %copy-done.2, bf16[512,1536]{1,0:T(8,128)(2,1)} %get-tuple-element.241.refs_3_, ...), custom_call_target="tpu_custom_call" | custom-call | flops 1000000 | bytes 1000000 | tf_op jit(solution)/shard_map/grad_ffn/pallas_call | solution.py:412
  165.2 8.4 %grad_attn.1 = (bf16[2,96,768]{2,1,0:T(8,128)(2,1)}, bf16[2,96,768]{2,1,0:T(8,128)(2,1)}, bf16[4,96,768]{2,1,0:T(8,128)(2,1)}, bf16[2,96,768]{2,1,0:T(8,128)(2,1...) custom-call(s32[4]{0:T(128)} %pad_add_fusion.at_ref.refs_0_, bf16[512,768]{1,0:T(8,128)(2,1)} %tok_ref.3, ...), custom_call_target="tpu_custom_call" | custom-call | flops 1000000 | bytes 1000000 | tf_op jit(solution)/shard_map/grad_attn/pallas_call | solution.py:461
  174.7 15.8 %table_grad.2 = f32[12,160]{1,0:T(8,128)} custom-call(s32[1,512,512]{2,1,0:T(8,128)} %one_ref.3, s32[1,512,512]{2,1,0:T(8,128)} %x_ref.3, s32[1,512,512]{2,1,0:T(8,128)} %y_ref.3, bf16[12,512,512]{2,1,0:T(8,128)(2,1)} %get-tuple-element.275.ds_ref), custom_call_target="tpu_custom_call" | custom-call | flops 1000000 | bytes 1000000 | tf_op jit(solution)/shard_map/table_grad/pallas_call | solution.py:259
  200.8 15.9 %table_grad.3 = f32[12,160]{1,0:T(8,128)} custom-call(s32[1,512,512]{2,1,0:T(8,128)} %one_ref.3, s32[1,512,512]{2,1,0:T(8,128)} %x_ref.3, s32[1,512,512]{2,1,0:T(8,128)} %y_ref.3, bf16[12,512,512]{2,1,0:T(8,128)(2,1)} %get-tuple-element.275.ds_ref), custom_call_target="tpu_custom_call" | custom-call | flops 1000000 | bytes 1000000 | tf_op jit(solution)/shard_map/table_grad/pallas_call | solution.py:259
  219.3 3.2 %collective-permute-start.48 = (bf16[192,768]{1,0:T(8,128)(2,1)}, bf16[192,768]{1,0:T(8,128)(2,1)}, u32[]{:S(2)}, u32[]{:S(2)}) collective-permute-start(bf16[192,768]{1,0:T(8,128)(2,1)} %fusion.11), channel_id=1, source_target_pairs={{0,8},{1,9},{2,10},{3,11},{4,12},{5,13},{6,14},{7,15},{8,0},{9,1},... | collective-permute-start | bytes 884744 | tf_op jit(solution)/shard_map/ppermute | solution.py:658
  229.3 2.2 fusion.6
  233.6 2.1 add_add_fusion
  235.8 3.1 %collective-permute-done.43 = bf16[2,96,768]{2,1,0:T(8,128)(2,1)S(1)} collective-permute-done((bf16[2,96,768]{2,1,0:T(8,128)(2,1)S(1)}, bf16[2,96,768]{2,1,0:T(8,128)(2,1)S(1)}, u32[]{:S(2)}, u32[]{:S(2)}) %collective-permute-start.43) | collective-permute-done | bytes 294944 | tf_op jit(solution)/shard_map/ppermute | solution.py:658
  244.2 1.8 collective-permute-start.46
  255.3 2.8 multiply_reduce_fusion
  258.1 5.6 %collective-permute-done.46 = bf16[96,768]{1,0:T(8,128)(2,1)} collective-permute-done((bf16[96,768]{1,0:T(8,128)(2,1)}, bf16[96,768]{1,0:T(8,128)(2,1)}, u32[]{:S(2)}, u32[]{:S(2)}) %collective-permute-start.46) | collective-permute-done | bytes 147488 | tf_op jit(solution)/shard_map/ppermute | solution.py:658
  263.7 2.3 multiply_reduce_fusion.1
  270.3 2.6 collective-permute-done.52
  273.7 3.3 %collective-permute-done.53 = f32[16,768]{1,0:T(8,128)S(1)} collective-permute-done((f32[16,768]{1,0:T(8,128)S(1)}, f32[16,768]{1,0:T(8,128)S(1)}, u32[]{:S(2)}, u32[]{:S(2)}) %collective-permute-start.53) | collective-permute-done | bytes 49184 | tf_op jit(solution)/shard_map/ppermute | solution.py:658
  277.0 2.1 collective-permute-start.54
  279.1 2.1 collective-permute-done.54
  281.2 3.4 %collective-permute-start.55 = (f32[16,768]{1,0:T(8,128)S(1)}, f32[16,768]{1,0:T(8,128)S(1)}, u32[]{:S(2)}, u32[]{:S(2)}) collective-permute-start(f32[16,768]{1,0:T(8,128)S(1)} %add.135), channel_id=1, source_target_pairs={{0,16},{1,17},{2,18},{3,19},{4,20},{5,21},{6,22},{7,23},{8,24},{9,... | collective-permute-start | bytes 147464 | tf_op jit(solution)/shard_map/ppermute | solution.py:658
  284.6 2.3 fusion
  288.9 5.9 %update.1 = (f32[1,1]{1,0:T(1,128)}, f32[12,768]{1,0:T(8,128)}, f32[96,768]{1,0:T(8,128)}, f32[96,768]{1,0:T(8,128)}, f32[96,768]{1,0:T(8,128)}, /*index=5*/f32[...) custom-call(f32[16,768]{1,0:T(8,128)} %add.136.total_ref, ...), custom_call_target="tpu_custom_call" | custom-call | tf_op jit(solution)/shard_map/update/pallas_call | solution.py:768
  (240 shorter events, 79.4 us)
Async XLA Ops:
  1.7 24.3 %collective-permute-start = (bf16[96,768]{1,0:T(8,128)(2,1)S(1)}, bf16[96,768]{1,0:T(8,128)(2,1)S(1)}, u32[]{:S(2)}, u32[]{:S(2)}) collective-permute-start(bf16[96,768]{1,0:T(8,128)(2,1)S(1)} %convert_element_type.127), channel_id=1, source_target_pairs={{0,8},{1,9},{2,10},{3,11},{4,12},{5,13},{6,14},{7,15},{8,0},{9,1},... | collective-permute-start | bytes 442376 | tf_op jit(solution)/shard_map/ppermute | solution.py:658
  4.8 21.1 %collective-permute-start.1 = (bf16[96,768]{1,0:T(8,128)(2,1)S(1)}, bf16[96,768]{1,0:T(8,128)(2,1)S(1)}, u32[]{:S(2)}, u32[]{:S(2)}) collective-permute-start(bf16[96,768]{1,0:T(8,128)(2,1)S(1)} %convert_element_type.127), channel_id=1, source_target_pairs={{0,16},{1,17},{2,18},{3,19},{4,20},{5,21},{6,22},{7,23},{8,24},{9,... | collective-permute-start | bytes 442376 | tf_op jit(solution)/shard_map/ppermute | solution.py:658
  7.4 18.6 %collective-permute-start.2 = (bf16[96,768]{1,0:T(8,128)(2,1)S(1)}, bf16[96,768]{1,0:T(8,128)(2,1)S(1)}, u32[]{:S(2)}, u32[]{:S(2)}) collective-permute-start(bf16[96,768]{1,0:T(8,128)(2,1)S(1)} %convert_element_type.127), channel_id=1, source_target_pairs={{0,24},{1,25},{2,26},{3,27},{4,28},{5,29},{6,30},{7,31},{8,16},{9,... | collective-permute-start | bytes 442376 | tf_op jit(solution)/shard_map/ppermute | solution.py:658
  8.5 17.5 %collective-permute-start.3 = (bf16[192,768]{1,0:T(8,128)(2,1)S(1)}, bf16[192,768]{1,0:T(8,128)(2,1)S(1)}, u32[]{:S(2)}, u32[]{:S(2)}) collective-permute-start(bf16[192,768]{1,0:T(8,128)(2,1)S(1)} %convert_element_type.128.refs_7_), channel_id=1, source_target_pairs={{0,4},{1,5},{2,6},{3,7},{4,0},{5,1},{6,2},{7,3},{8,12},{9,13},{10,... | collective-permute-start | bytes 884744 | tf_op jit(solution)/shard_map/ppermute | solution.py:658
  10.3 15.8 %collective-permute-start.4 = (bf16[192,768]{1,0:T(8,128)(2,1)S(1)}, bf16[192,768]{1,0:T(8,128)(2,1)S(1)}, u32[]{:S(2)}, u32[]{:S(2)}) collective-permute-start(bf16[192,768]{1,0:T(8,128)(2,1)S(1)} %convert_element_type.128.refs_7_), channel_id=1, source_target_pairs={{0,2},{1,3},{2,0},{3,1},{4,6},{5,7},{6,4},{7,5},{8,10},{9,11},{10,... | collective-permute-start | bytes 884744 | tf_op jit(solution)/shard_map/ppermute | solution.py:658
  26.0 27.6 %collective-permute-start.5 = (bf16[384,768]{1,0:T(8,128)(2,1)S(1)}, bf16[384,768]{1,0:T(8,128)(2,1)S(1)}, u32[]{:S(2)}, u32[]{:S(2)}) collective-permute-start(bf16[384,768]{1,0:T(8,128)(2,1)S(1)} %pad_maximum_fusion.2.refs_0_), channel_id=1, source_target_pairs={{0,4},{1,5},{2,6},{3,7},{4,0},{5,1},{6,2},{7,3},{8,12},{9,13},{10,... | collective-permute-start | bytes 1769480 | tf_op jit(solution)/shard_map/ppermute | solution.py:658
  26.6 27.0 %collective-permute-start.6 = (bf16[384,768]{1,0:T(8,128)(2,1)S(1)}, bf16[384,768]{1,0:T(8,128)(2,1)S(1)}, u32[]{:S(2)}, u32[]{:S(2)}) collective-permute-start(bf16[384,768]{1,0:T(8,128)(2,1)S(1)} %pad_maximum_fusion.2.refs_0_), channel_id=1, source_target_pairs={{0,2},{1,3},{2,0},{3,1},{4,6},{5,7},{6,4},{7,5},{8,10},{9,11},{10,... | collective-permute-start | bytes 1769480 | tf_op jit(solution)/shard_map/ppermute | solution.py:658
  26.9 23.4 %collective-permute-start.7 = (bf16[192,768]{1,0:T(8,128)(2,1)S(1)}, bf16[192,768]{1,0:T(8,128)(2,1)S(1)}, u32[]{:S(2)}, u32[]{:S(2)}) collective-permute-start(bf16[192,768]{1,0:T(8,128)(2,1)S(1)} %convert_element_type.128.refs_7_), channel_id=1, source_target_pairs={{0,8},{1,9},{2,10},{3,11},{4,12},{5,13},{6,14},{7,15},{8,0},{9,1},... | collective-permute-start | bytes 884744 | tf_op jit(solution)/shard_map/ppermute | solution.py:658
  27.8 24.0 %collective-permute-start.8 = (bf16[192,768]{1,0:T(8,128)(2,1)S(1)}, bf16[192,768]{1,0:T(8,128)(2,1)S(1)}, u32[]{:S(2)}, u32[]{:S(2)}) collective-permute-start(bf16[192,768]{1,0:T(8,128)(2,1)S(1)} %convert_element_type.128.refs_7_), channel_id=1, source_target_pairs={{0,16},{1,17},{2,18},{3,19},{4,20},{5,21},{6,22},{7,23},{8,24},{9,... | collective-permute-start | bytes 884744 | tf_op jit(solution)/shard_map/ppermute | solution.py:658
  31.3 21.2 %collective-permute-start.9 = (bf16[192,768]{1,0:T(8,128)(2,1)S(1)}, bf16[192,768]{1,0:T(8,128)(2,1)}, u32[]{:S(2)}, u32[]{:S(2)}) collective-permute-start(bf16[192,768]{1,0:T(8,128)(2,1)S(1)} %convert_element_type.128.refs_7_), channel_id=1, source_target_pairs={{0,24},{1,25},{2,26},{3,27},{4,28},{5,29},{6,30},{7,31},{8,16},{9,... | collective-permute-start | bytes 884744 | tf_op jit(solution)/shard_map/ppermute | solution.py:658
  55.2 13.2 %collective-permute-start.12 = (bf16[1152,768]{1,0:T(8,128)(2,1)}, bf16[1152,768]{1,0:T(8,128)(2,1)}, u32[]{:S(2)}, u32[]{:S(2)}) collective-permute-start(bf16[1152,768]{1,0:T(8,128)(2,1)} %pad_maximum_fusion), channel_id=1, source_target_pairs={{0,1},{1,0},{2,3},{3,2},{4,5},{5,4},{6,7},{7,6},{8,9},{9,8},{10,11... | collective-permute-start | bytes 5308424 | tf_op jit(solution)/shard_map/ppermute | solution.py:658
  59.7 26.8 %collective-permute-start.16 = (bf16[576,768]{1,0:T(8,128)(2,1)S(1)}, bf16[576,768]{1,0:T(8,128)(2,1)S(1)}, u32[]{:S(2)}, u32[]{:S(2)}) collective-permute-start(bf16[576,768]{1,0:T(8,128)(2,1)S(1)} %pad_maximum_fusion.1.refs_10_), channel_id=1, source_target_pairs={{0,4},{1,5},{2,6},{3,7},{4,0},{5,1},{6,2},{7,3},{8,12},{9,13},{10,... | collective-permute-start | bytes 2654216 | tf_op jit(solution)/shard_map/ppermute | solution.py:658
  60.2 26.3 %collective-permute-start.17 = (bf16[576,768]{1,0:T(8,128)(2,1)S(1)}, bf16[576,768]{1,0:T(8,128)(2,1)S(1)}, u32[]{:S(2)}, u32[]{:S(2)}) collective-permute-start(bf16[576,768]{1,0:T(8,128)(2,1)S(1)} %pad_maximum_fusion.1.refs_10_), channel_id=1, source_target_pairs={{0,2},{1,3},{2,0},{3,1},{4,6},{5,7},{6,4},{7,5},{8,10},{9,11},{10,... | collective-permute-start | bytes 2654216 | tf_op jit(solution)/shard_map/ppermute | solution.py:658
  68.9 17.6 %collective-permute-start.13 = (bf16[192,768]{1,0:T(8,128)(2,1)S(1)}, bf16[192,768]{1,0:T(8,128)(2,1)}, u32[]{:S(2)}, u32[]{:S(2)}) collective-permute-start(bf16[192,768]{1,0:T(8,128)(2,1)S(1)} %convert_element_type.128.refs_7_), channel_id=1, source_target_pairs={{0,1},{1,0},{2,3},{3,2},{4,5},{5,4},{6,7},{7,6},{8,9},{9,8},{10,11... | collective-permute-start | bytes 884744 | tf_op jit(solution)/shard_map/ppermute | solution.py:658
  70.7 15.9 %collective-permute-start.14 = (bf16[192,768]{1,0:T(8,128)(2,1)S(1)}, bf16[192,768]{1,0:T(8,128)(2,1)}, u32[]{:S(2)}, u32[]{:S(2)}) collective-permute-start(bf16[192,768]{1,0:T(8,128)(2,1)S(1)} %collective-permute-done.3.refs_8_), channel_id=1, source_target_pairs={{0,1},{1,0},{2,3},{3,2},{4,5},{5,4},{6,7},{7,6},{8,9},{9,8},{10,11... | collective-permute-start | bytes 884744 | tf_op jit(solution)/shard_map/ppermute | solution.py:658
  70.8 15.7 %collective-permute-start.15 = (bf16[192,768]{1,0:T(8,128)(2,1)}, bf16[192,768]{1,0:T(8,128)(2,1)}, u32[]{:S(2)}, u32[]{:S(2)}) collective-permute-start(bf16[192,768]{1,0:T(8,128)(2,1)} %copy-done.28), channel_id=1, source_target_pairs={{0,1},{1,0},{2,3},{3,2},{4,5},{5,4},{6,7},{7,6},{8,9},{9,8},{10,11... | collective-permute-start | bytes 884744 | tf_op jit(solution)/shard_map/ppermute | solution.py:658
  86.5 17.3 %collective-permute-start.22 = (bf16[576,768]{1,0:T(8,128)(2,1)S(1)}, bf16[576,768]{1,0:T(8,128)(2,1)}, u32[]{:S(2)}, u32[]{:S(2)}) collective-permute-start(bf16[576,768]{1,0:T(8,128)(2,1)S(1)} %pad_maximum_fusion.1.refs_10_), channel_id=1, source_target_pairs={{0,1},{1,0},{2,3},{3,2},{4,5},{5,4},{6,7},{7,6},{8,9},{9,8},{10,11... | collective-permute-start | bytes 2654216 | tf_op jit(solution)/shard_map/ppermute | solution.py:658
  86.5 18.6 %collective-permute-start.23 = (bf16[576,768]{1,0:T(8,128)(2,1)S(1)}, bf16[576,768]{1,0:T(8,128)(2,1)}, u32[]{:S(2)}, u32[]{:S(2)}) collective-permute-start(bf16[576,768]{1,0:T(8,128)(2,1)S(1)} %collective-permute-done.16.refs_11_), channel_id=1, source_target_pairs={{0,1},{1,0},{2,3},{3,2},{4,5},{5,4},{6,7},{7,6},{8,9},{9,8},{10,11... | collective-permute-start | bytes 2654216 | tf_op jit(solution)/shard_map/ppermute | solution.py:658
  87.1 18.0 %collective-permute-start.24 = (bf16[576,768]{1,0:T(8,128)(2,1)S(1)}, bf16[576,768]{1,0:T(8,128)(2,1)}, u32[]{:S(2)}, u32[]{:S(2)}) collective-permute-start(bf16[576,768]{1,0:T(8,128)(2,1)S(1)} %collective-permute-done.17.refs_12_), channel_id=1, source_target_pairs={{0,1},{1,0},{2,3},{3,2},{4,5},{5,4},{6,7},{7,6},{8,9},{9,8},{10,11... | collective-permute-start | bytes 2654216 | tf_op jit(solution)/shard_map/ppermute | solution.py:658
  88.9 15.9 %collective-permute-start.20 = (bf16[384,768]{1,0:T(8,128)(2,1)}, bf16[384,768]{1,0:T(8,128)(2,1)S(1)}, u32[]{:S(2)}, u32[]{:S(2)}) collective-permute-start(bf16[384,768]{1,0:T(8,128)(2,1)} %pad_maximum_fusion.3), channel_id=1, source_target_pairs={{0,2},{1,3},{2,0},{3,1},{4,6},{5,7},{6,4},{7,5},{8,10},{9,11},{10,... | collective-permute-start | bytes 1769480 | tf_op jit(solution)/shard_map/ppermute | solution.py:658
  89.4 15.7 %collective-permute-start.21 = (bf16[384,768]{1,0:T(8,128)(2,1)}, bf16[384,768]{1,0:T(8,128)(2,1)}, u32[]{:S(2)}, u32[]{:S(2)}) collective-permute-start(bf16[384,768]{1,0:T(8,128)(2,1)} %slice.126), channel_id=1, source_target_pairs={{0,4},{1,5},{2,6},{3,7},{4,0},{5,1},{6,2},{7,3},{8,12},{9,13},{10,... | collective-permute-start | bytes 1769480 | tf_op jit(solution)/shard_map/ppermute | solution.py:658
  162.1 29.1 %collective-permute-start.40 = (bf16[4,192,768]{2,1,0:T(8,128)(2,1)}, bf16[4,192,768]{2,1,0:T(8,128)(2,1)S(1)}, u32[]{:S(2)}, u32[]{:S(2)}) collective-permute-start(bf16[4,192,768]{2,1,0:T(8,128)(2,1)} %get-tuple-element.270), channel_id=1, source_target_pairs={{0,4},{1,5},{2,6},{3,7},{4,0},{5,1},{6,2},{7,3},{8,12},{9,13},{10,... | collective-permute-start | bytes 3538952 | tf_op jit(solution)/shard_map/ppermute | solution.py:658
  163.7 29.1 %collective-permute-start.39 = (bf16[4,192,768]{2,1,0:T(8,128)(2,1)}, bf16[4,192,768]{2,1,0:T(8,128)(2,1)S(1)}, u32[]{:S(2)}, u32[]{:S(2)}) collective-permute-start(bf16[4,192,768]{2,1,0:T(8,128)(2,1)} %get-tuple-element.269), channel_id=1, source_target_pairs={{0,2},{1,3},{2,0},{3,1},{4,6},{5,7},{6,4},{7,5},{8,10},{9,11},{10,... | collective-permute-start | bytes 3538952 | tf_op jit(solution)/shard_map/ppermute | solution.py:658
  173.6 43.1 %collective-permute-start.37 = (bf16[4,96,768]{2,1,0:T(8,128)(2,1)}, bf16[4,96,768]{2,1,0:T(8,128)(2,1)}, u32[]{:S(2)}, u32[]{:S(2)}) collective-permute-start(bf16[4,96,768]{2,1,0:T(8,128)(2,1)} %get-tuple-element.266), channel_id=1, source_target_pairs={{0,2},{1,3},{2,0},{3,1},{4,6},{5,7},{6,4},{7,5},{8,10},{9,11},{10,... | collective-permute-start | bytes 1769480 | tf_op jit(solution)/shard_map/ppermute | solution.py:658
  174.2 42.5 %collective-permute-start.38 = (bf16[4,96,768]{2,1,0:T(8,128)(2,1)}, bf16[4,96,768]{2,1,0:T(8,128)(2,1)}, u32[]{:S(2)}, u32[]{:S(2)}) collective-permute-start(bf16[4,96,768]{2,1,0:T(8,128)(2,1)} %get-tuple-element.267), channel_id=1, source_target_pairs={{0,4},{1,5},{2,6},{3,7},{4,0},{5,1},{6,2},{7,3},{8,12},{9,13},{10,... | collective-permute-start | bytes 1769480 | tf_op jit(solution)/shard_map/ppermute | solution.py:658
  192.8 24.1 %collective-permute-start.42 = (bf16[2,192,768]{2,1,0:T(8,128)(2,1)S(1)}, bf16[2,192,768]{2,1,0:T(8,128)(2,1)}, u32[]{:S(2)}, u32[]{:S(2)}) collective-permute-start(bf16[2,192,768]{2,1,0:T(8,128)(2,1)S(1)} %add_convert_fusion.1), channel_id=1, source_target_pairs={{0,2},{1,3},{2,0},{3,1},{4,6},{5,7},{6,4},{7,5},{8,10},{9,11},{10,... | collective-permute-start | bytes 1769480 | tf_op jit(solution)/shard_map/ppermute | solution.py:658
  194.6 22.4 %collective-permute-start.41 = (bf16[2,192,768]{2,1,0:T(8,128)(2,1)S(1)}, bf16[2,192,768]{2,1,0:T(8,128)(2,1)}, u32[]{:S(2)}, u32[]{:S(2)}) collective-permute-start(bf16[2,192,768]{2,1,0:T(8,128)(2,1)S(1)} %add_convert_fusion.2), channel_id=1, source_target_pairs={{0,4},{1,5},{2,6},{3,7},{4,0},{5,1},{6,2},{7,3},{8,12},{9,13},{10,... | collective-permute-start | bytes 1769480 | tf_op jit(solution)/shard_map/ppermute | solution.py:658
  219.3 34.4 %collective-permute-start.48 = (bf16[192,768]{1,0:T(8,128)(2,1)}, bf16[192,768]{1,0:T(8,128)(2,1)}, u32[]{:S(2)}, u32[]{:S(2)}) collective-permute-start(bf16[192,768]{1,0:T(8,128)(2,1)} %fusion.11), channel_id=1, source_target_pairs={{0,8},{1,9},{2,10},{3,11},{4,12},{5,13},{6,14},{7,15},{8,0},{9,1},... | collective-permute-start | bytes 884744 | tf_op jit(solution)/shard_map/ppermute | solution.py:658
  224.7 30.6 %collective-permute-start.49 = (bf16[192,768]{1,0:T(8,128)(2,1)}, bf16[192,768]{1,0:T(8,128)(2,1)}, u32[]{:S(2)}, u32[]{:S(2)}) collective-permute-start(bf16[192,768]{1,0:T(8,128)(2,1)} %get-tuple-element.332), channel_id=1, source_target_pairs={{0,16},{1,17},{2,18},{3,19},{4,20},{5,21},{6,22},{7,23},{8,24},{9,... | collective-permute-start | bytes 884744 | tf_op jit(solution)/shard_map/ppermute | solution.py:658
  225.7 29.6 %collective-permute-start.50 = (bf16[192,768]{1,0:T(8,128)(2,1)}, bf16[192,768]{1,0:T(8,128)(2,1)}, u32[]{:S(2)}, u32[]{:S(2)}) collective-permute-start(bf16[192,768]{1,0:T(8,128)(2,1)} %get-tuple-element.333), channel_id=1, source_target_pairs={{0,24},{1,25},{2,26},{3,27},{4,28},{5,29},{6,30},{7,31},{8,16},{9,... | collective-permute-start | bytes 884744 | tf_op jit(solution)/shard_map/ppermute | solution.py:658
  241.3 16.7 %collective-permute-start.45 = (bf16[96,768]{1,0:T(8,128)(2,1)}, bf16[96,768]{1,0:T(8,128)(2,1)S(1)}, u32[]{:S(2)}, u32[]{:S(2)}) collective-permute-start(bf16[96,768]{1,0:T(8,128)(2,1)} %fusion.15), channel_id=1, source_target_pairs={{0,8},{1,9},{2,10},{3,11},{4,12},{5,13},{6,14},{7,15},{8,0},{9,1},... | collective-permute-start | bytes 442376 | tf_op jit(solution)/shard_map/ppermute | solution.py:658
  244.2 19.4 %collective-permute-start.46 = (bf16[96,768]{1,0:T(8,128)(2,1)}, bf16[96,768]{1,0:T(8,128)(2,1)}, u32[]{:S(2)}, u32[]{:S(2)}) collective-permute-start(bf16[96,768]{1,0:T(8,128)(2,1)} %get-tuple-element.334), channel_id=1, source_target_pairs={{0,16},{1,17},{2,18},{3,19},{4,20},{5,21},{6,22},{7,23},{8,24},{9,... | collective-permute-start | bytes 442376 | tf_op jit(solution)/shard_map/ppermute | solution.py:658
  (61 other events, 586.1 us)

commit v2 on v1

--- a/solution.py
+++ b/solution.py
@@ -73,7 +73,7 @@
     lax.fori_loop(0, rows // 8, eight, 0)
 
 
-PARTS = 2
+TABLE_ROWS = ((0, 256), (256, 160), (416, 96))
 BIAS_ROWS = ((0, 128), (128, 320), (448, 64))
 
 
@@ -253,8 +253,7 @@
 
 def table_grad(rel_1d, rel_x, rel_y, d_scores, part):
     rows = 16
-    count = SEQ // rows // PARTS
-    first = part * count
+    first, count = TABLE_ROWS[part][0] // rows, TABLE_ROWS[part][1] // rows
     ids = pl.BlockSpec((1, rows, SEQ), lambda i: (0, first + i, 0))
     return pl.pallas_call(
         table_kernel,
@@ -761,7 +760,7 @@
 def update(total, attn_sum, ffn_sum, states):
     like = lambda a: jax.ShapeDtypeStruct(a.shape, F32)
     one = jax.ShapeDtypeStruct((1, 1), F32)
-    steps = 4 if attn_sum.shape[0] % 32 == 0 else 1
+    steps = 1
     whole = lambda shape: pl.BlockSpec(shape, lambda i: (0, 0))
     part = lambda a: pl.BlockSpec((a.shape[0] // steps, D), lambda i: (i, 0))
     states_specs = [part(a) for a in states[:8]] + [whole(a.shape) for a in states[8:]]
@@ -903,9 +902,10 @@
         sent, d_three = together(scatter_sums(parts[:3], parts[3:], *attn_first), d_three)
         attn_second = scatter_second(*sent)
         grad_input = input_grad(d_resid_one, d_three, attn_full, (0, 1))
-        late = (sums, qv_sums, grad_bias_first, tables, d_three[2])
+        late = (sums, qv_sums, grad_bias_first, tables, d_three[2], d_scores)
         attn_second, grad_input, late = together(attn_second, grad_input, late)
-        sums, qv_sums, grad_bias_first, tables, last_grad = late
+        sums, qv_sums, grad_bias_first, tables, last_grad, d_scores = late
+        tables.append(table_grad(*rel, d_scores, 2))
         grad_input = input_grad(grad_input, (last_grad,), attn_full[2 * D :], (0,))
         attn_own, attn_three = scatter_third(parts[:3], parts[3:], *attn_first, *attn_second)
         ffn_shard = sum((wide(a) for a in ffn_three), ffn_own)
@@ -921,7 +921,7 @@
             parts = grad_attn(spot, tokens, tokens_far, ctx, ctx_far, grads)
             attn_sides.append((parts[:3], parts[3:]))
         ffn_shard, attn_shard = scatter_full(sides), scatter_full(attn_sides)
-        tables = [table_grad(*rel, d_scores, part) for part in range(PARTS)]
+        tables = [table_grad(*rel, d_scores, part) for part in range(len(TABLE_ROWS))]
         grad_input = input_grad(d_resid_one, d_three, attn_full)
     grad_table = pack_table(sum(tables[1:], tables[0]))
     grad_bias_first = grad_bias_first.reshape(2, 2, 2, 2, F_ROWS).transpose(1, 2, 3, 0, 4)

time: 297 us -> 299 us (level)
  waiting for transfers between devices: 37.3 us -> 43.2 us
  starting transfers between devices: 51.7 us -> 46.6 us
    ppermute x56, waiting for transfers between devices: 37.3 us -> 43.2 us  [swap(): return lax.ppermute(array, ALL, [(i, i ^ mask) for i in range(BLOCKS)])]
    ppermute x56, starting transfers between devices: 51.7 us -> 46.6 us  [swap(): return lax.ppermute(array, ALL, [(i, i ^ mask) for i in range(BLOCKS)])]
    pallas_call x2 -> x3, Pallas kernels: 31.7 us -> 33.1 us  [table_grad(): pl.pallas_call(table_kernel, grid=(count,), in_specs=[ids, ids, ids, pl.B...]
  transfers between devices with their start and end apart: 56 -> 56, of which waited for: 19 -> 20; matrix products, arithmetic and copies ran while one was open for 13% -> 13% of each run, Pallas kernels for 38% -> 38%
where the time goes in v2:
time: 299 us; the launch traced here: 297 us
  Pallas kernels  151 us (51%)
  starting transfers between devices  46.6 us (16%)
  waiting for transfers between devices  43.2 us (14%)
  other arithmetic  23.3 us (8%)
  local copies, waits for them, and re-layouts  19 us (6%)
  between operations  7.5 us (3%)
  matrix products  6.69 us (2%)
    ppermute x56, starting transfers between devices, swap(): return lax.ppermute(array, ALL, [(i, i ^ mask) for i in range(BLOCKS)])  46.6 us
    ppermute x56, waiting for transfers between devices, swap(): return lax.ppermute(array, ALL, [(i, i ^ mask) for i in range(BLOCKS)])  43.2 us
    pallas_call x3, Pallas kernels, page_bias(): pl.pallas_call(lambda *refs: bias_kernel(*refs[:5], refs[-1]), grid_spec=...  33.4 us
    pallas_call x3, Pallas kernels, table_grad(): pl.pallas_call(table_kernel, grid=(count,), in_specs=[ids, ids, ids, pl.B...  33.1 us
    pallas_call x1, Pallas kernels, block_pass(): pl.pallas_call(lambda *refs: block_kernel(*refs, wide=768), grid_spec=plt...  25.7 us
    pallas_call x2, Pallas kernels, grad_ffn(): pl.pallas_call(lambda *refs: grad_ffn_kernel(*refs, high=high), in_specs=...  13.8 us
    pallas_call x1, Pallas kernels, attend(): pl.pallas_call(lambda *refs: attend_kernel(*refs, rows=256), grid=(n,), i...  12.9 us
    pallas_call x1, Pallas kernels, attend_back(): pl.pallas_call(lambda *refs: attend_back_kernel(*refs, rows=256), grid=(n...  10.9 us
  transfers between devices with their start and end apart: 56, of which 20 were waited for; matrix products, arithmetic and copies ran while one was open for 13% of the time, Pallas kernels for 38%

profile of v2, /device:TPU:0, one launch (start us, length us, event | category | flops | bytes accessed | tf_op | source)
XLA Modules:
  0.0 297.1 jit_solution(6393691831092833432)
XLA Ops:
  1.7 3.1 %collective-permute-start = (bf16[96,768]{1,0:T(8,128)(2,1)S(1)}, bf16[96,768]{1,0:T(8,128)(2,1)S(1)}, u32[]{:S(2)}, u32[]{:S(2)}) collective-permute-start(bf16[96,768]{1,0:T(8,128)(2,1)S(1)} %convert_element_type.127), channel_id=1, source_target_pairs={{0,8},{1,9},{2,10},{3,11},{4,12},{5,13},{6,14},{7,15},{8,0},{9,1},... | collective-permute-start | bytes 442376 | tf_op jit(solution)/shard_map/ppermute | solution.py:657
  4.8 2.6 collective-permute-start.1
  8.5 1.8 collective-permute-start.3
  16.4 8.9 %bias.3.refs_5_ = f32[12,512,512]{2,1,0:T(8,128)} custom-call(s32[1]{0:T(128)S(6)} %copy.54.refs_0_, f32[12,3,128]{2,1,0:T(4,128)} %copy.44.refs_1_, s32[1,512,512]{2,1,0:T(8,128)} %one_ref.5, s32[1,512,512]{2,1,0:T(8,128)} %x_ref.5, s32[1,512,512]{2,1,0:T(8,128)} %y_ref.5), custom_call_target="tpu_custom_call" | custom-call | flops 1000000 | bytes 1000000 | tf_op jit(solution)/shard_map/bias/pallas_call | solution.py:97
  27.8 3.5 %collective-permute-start.8 = (bf16[192,768]{1,0:T(8,128)(2,1)S(1)}, bf16[192,768]{1,0:T(8,128)(2,1)S(1)}, u32[]{:S(2)}, u32[]{:S(2)}) collective-permute-start(bf16[192,768]{1,0:T(8,128)(2,1)S(1)} %convert_element_type.128.refs_7_), channel_id=1, source_target_pairs={{0,16},{1,17},{2,18},{3,19},{4,20},{5,21},{6,22},{7,23},{8,24},{9,... | collective-permute-start | bytes 884744 | tf_op jit(solution)/shard_map/ppermute | solution.py:657
  31.3 19.0 %bias.4.refs_5_ = f32[12,512,512]{2,1,0:T(8,128)} custom-call(s32[1]{0:T(128)S(6)} %copy.54.refs_0_, f32[12,3,128]{2,1,0:T(4,128)} %copy.44.refs_1_, s32[1,512,512]{2,1,0:T(8,128)} %one_ref.5, s32[1,512,512]{2,1,0:T(8,128)} %x_ref.5, s32[1,512,512]{2,1,0:T(8,128)} %y_ref.5, f32[12,512,512]{2,1,0:T(8,128)} %bias.3.refs_5_), custom_call_target="tpu_custom_call", output_to_operand_aliasing={{}: (5, {})} | custom-call | flops 1000000 | bytes 1000000 | tf_op jit(solution)/shard_map/bias/pallas_call | solution.py:97
  60.7 5.6 %bias.5.refs_3_ = f32[12,512,512]{2,1,0:T(8,128)} custom-call(s32[1]{0:T(128)S(6)} %copy.54.refs_0_, f32[12,3,128]{2,1,0:T(4,128)} %copy.44.refs_1_, s32[1,512,512]{2,1,0:T(8,128)} %one_ref.5, s32[1,512,512]{2,1,0:T(8,128)} %x_ref.5, s32[1,512,512]{2,1,0:T(8,128)} %y_ref.5, f32[12,512,512]{2,1,0:T(8,128)} %bias.4.refs_5_), custom_call_target="tpu_custom_call", output_to_operand_aliasing={{}: (5, {})} | custom-call | flops 1000000 | bytes 1000000 | tf_op jit(solution)/shard_map/bias/pallas_call | solution.py:97
  71.2 7.5 %project.1 = (bf16[512,2304]{1,0:T(8,128)(2,1)}, bf16[3072,768]{1,0:T(8,128)(2,1)}) custom-call(s32[4]{0:T(128)} %pad_add_fusion.at_ref.refs_0_, bf16[512,768]{1,0:T(8,128)(2,1)} %tok_ref.3, f32[1,2304]{1,0:T(1,128)} %reshape.75.add_ref, bf16[384,768]{1,0:T(8,128)(2,1)} %copy-done.3, bf16[384,768]{1,0:T(8,128)(2,1)} %copy-done.4, ...), custom_call_target="tpu_custom_call" | custom-call | flops 1000000 | bytes 1000000 | tf_op jit(solution)/shard_map/project/pallas_call | solution.py:358
  78.7 7.8 %collective-permute-done.16.refs_11_ = bf16[576,768]{1,0:T(8,128)(2,1)S(1)} collective-permute-done((bf16[576,768]{1,0:T(8,128)(2,1)S(1)}, bf16[576,768]{1,0:T(8,128)(2,1)S(1)}, u32[]{:S(2)}, u32[]{:S(2)}) %collective-permute-start.16) | collective-permute-done | bytes 884768 | tf_op jit(solution)/shard_map/ppermute | solution.py:657
  90.9 12.9 %attend.1 = (bf16[512,768]{1,0:T(8,128)(2,1)}, bf16[12,512,512]{2,1,0:T(8,128)(2,1)}) custom-call(bf16[512,2304]{1,0:T(8,128)(2,1)} %get-tuple-element.198.refs_0_.refs_1_.refs_2_, bf16[512,2304]{1,0:T(8,128)(2,1)} %get-tuple-element.198.refs_0_.refs_1_.refs_2_, bf16[512,2304]{1,0:T(8,128)(2,1)} %get-tuple-element.198.refs_0_.refs_1_.refs_2_, ...), custom_call_target="tpu_custom_call" | custom-call | flops 1000000 | bytes 1000000 | tf_op jit(solution)/shard_map/attend/pallas_call | solution.py:149
  108.8 25.7 %block_pass.1 = (bf16[512,768]{1,0:T(8,128)(2,1)}, bf16[512,768]{1,0:T(8,128)(2,1)}, bf16[512,1536]{1,0:T(8,128)(2,1)}, bf16[512,1536]{1,0:T(8,128)(2,1)}, bf16[...) custom-call(s32[4]{0:T(128)} %pad_add_fusion.at_ref.refs_0_, ...), custom_call_target="tpu_custom_call" | custom-call | flops 1000000 | bytes 1000000 | tf_op jit(solution)/shard_map/block_pass/pallas_call | solution.py:601
  135.8 10.9 %attend_back.1 = (bf16[512,768]{1,0:T(8,128)(2,1)}, bf16[512,768]{1,0:T(8,128)(2,1)}, bf16[512,768]{1,0:T(8,128)(2,1)}, bf16[12,512,512]{2,1,0:T(8,128)(2,1)}, f32[8,768]{1,0:T(8,128)}) custom-call(bf16[512,2304]{1,0:T(8,128)(2,1)} %get-tuple-element.198.refs_0_.refs_1_.refs_2_, bf16[512,2304]{1,0:T(8,128)(2,1)} %get-tuple-element.198.refs_0_.refs_1_.refs_2_, ...), custom_call_target="tpu_custom_call" | custom-call | flops 1000000 | bytes 1000000 | tf_op jit(solution)/shard_map/attend_back/pallas_call | solution.py:204
  148.2 6.9 %grad_ffn.2 = (bf16[2,192,768]{2,1,0:T(8,128)(2,1)}, bf16[2,192,768]{2,1,0:T(8,128)(2,1)}, bf16[4,192,768]{2,1,0:T(8,128)(2,1)}) custom-call(s32[4]{0:T(128)} %pad_add_fusion.at_ref.refs_0_, bf16[512,1536]{1,0:T(8,128)(2,1)} %get-tuple-element.240.refs_1_, bf16[512,1536]{1,0:T(8,128)(2,1)} %copy-done.2, bf16[512,1536]{1,0:T(8,128)(2,1)} %get-tuple-element.242.refs_3_, ...), custom_call_target="tpu_custom_call" | custom-call | flops 1000000 | bytes 1000000 | tf_op jit(solution)/shard_map/grad_ffn/pallas_call | solution.py:411
  155.1 7.0 %grad_ffn.3 = (bf16[2,192,768]{2,1,0:T(8,128)(2,1)}, bf16[2,192,768]{2,1,0:T(8,128)(2,1)}, bf16[4,192,768]{2,1,0:T(8,128)(2,1)}) custom-call(s32[4]{0:T(128)} %pad_add_fusion.at_ref.refs_0_, bf16[512,1536]{1,0:T(8,128)(2,1)} %get-tuple-element.240.refs_1_, bf16[512,1536]{1,0:T(8,128)(2,1)} %copy-done.2, bf16[512,1536]{1,0:T(8,128)(2,1)} %get-tuple-element.242.refs_3_, ...), custom_call_target="tpu_custom_call" | custom-call | flops 1000000 | bytes 1000000 | tf_op jit(solution)/shard_map/grad_ffn/pallas_call | solution.py:411
  165.2 8.4 %grad_attn.1 = (bf16[2,96,768]{2,1,0:T(8,128)(2,1)}, bf16[2,96,768]{2,1,0:T(8,128)(2,1)}, bf16[4,96,768]{2,1,0:T(8,128)(2,1)}, bf16[2,96,768]{2,1,0:T(8,128)(2,1...) custom-call(s32[4]{0:T(128)} %pad_add_fusion.at_ref.refs_0_, bf16[512,768]{1,0:T(8,128)(2,1)} %tok_ref.3, ...), custom_call_target="tpu_custom_call" | custom-call | flops 1000000 | bytes 1000000 | tf_op jit(solution)/shard_map/grad_attn/pallas_call | solution.py:460
  174.7 15.8 %table_grad.3 = f32[12,160]{1,0:T(8,128)} custom-call(s32[1,512,512]{2,1,0:T(8,128)} %one_ref.5, s32[1,512,512]{2,1,0:T(8,128)} %x_ref.5, s32[1,512,512]{2,1,0:T(8,128)} %y_ref.5, bf16[12,512,512]{2,1,0:T(8,128)(2,1)} %get-tuple-element.309.ds_ref), custom_call_target="tpu_custom_call" | custom-call | flops 1000000 | bytes 1000000 | tf_op jit(solution)/shard_map/table_grad/pallas_call | solution.py:258
  200.8 10.4 %table_grad.4 = f32[12,160]{1,0:T(8,128)} custom-call(s32[1,512,512]{2,1,0:T(8,128)} %one_ref.5, s32[1,512,512]{2,1,0:T(8,128)} %x_ref.5, s32[1,512,512]{2,1,0:T(8,128)} %y_ref.5, bf16[12,512,512]{2,1,0:T(8,128)(2,1)} %get-tuple-element.309.ds_ref), custom_call_target="tpu_custom_call" | custom-call | flops 1000000 | bytes 1000000 | tf_op jit(solution)/shard_map/table_grad/pallas_call | solution.py:258
  211.2 5.7 %collective-permute-done.42 = bf16[2,192,768]{2,1,0:T(8,128)(2,1)} collective-permute-done((bf16[2,192,768]{2,1,0:T(8,128)(2,1)S(1)}, bf16[2,192,768]{2,1,0:T(8,128)(2,1)}, u32[]{:S(2)}, u32[]{:S(2)}) %collective-permute-start.42) | collective-permute-done | bytes 589856 | tf_op jit(solution)/shard_map/ppermute | solution.py:657
  219.3 3.2 %collective-permute-start.48 = (bf16[192,768]{1,0:T(8,128)(2,1)}, bf16[192,768]{1,0:T(8,128)(2,1)}, u32[]{:S(2)}, u32[]{:S(2)}) collective-permute-start(bf16[192,768]{1,0:T(8,128)(2,1)} %fusion.11), channel_id=1, source_target_pairs={{0,8},{1,9},{2,10},{3,11},{4,12},{5,13},{6,14},{7,15},{8,0},{9,1},... | collective-permute-start | bytes 884744 | tf_op jit(solution)/shard_map/ppermute | solution.py:657
  229.3 2.2 fusion.6
  233.6 2.1 add_add_fusion
  235.8 3.1 %collective-permute-done.43 = bf16[2,96,768]{2,1,0:T(8,128)(2,1)S(1)} collective-permute-done((bf16[2,96,768]{2,1,0:T(8,128)(2,1)S(1)}, bf16[2,96,768]{2,1,0:T(8,128)(2,1)S(1)}, u32[]{:S(2)}, u32[]{:S(2)}) %collective-permute-start.43) | collective-permute-done | bytes 294944 | tf_op jit(solution)/shard_map/ppermute | solution.py:657
  243.8 2.2 collective-permute-start.46
  246.0 6.8 %table_grad.5 = f32[12,160]{1,0:T(8,128)} custom-call(s32[1,512,512]{2,1,0:T(8,128)} %one_ref.5, s32[1,512,512]{2,1,0:T(8,128)} %x_ref.5, s32[1,512,512]{2,1,0:T(8,128)} %y_ref.5, bf16[12,512,512]{2,1,0:T(8,128)(2,1)} %get-tuple-element.309.ds_ref), custom_call_target="tpu_custom_call" | custom-call | flops 1000000 | bytes 1000000 | tf_op jit(solution)/shard_map/table_grad/pallas_call | solution.py:258
  262.7 2.8 multiply_reduce_fusion
  265.5 2.9 collective-permute-done.47
  268.4 2.3 multiply_reduce_fusion.1
  274.8 2.8 collective-permute-done.52
  278.9 2.8 collective-permute-done.53
  281.8 4.1 %collective-permute-done.54 = f32[16,768]{1,0:T(8,128)S(1)} collective-permute-done((f32[16,768]{1,0:T(8,128)S(1)}, f32[16,768]{1,0:T(8,128)S(1)}, u32[]{:S(2)}, u32[]{:S(2)}) %collective-permute-start.54) | collective-permute-done | bytes 49184 | tf_op jit(solution)/shard_map/ppermute | solution.py:657
  286.0 2.3 fusion
  291.9 5.0 %update.1 = (f32[1,1]{1,0:T(1,128)}, f32[12,768]{1,0:T(8,128)}, f32[96,768]{1,0:T(8,128)}, f32[96,768]{1,0:T(8,128)}, f32[96,768]{1,0:T(8,128)}, /*index=5*/f32[...) custom-call(f32[16,768]{1,0:T(8,128)} %add.140.total_ref, ...), custom_call_target="tpu_custom_call" | custom-call | tf_op jit(solution)/shard_map/update/pallas_call | solution.py:767
  (241 shorter events, 81.5 us)
Async XLA Ops:
  1.7 24.3 %collective-permute-start = (bf16[96,768]{1,0:T(8,128)(2,1)S(1)}, bf16[96,768]{1,0:T(8,128)(2,1)S(1)}, u32[]{:S(2)}, u32[]{:S(2)}) collective-permute-start(bf16[96,768]{1,0:T(8,128)(2,1)S(1)} %convert_element_type.127), channel_id=1, source_target_pairs={{0,8},{1,9},{2,10},{3,11},{4,12},{5,13},{6,14},{7,15},{8,0},{9,1},... | collective-permute-start | bytes 442376 | tf_op jit(solution)/shard_map/ppermute | solution.py:657
  4.8 21.1 %collective-permute-start.1 = (bf16[96,768]{1,0:T(8,128)(2,1)S(1)}, bf16[96,768]{1,0:T(8,128)(2,1)S(1)}, u32[]{:S(2)}, u32[]{:S(2)}) collective-permute-start(bf16[96,768]{1,0:T(8,128)(2,1)S(1)} %convert_element_type.127), channel_id=1, source_target_pairs={{0,16},{1,17},{2,18},{3,19},{4,20},{5,21},{6,22},{7,23},{8,24},{9,... | collective-permute-start | bytes 442376 | tf_op jit(solution)/shard_map/ppermute | solution.py:657
  7.4 18.6 %collective-permute-start.2 = (bf16[96,768]{1,0:T(8,128)(2,1)S(1)}, bf16[96,768]{1,0:T(8,128)(2,1)S(1)}, u32[]{:S(2)}, u32[]{:S(2)}) collective-permute-start(bf16[96,768]{1,0:T(8,128)(2,1)S(1)} %convert_element_type.127), channel_id=1, source_target_pairs={{0,24},{1,25},{2,26},{3,27},{4,28},{5,29},{6,30},{7,31},{8,16},{9,... | collective-permute-start | bytes 442376 | tf_op jit(solution)/shard_map/ppermute | solution.py:657
  8.5 17.5 %collective-permute-start.3 = (bf16[192,768]{1,0:T(8,128)(2,1)S(1)}, bf16[192,768]{1,0:T(8,128)(2,1)S(1)}, u32[]{:S(2)}, u32[]{:S(2)}) collective-permute-start(bf16[192,768]{1,0:T(8,128)(2,1)S(1)} %convert_element_type.128.refs_7_), channel_id=1, source_target_pairs={{0,4},{1,5},{2,6},{3,7},{4,0},{5,1},{6,2},{7,3},{8,12},{9,13},{10,... | collective-permute-start | bytes 884744 | tf_op jit(solution)/shard_map/ppermute | solution.py:657
  10.3 15.8 %collective-permute-start.4 = (bf16[192,768]{1,0:T(8,128)(2,1)S(1)}, bf16[192,768]{1,0:T(8,128)(2,1)S(1)}, u32[]{:S(2)}, u32[]{:S(2)}) collective-permute-start(bf16[192,768]{1,0:T(8,128)(2,1)S(1)} %convert_element_type.128.refs_7_), channel_id=1, source_target_pairs={{0,2},{1,3},{2,0},{3,1},{4,6},{5,7},{6,4},{7,5},{8,10},{9,11},{10,... | collective-permute-start | bytes 884744 | tf_op jit(solution)/shard_map/ppermute | solution.py:657
  26.0 27.6 %collective-permute-start.5 = (bf16[384,768]{1,0:T(8,128)(2,1)S(1)}, bf16[384,768]{1,0:T(8,128)(2,1)S(1)}, u32[]{:S(2)}, u32[]{:S(2)}) collective-permute-start(bf16[384,768]{1,0:T(8,128)(2,1)S(1)} %pad_maximum_fusion.2.refs_0_), channel_id=1, source_target_pairs={{0,4},{1,5},{2,6},{3,7},{4,0},{5,1},{6,2},{7,3},{8,12},{9,13},{10,... | collective-permute-start | bytes 1769480 | tf_op jit(solution)/shard_map/ppermute | solution.py:657
  26.6 27.0 %collective-permute-start.6 = (bf16[384,768]{1,0:T(8,128)(2,1)S(1)}, bf16[384,768]{1,0:T(8,128)(2,1)S(1)}, u32[]{:S(2)}, u32[]{:S(2)}) collective-permute-start(bf16[384,768]{1,0:T(8,128)(2,1)S(1)} %pad_maximum_fusion.2.refs_0_), channel_id=1, source_target_pairs={{0,2},{1,3},{2,0},{3,1},{4,6},{5,7},{6,4},{7,5},{8,10},{9,11},{10,... | collective-permute-start | bytes 1769480 | tf_op jit(solution)/shard_map/ppermute | solution.py:657
  26.9 23.4 %collective-permute-start.7 = (bf16[192,768]{1,0:T(8,128)(2,1)S(1)}, bf16[192,768]{1,0:T(8,128)(2,1)S(1)}, u32[]{:S(2)}, u32[]{:S(2)}) collective-permute-start(bf16[192,768]{1,0:T(8,128)(2,1)S(1)} %convert_element_type.128.refs_7_), channel_id=1, source_target_pairs={{0,8},{1,9},{2,10},{3,11},{4,12},{5,13},{6,14},{7,15},{8,0},{9,1},... | collective-permute-start | bytes 884744 | tf_op jit(solution)/shard_map/ppermute | solution.py:657
  27.8 24.0 %collective-permute-start.8 = (bf16[192,768]{1,0:T(8,128)(2,1)S(1)}, bf16[192,768]{1,0:T(8,128)(2,1)S(1)}, u32[]{:S(2)}, u32[]{:S(2)}) collective-permute-start(bf16[192,768]{1,0:T(8,128)(2,1)S(1)} %convert_element_type.128.refs_7_), channel_id=1, source_target_pairs={{0,16},{1,17},{2,18},{3,19},{4,20},{5,21},{6,22},{7,23},{8,24},{9,... | collective-permute-start | bytes 884744 | tf_op jit(solution)/shard_map/ppermute | solution.py:657
  31.3 21.2 %collective-permute-start.9 = (bf16[192,768]{1,0:T(8,128)(2,1)S(1)}, bf16[192,768]{1,0:T(8,128)(2,1)}, u32[]{:S(2)}, u32[]{:S(2)}) collective-permute-start(bf16[192,768]{1,0:T(8,128)(2,1)S(1)} %convert_element_type.128.refs_7_), channel_id=1, source_target_pairs={{0,24},{1,25},{2,26},{3,27},{4,28},{5,29},{6,30},{7,31},{8,16},{9,... | collective-permute-start | bytes 884744 | tf_op jit(solution)/shard_map/ppermute | solution.py:657
  55.2 13.2 %collective-permute-start.12 = (bf16[1152,768]{1,0:T(8,128)(2,1)}, bf16[1152,768]{1,0:T(8,128)(2,1)}, u32[]{:S(2)}, u32[]{:S(2)}) collective-permute-start(bf16[1152,768]{1,0:T(8,128)(2,1)} %pad_maximum_fusion), channel_id=1, source_target_pairs={{0,1},{1,0},{2,3},{3,2},{4,5},{5,4},{6,7},{7,6},{8,9},{9,8},{10,11... | collective-permute-start | bytes 5308424 | tf_op jit(solution)/shard_map/ppermute | solution.py:657
  59.7 26.8 %collective-permute-start.16 = (bf16[576,768]{1,0:T(8,128)(2,1)S(1)}, bf16[576,768]{1,0:T(8,128)(2,1)S(1)}, u32[]{:S(2)}, u32[]{:S(2)}) collective-permute-start(bf16[576,768]{1,0:T(8,128)(2,1)S(1)} %pad_maximum_fusion.1.refs_10_), channel_id=1, source_target_pairs={{0,4},{1,5},{2,6},{3,7},{4,0},{5,1},{6,2},{7,3},{8,12},{9,13},{10,... | collective-permute-start | bytes 2654216 | tf_op jit(solution)/shard_map/ppermute | solution.py:657
  60.2 26.3 %collective-permute-start.17 = (bf16[576,768]{1,0:T(8,128)(2,1)S(1)}, bf16[576,768]{1,0:T(8,128)(2,1)S(1)}, u32[]{:S(2)}, u32[]{:S(2)}) collective-permute-start(bf16[576,768]{1,0:T(8,128)(2,1)S(1)} %pad_maximum_fusion.1.refs_10_), channel_id=1, source_target_pairs={{0,2},{1,3},{2,0},{3,1},{4,6},{5,7},{6,4},{7,5},{8,10},{9,11},{10,... | collective-permute-start | bytes 2654216 | tf_op jit(solution)/shard_map/ppermute | solution.py:657
  68.9 17.6 %collective-permute-start.13 = (bf16[192,768]{1,0:T(8,128)(2,1)S(1)}, bf16[192,768]{1,0:T(8,128)(2,1)}, u32[]{:S(2)}, u32[]{:S(2)}) collective-permute-start(bf16[192,768]{1,0:T(8,128)(2,1)S(1)} %convert_element_type.128.refs_7_), channel_id=1, source_target_pairs={{0,1},{1,0},{2,3},{3,2},{4,5},{5,4},{6,7},{7,6},{8,9},{9,8},{10,11... | collective-permute-start | bytes 884744 | tf_op jit(solution)/shard_map/ppermute | solution.py:657
  70.7 15.9 %collective-permute-start.14 = (bf16[192,768]{1,0:T(8,128)(2,1)S(1)}, bf16[192,768]{1,0:T(8,128)(2,1)}, u32[]{:S(2)}, u32[]{:S(2)}) collective-permute-start(bf16[192,768]{1,0:T(8,128)(2,1)S(1)} %collective-permute-done.3.refs_8_), channel_id=1, source_target_pairs={{0,1},{1,0},{2,3},{3,2},{4,5},{5,4},{6,7},{7,6},{8,9},{9,8},{10,11... | collective-permute-start | bytes 884744 | tf_op jit(solution)/shard_map/ppermute | solution.py:657
  70.8 15.7 %collective-permute-start.15 = (bf16[192,768]{1,0:T(8,128)(2,1)}, bf16[192,768]{1,0:T(8,128)(2,1)}, u32[]{:S(2)}, u32[]{:S(2)}) collective-permute-start(bf16[192,768]{1,0:T(8,128)(2,1)} %copy-done.28), channel_id=1, source_target_pairs={{0,1},{1,0},{2,3},{3,2},{4,5},{5,4},{6,7},{7,6},{8,9},{9,8},{10,11... | collective-permute-start | bytes 884744 | tf_op jit(solution)/shard_map/ppermute | solution.py:657
  86.5 17.3 %collective-permute-start.22 = (bf16[576,768]{1,0:T(8,128)(2,1)S(1)}, bf16[576,768]{1,0:T(8,128)(2,1)}, u32[]{:S(2)}, u32[]{:S(2)}) collective-permute-start(bf16[576,768]{1,0:T(8,128)(2,1)S(1)} %pad_maximum_fusion.1.refs_10_), channel_id=1, source_target_pairs={{0,1},{1,0},{2,3},{3,2},{4,5},{5,4},{6,7},{7,6},{8,9},{9,8},{10,11... | collective-permute-start | bytes 2654216 | tf_op jit(solution)/shard_map/ppermute | solution.py:657
  86.5 18.6 %collective-permute-start.23 = (bf16[576,768]{1,0:T(8,128)(2,1)S(1)}, bf16[576,768]{1,0:T(8,128)(2,1)}, u32[]{:S(2)}, u32[]{:S(2)}) collective-permute-start(bf16[576,768]{1,0:T(8,128)(2,1)S(1)} %collective-permute-done.16.refs_11_), channel_id=1, source_target_pairs={{0,1},{1,0},{2,3},{3,2},{4,5},{5,4},{6,7},{7,6},{8,9},{9,8},{10,11... | collective-permute-start | bytes 2654216 | tf_op jit(solution)/shard_map/ppermute | solution.py:657
  87.1 18.0 %collective-permute-start.24 = (bf16[576,768]{1,0:T(8,128)(2,1)S(1)}, bf16[576,768]{1,0:T(8,128)(2,1)}, u32[]{:S(2)}, u32[]{:S(2)}) collective-permute-start(bf16[576,768]{1,0:T(8,128)(2,1)S(1)} %collective-permute-done.17.refs_12_), channel_id=1, source_target_pairs={{0,1},{1,0},{2,3},{3,2},{4,5},{5,4},{6,7},{7,6},{8,9},{9,8},{10,11... | collective-permute-start | bytes 2654216 | tf_op jit(solution)/shard_map/ppermute | solution.py:657
  88.9 15.9 %collective-permute-start.20 = (bf16[384,768]{1,0:T(8,128)(2,1)}, bf16[384,768]{1,0:T(8,128)(2,1)S(1)}, u32[]{:S(2)}, u32[]{:S(2)}) collective-permute-start(bf16[384,768]{1,0:T(8,128)(2,1)} %pad_maximum_fusion.3), channel_id=1, source_target_pairs={{0,2},{1,3},{2,0},{3,1},{4,6},{5,7},{6,4},{7,5},{8,10},{9,11},{10,... | collective-permute-start | bytes 1769480 | tf_op jit(solution)/shard_map/ppermute | solution.py:657
  89.4 15.7 %collective-permute-start.21 = (bf16[384,768]{1,0:T(8,128)(2,1)}, bf16[384,768]{1,0:T(8,128)(2,1)}, u32[]{:S(2)}, u32[]{:S(2)}) collective-permute-start(bf16[384,768]{1,0:T(8,128)(2,1)} %slice.126), channel_id=1, source_target_pairs={{0,4},{1,5},{2,6},{3,7},{4,0},{5,1},{6,2},{7,3},{8,12},{9,13},{10,... | collective-permute-start | bytes 1769480 | tf_op jit(solution)/shard_map/ppermute | solution.py:657
  162.1 29.1 %collective-permute-start.40 = (bf16[4,192,768]{2,1,0:T(8,128)(2,1)}, bf16[4,192,768]{2,1,0:T(8,128)(2,1)S(1)}, u32[]{:S(2)}, u32[]{:S(2)}) collective-permute-start(bf16[4,192,768]{2,1,0:T(8,128)(2,1)} %get-tuple-element.271), channel_id=1, source_target_pairs={{0,4},{1,5},{2,6},{3,7},{4,0},{5,1},{6,2},{7,3},{8,12},{9,13},{10,... | collective-permute-start | bytes 3538952 | tf_op jit(solution)/shard_map/ppermute | solution.py:657
  163.7 29.1 %collective-permute-start.39 = (bf16[4,192,768]{2,1,0:T(8,128)(2,1)}, bf16[4,192,768]{2,1,0:T(8,128)(2,1)S(1)}, u32[]{:S(2)}, u32[]{:S(2)}) collective-permute-start(bf16[4,192,768]{2,1,0:T(8,128)(2,1)} %get-tuple-element.270), channel_id=1, source_target_pairs={{0,2},{1,3},{2,0},{3,1},{4,6},{5,7},{6,4},{7,5},{8,10},{9,11},{10,... | collective-permute-start | bytes 3538952 | tf_op jit(solution)/shard_map/ppermute | solution.py:657
  173.6 37.7 %collective-permute-start.37 = (bf16[4,96,768]{2,1,0:T(8,128)(2,1)}, bf16[4,96,768]{2,1,0:T(8,128)(2,1)}, u32[]{:S(2)}, u32[]{:S(2)}) collective-permute-start(bf16[4,96,768]{2,1,0:T(8,128)(2,1)} %get-tuple-element.267), channel_id=1, source_target_pairs={{0,2},{1,3},{2,0},{3,1},{4,6},{5,7},{6,4},{7,5},{8,10},{9,11},{10,... | collective-permute-start | bytes 1769480 | tf_op jit(solution)/shard_map/ppermute | solution.py:657
  174.2 37.1 %collective-permute-start.38 = (bf16[4,96,768]{2,1,0:T(8,128)(2,1)}, bf16[4,96,768]{2,1,0:T(8,128)(2,1)}, u32[]{:S(2)}, u32[]{:S(2)}) collective-permute-start(bf16[4,96,768]{2,1,0:T(8,128)(2,1)} %get-tuple-element.268), channel_id=1, source_target_pairs={{0,4},{1,5},{2,6},{3,7},{4,0},{5,1},{6,2},{7,3},{8,12},{9,13},{10,... | collective-permute-start | bytes 1769480 | tf_op jit(solution)/shard_map/ppermute | solution.py:657
  192.8 24.1 %collective-permute-start.42 = (bf16[2,192,768]{2,1,0:T(8,128)(2,1)S(1)}, bf16[2,192,768]{2,1,0:T(8,128)(2,1)}, u32[]{:S(2)}, u32[]{:S(2)}) collective-permute-start(bf16[2,192,768]{2,1,0:T(8,128)(2,1)S(1)} %add_convert_fusion.1), channel_id=1, source_target_pairs={{0,2},{1,3},{2,0},{3,1},{4,6},{5,7},{6,4},{7,5},{8,10},{9,11},{10,... | collective-permute-start | bytes 1769480 | tf_op jit(solution)/shard_map/ppermute | solution.py:657
  194.6 22.4 %collective-permute-start.41 = (bf16[2,192,768]{2,1,0:T(8,128)(2,1)S(1)}, bf16[2,192,768]{2,1,0:T(8,128)(2,1)}, u32[]{:S(2)}, u32[]{:S(2)}) collective-permute-start(bf16[2,192,768]{2,1,0:T(8,128)(2,1)S(1)} %add_convert_fusion.2), channel_id=1, source_target_pairs={{0,4},{1,5},{2,6},{3,7},{4,0},{5,1},{6,2},{7,3},{8,12},{9,13},{10,... | collective-permute-start | bytes 1769480 | tf_op jit(solution)/shard_map/ppermute | solution.py:657
  219.3 41.8 %collective-permute-start.48 = (bf16[192,768]{1,0:T(8,128)(2,1)}, bf16[192,768]{1,0:T(8,128)(2,1)}, u32[]{:S(2)}, u32[]{:S(2)}) collective-permute-start(bf16[192,768]{1,0:T(8,128)(2,1)} %fusion.11), channel_id=1, source_target_pairs={{0,8},{1,9},{2,10},{3,11},{4,12},{5,13},{6,14},{7,15},{8,0},{9,1},... | collective-permute-start | bytes 884744 | tf_op jit(solution)/shard_map/ppermute | solution.py:657
  224.7 38.0 %collective-permute-start.49 = (bf16[192,768]{1,0:T(8,128)(2,1)}, bf16[192,768]{1,0:T(8,128)(2,1)}, u32[]{:S(2)}, u32[]{:S(2)}) collective-permute-start(bf16[192,768]{1,0:T(8,128)(2,1)} %get-tuple-element.334), channel_id=1, source_target_pairs={{0,16},{1,17},{2,18},{3,19},{4,20},{5,21},{6,22},{7,23},{8,24},{9,... | collective-permute-start | bytes 884744 | tf_op jit(solution)/shard_map/ppermute | solution.py:657
  225.7 37.0 %collective-permute-start.50 = (bf16[192,768]{1,0:T(8,128)(2,1)}, bf16[192,768]{1,0:T(8,128)(2,1)}, u32[]{:S(2)}, u32[]{:S(2)}) collective-permute-start(bf16[192,768]{1,0:T(8,128)(2,1)} %get-tuple-element.335), channel_id=1, source_target_pairs={{0,24},{1,25},{2,26},{3,27},{4,28},{5,29},{6,30},{7,31},{8,16},{9,... | collective-permute-start | bytes 884744 | tf_op jit(solution)/shard_map/ppermute | solution.py:657
  241.2 24.3 %collective-permute-start.45 = (bf16[96,768]{1,0:T(8,128)(2,1)}, bf16[96,768]{1,0:T(8,128)(2,1)S(1)}, u32[]{:S(2)}, u32[]{:S(2)}) collective-permute-start(bf16[96,768]{1,0:T(8,128)(2,1)} %fusion.15), channel_id=1, source_target_pairs={{0,8},{1,9},{2,10},{3,11},{4,12},{5,13},{6,14},{7,15},{8,0},{9,1},... | collective-permute-start | bytes 442376 | tf_op jit(solution)/shard_map/ppermute | solution.py:657
  243.8 21.7 %collective-permute-start.46 = (bf16[96,768]{1,0:T(8,128)(2,1)}, bf16[96,768]{1,0:T(8,128)(2,1)}, u32[]{:S(2)}, u32[]{:S(2)}) collective-permute-start(bf16[96,768]{1,0:T(8,128)(2,1)} %get-tuple-element.336), channel_id=1, source_target_pairs={{0,16},{1,17},{2,18},{3,19},{4,20},{5,21},{6,22},{7,23},{8,24},{9,... | collective-permute-start | bytes 442376 | tf_op jit(solution)/shard_map/ppermute | solution.py:657
  (61 other events, 583.4 us)

commit v3 on v1

--- a/solution.py
+++ b/solution.py
@@ -761,7 +761,7 @@
 def update(total, attn_sum, ffn_sum, states):
     like = lambda a: jax.ShapeDtypeStruct(a.shape, F32)
     one = jax.ShapeDtypeStruct((1, 1), F32)
-    steps = 4 if attn_sum.shape[0] % 32 == 0 else 1
+    steps = 1
     whole = lambda shape: pl.BlockSpec(shape, lambda i: (0, 0))
     part = lambda a: pl.BlockSpec((a.shape[0] // steps, D), lambda i: (i, 0))
     states_specs = [part(a) for a in states[:8]] + [whole(a.shape) for a in states[8:]]
@@ -902,11 +902,10 @@
         ffn_own, ffn_three = scatter_third(low, high, *ffn_first, *ffn_second)
         sent, d_three = together(scatter_sums(parts[:3], parts[3:], *attn_first), d_three)
         attn_second = scatter_second(*sent)
-        grad_input = input_grad(d_resid_one, d_three, attn_full, (0, 1))
-        late = (sums, qv_sums, grad_bias_first, tables, d_three[2])
-        attn_second, grad_input, late = together(attn_second, grad_input, late)
-        sums, qv_sums, grad_bias_first, tables, last_grad = late
-        grad_input = input_grad(grad_input, (last_grad,), attn_full[2 * D :], (0,))
+        late = (sums, qv_sums, grad_bias_first, tables, d_three)
+        attn_second, late = together(attn_second, late)
+        sums, qv_sums, grad_bias_first, tables, d_three = late
+        grad_input = input_grad(d_resid_one, d_three, attn_full)
         attn_own, attn_three = scatter_third(parts[:3], parts[3:], *attn_first, *attn_second)
         ffn_shard = sum((wide(a) for a in ffn_three), ffn_own)
         attn_shard = sum((wide(a) for a in attn_three), attn_own)

time: 297 us -> 299 us (level)
  waiting for transfers between devices: 37.3 us -> 44 us
  local copies, waits for them, and re-layouts: 19 us -> 14 us
    ppermute x56, waiting for transfers between devices: 37.3 us -> 44 us  [swap(): return lax.ppermute(array, ALL, [(i, i ^ mask) for i in range(BLOCKS)])]
  transfers between devices with their start and end apart: 56 -> 56, of which waited for: 19 -> 18; matrix products, arithmetic and copies ran while one was open for 13% -> 11% of each run, Pallas kernels for 38% -> 38%
where the time goes in v3:
time: 299 us; the launch traced here: 297 us
  Pallas kernels  149 us (50%)
  starting transfers between devices  52.6 us (18%)
  waiting for transfers between devices  44 us (15%)
  other arithmetic  21.8 us (7%)
  local copies, waits for them, and re-layouts  14 us (5%)
  between operations  7.52 us (3%)
  matrix products  7.43 us (2%)
    ppermute x56, starting transfers between devices, swap(): return lax.ppermute(array, ALL, [(i, i ^ mask) for i in range(BLOCKS)])  52.6 us
    ppermute x56, waiting for transfers between devices, swap(): return lax.ppermute(array, ALL, [(i, i ^ mask) for i in range(BLOCKS)])  44 us
    pallas_call x3, Pallas kernels, page_bias(): pl.pallas_call(lambda *refs: bias_kernel(*refs[:5], refs[-1]), grid_spec=...  33.4 us
    pallas_call x2, Pallas kernels, table_grad(): pl.pallas_call(table_kernel, grid=(count,), in_specs=[ids, ids, ids, pl.B...  31.7 us
    pallas_call x1, Pallas kernels, block_pass(): pl.pallas_call(lambda *refs: block_kernel(*refs, wide=768), grid_spec=plt...  25.8 us
    pallas_call x2, Pallas kernels, grad_ffn(): pl.pallas_call(lambda *refs: grad_ffn_kernel(*refs, high=high), in_specs=...  13.9 us
    pallas_call x1, Pallas kernels, attend(): pl.pallas_call(lambda *refs: attend_kernel(*refs, rows=256), grid=(n,), i...  12.9 us
    pallas_call x1, Pallas kernels, attend_back(): pl.pallas_call(lambda *refs: attend_back_kernel(*refs, rows=256), grid=(n...  10.8 us
  transfers between devices with their start and end apart: 56, of which 18 were waited for; matrix products, arithmetic and copies ran while one was open for 11% of the time, Pallas kernels for 38%

profile of v3, /device:TPU:0, one launch (start us, length us, event | category | flops | bytes accessed | tf_op | source)
XLA Modules:
  0.0 296.7 jit_solution(15556156934465998962)
XLA Ops:
  1.7 3.1 %collective-permute-start = (bf16[96,768]{1,0:T(8,128)(2,1)S(1)}, bf16[96,768]{1,0:T(8,128)(2,1)S(1)}, u32[]{:S(2)}, u32[]{:S(2)}) collective-permute-start(bf16[96,768]{1,0:T(8,128)(2,1)S(1)} %convert_element_type.127), channel_id=1, source_target_pairs={{0,8},{1,9},{2,10},{3,11},{4,12},{5,13},{6,14},{7,15},{8,0},{9,1},... | collective-permute-start | bytes 442376 | tf_op jit(solution)/shard_map/ppermute | solution.py:658
  4.8 2.6 collective-permute-start.1
  8.5 1.8 collective-permute-start.3
  16.4 8.9 %bias.3.refs_5_ = f32[12,512,512]{2,1,0:T(8,128)} custom-call(s32[1]{0:T(128)S(6)} %copy.54.refs_0_, f32[12,3,128]{2,1,0:T(4,128)} %copy.44.refs_1_, s32[1,512,512]{2,1,0:T(8,128)} %one_ref.3, s32[1,512,512]{2,1,0:T(8,128)} %x_ref.3, s32[1,512,512]{2,1,0:T(8,128)} %y_ref.3), custom_call_target="tpu_custom_call" | custom-call | flops 1000000 | bytes 1000000 | tf_op jit(solution)/shard_map/bias/pallas_call | solution.py:97
  27.8 3.5 %collective-permute-start.8 = (bf16[192,768]{1,0:T(8,128)(2,1)S(1)}, bf16[192,768]{1,0:T(8,128)(2,1)S(1)}, u32[]{:S(2)}, u32[]{:S(2)}) collective-permute-start(bf16[192,768]{1,0:T(8,128)(2,1)S(1)} %convert_element_type.128.refs_7_), channel_id=1, source_target_pairs={{0,16},{1,17},{2,18},{3,19},{4,20},{5,21},{6,22},{7,23},{8,24},{9,... | collective-permute-start | bytes 884744 | tf_op jit(solution)/shard_map/ppermute | solution.py:658
  31.3 19.0 %bias.4.refs_5_ = f32[12,512,512]{2,1,0:T(8,128)} custom-call(s32[1]{0:T(128)S(6)} %copy.54.refs_0_, f32[12,3,128]{2,1,0:T(4,128)} %copy.44.refs_1_, s32[1,512,512]{2,1,0:T(8,128)} %one_ref.3, s32[1,512,512]{2,1,0:T(8,128)} %x_ref.3, s32[1,512,512]{2,1,0:T(8,128)} %y_ref.3, f32[12,512,512]{2,1,0:T(8,128)} %bias.3.refs_5_), custom_call_target="tpu_custom_call", output_to_operand_aliasing={{}: (5, {})} | custom-call | flops 1000000 | bytes 1000000 | tf_op jit(solution)/shard_map/bias/pallas_call | solution.py:97
  60.6 5.6 %bias.5.refs_3_ = f32[12,512,512]{2,1,0:T(8,128)} custom-call(s32[1]{0:T(128)S(6)} %copy.54.refs_0_, f32[12,3,128]{2,1,0:T(4,128)} %copy.44.refs_1_, s32[1,512,512]{2,1,0:T(8,128)} %one_ref.3, s32[1,512,512]{2,1,0:T(8,128)} %x_ref.3, s32[1,512,512]{2,1,0:T(8,128)} %y_ref.3, f32[12,512,512]{2,1,0:T(8,128)} %bias.4.refs_5_), custom_call_target="tpu_custom_call", output_to_operand_aliasing={{}: (5, {})} | custom-call | flops 1000000 | bytes 1000000 | tf_op jit(solution)/shard_map/bias/pallas_call | solution.py:97
  66.7 1.6 collective-permute-done.11.refs_4_
  71.1 7.5 %project.1 = (bf16[512,2304]{1,0:T(8,128)(2,1)}, bf16[3072,768]{1,0:T(8,128)(2,1)}) custom-call(s32[4]{0:T(128)} %pad_add_fusion.at_ref.refs_0_, bf16[512,768]{1,0:T(8,128)(2,1)} %tok_ref.3, f32[1,2304]{1,0:T(1,128)} %reshape.75.add_ref, bf16[384,768]{1,0:T(8,128)(2,1)} %copy-done.3, bf16[384,768]{1,0:T(8,128)(2,1)} %copy-done.4, ...), custom_call_target="tpu_custom_call" | custom-call | flops 1000000 | bytes 1000000 | tf_op jit(solution)/shard_map/project/pallas_call | solution.py:359
  78.6 7.8 %collective-permute-done.16.refs_11_ = bf16[576,768]{1,0:T(8,128)(2,1)S(1)} collective-permute-done((bf16[576,768]{1,0:T(8,128)(2,1)S(1)}, bf16[576,768]{1,0:T(8,128)(2,1)S(1)}, u32[]{:S(2)}, u32[]{:S(2)}) %collective-permute-start.16) | collective-permute-done | bytes 884768 | tf_op jit(solution)/shard_map/ppermute | solution.py:658
  90.8 12.9 %attend.1 = (bf16[512,768]{1,0:T(8,128)(2,1)}, bf16[12,512,512]{2,1,0:T(8,128)(2,1)}) custom-call(bf16[512,2304]{1,0:T(8,128)(2,1)} %get-tuple-element.198.refs_0_.refs_1_.refs_2_, bf16[512,2304]{1,0:T(8,128)(2,1)} %get-tuple-element.198.refs_0_.refs_1_.refs_2_, bf16[512,2304]{1,0:T(8,128)(2,1)} %get-tuple-element.198.refs_0_.refs_1_.refs_2_, ...), custom_call_target="tpu_custom_call" | custom-call | flops 1000000 | bytes 1000000 | tf_op jit(solution)/shard_map/attend/pallas_call | solution.py:149
  108.7 25.8 %block_pass.1 = (bf16[512,768]{1,0:T(8,128)(2,1)}, bf16[512,768]{1,0:T(8,128)(2,1)}, bf16[512,1536]{1,0:T(8,128)(2,1)}, bf16[512,1536]{1,0:T(8,128)(2,1)}, bf16[...) custom-call(s32[4]{0:T(128)} %pad_add_fusion.at_ref.refs_0_, ...), custom_call_target="tpu_custom_call" | custom-call | flops 1000000 | bytes 1000000 | tf_op jit(solution)/shard_map/block_pass/pallas_call | solution.py:602
  135.7 10.8 %attend_back.1 = (bf16[512,768]{1,0:T(8,128)(2,1)}, bf16[512,768]{1,0:T(8,128)(2,1)}, bf16[512,768]{1,0:T(8,128)(2,1)}, bf16[12,512,512]{2,1,0:T(8,128)(2,1)}, f32[8,768]{1,0:T(8,128)}) custom-call(bf16[512,2304]{1,0:T(8,128)(2,1)} %get-tuple-element.198.refs_0_.refs_1_.refs_2_, bf16[512,2304]{1,0:T(8,128)(2,1)} %get-tuple-element.198.refs_0_.refs_1_.refs_2_, ...), custom_call_target="tpu_custom_call" | custom-call | flops 1000000 | bytes 1000000 | tf_op jit(solution)/shard_map/attend_back/pallas_call | solution.py:204
  148.1 6.9 %grad_ffn.2 = (bf16[2,192,768]{2,1,0:T(8,128)(2,1)}, bf16[2,192,768]{2,1,0:T(8,128)(2,1)}, bf16[4,192,768]{2,1,0:T(8,128)(2,1)}) custom-call(s32[4]{0:T(128)} %pad_add_fusion.at_ref.refs_0_, bf16[512,1536]{1,0:T(8,128)(2,1)} %get-tuple-element.241.refs_1_, bf16[512,1536]{1,0:T(8,128)(2,1)} %copy-done.2, bf16[512,1536]{1,0:T(8,128)(2,1)} %get-tuple-element.243.refs_3_, ...), custom_call_target="tpu_custom_call" | custom-call | flops 1000000 | bytes 1000000 | tf_op jit(solution)/shard_map/grad_ffn/pallas_call | solution.py:412
  155.1 7.0 %grad_ffn.3 = (bf16[2,192,768]{2,1,0:T(8,128)(2,1)}, bf16[2,192,768]{2,1,0:T(8,128)(2,1)}, bf16[4,192,768]{2,1,0:T(8,128)(2,1)}) custom-call(s32[4]{0:T(128)} %pad_add_fusion.at_ref.refs_0_, bf16[512,1536]{1,0:T(8,128)(2,1)} %get-tuple-element.241.refs_1_, bf16[512,1536]{1,0:T(8,128)(2,1)} %copy-done.2, bf16[512,1536]{1,0:T(8,128)(2,1)} %get-tuple-element.243.refs_3_, ...), custom_call_target="tpu_custom_call" | custom-call | flops 1000000 | bytes 1000000 | tf_op jit(solution)/shard_map/grad_ffn/pallas_call | solution.py:412
  165.1 8.4 %grad_attn.1 = (bf16[2,96,768]{2,1,0:T(8,128)(2,1)}, bf16[2,96,768]{2,1,0:T(8,128)(2,1)}, bf16[4,96,768]{2,1,0:T(8,128)(2,1)}, bf16[2,96,768]{2,1,0:T(8,128)(2,1...) custom-call(s32[4]{0:T(128)} %pad_add_fusion.at_ref.refs_0_, bf16[512,768]{1,0:T(8,128)(2,1)} %tok_ref.3, ...), custom_call_target="tpu_custom_call" | custom-call | flops 1000000 | bytes 1000000 | tf_op jit(solution)/shard_map/grad_attn/pallas_call | solution.py:461
  174.6 15.8 %table_grad.2 = f32[12,160]{1,0:T(8,128)} custom-call(s32[1,512,512]{2,1,0:T(8,128)} %one_ref.3, s32[1,512,512]{2,1,0:T(8,128)} %x_ref.3, s32[1,512,512]{2,1,0:T(8,128)} %y_ref.3, bf16[12,512,512]{2,1,0:T(8,128)(2,1)} %get-tuple-element.277.ds_ref), custom_call_target="tpu_custom_call" | custom-call | flops 1000000 | bytes 1000000 | tf_op jit(solution)/shard_map/table_grad/pallas_call | solution.py:259
  193.9 1.6 collective-permute-start.42
  201.4 15.9 %table_grad.3 = f32[12,160]{1,0:T(8,128)} custom-call(s32[1,512,512]{2,1,0:T(8,128)} %one_ref.3, s32[1,512,512]{2,1,0:T(8,128)} %x_ref.3, s32[1,512,512]{2,1,0:T(8,128)} %y_ref.3, bf16[12,512,512]{2,1,0:T(8,128)(2,1)} %get-tuple-element.277.ds_ref), custom_call_target="tpu_custom_call" | custom-call | flops 1000000 | bytes 1000000 | tf_op jit(solution)/shard_map/table_grad/pallas_call | solution.py:259
  219.6 3.2 %collective-permute-start.48 = (bf16[192,768]{1,0:T(8,128)(2,1)}, bf16[192,768]{1,0:T(8,128)(2,1)S(1)}, u32[]{:S(2)}, u32[]{:S(2)}) collective-permute-start(bf16[192,768]{1,0:T(8,128)(2,1)} %fusion.11), channel_id=1, source_target_pairs={{0,8},{1,9},{2,10},{3,11},{4,12},{5,13},{6,14},{7,15},{8,0},{9,1},... | collective-permute-start | bytes 884744 | tf_op jit(solution)/shard_map/ppermute | solution.py:658
  236.8 2.9 collective-permute-start.46
  244.0 12.2 %collective-permute-done.49 = bf16[192,768]{1,0:T(8,128)(2,1)S(1)} collective-permute-done((bf16[192,768]{1,0:T(8,128)(2,1)}, bf16[192,768]{1,0:T(8,128)(2,1)S(1)}, u32[]{:S(2)}, u32[]{:S(2)}) %collective-permute-start.49) | collective-permute-done | bytes 294944 | tf_op jit(solution)/shard_map/ppermute | solution.py:658
  256.2 2.6 multiply_reduce_fusion
  258.8 6.9 %collective-permute-done.46 = bf16[96,768]{1,0:T(8,128)(2,1)S(1)} collective-permute-done((bf16[96,768]{1,0:T(8,128)(2,1)}, bf16[96,768]{1,0:T(8,128)(2,1)S(1)}, u32[]{:S(2)}, u32[]{:S(2)}) %collective-permute-start.46) | collective-permute-done | bytes 147488 | tf_op jit(solution)/shard_map/ppermute | solution.py:658
  265.7 2.3 multiply_reduce_fusion.1
  272.3 2.6 collective-permute-done.52
  275.9 2.1 fusion.6
  279.1 3.3 %collective-permute-start.54 = (f32[16,768]{1,0:T(8,128)S(1)}, f32[16,768]{1,0:T(8,128)S(1)}, u32[]{:S(2)}, u32[]{:S(2)}) collective-permute-start(f32[16,768]{1,0:T(8,128)S(1)} %add.134), channel_id=1, source_target_pairs={{0,8},{1,9},{2,10},{3,11},{4,12},{5,13},{6,14},{7,15},{8,0},{9,1},... | collective-permute-start | bytes 147464 | tf_op jit(solution)/shard_map/ppermute | solution.py:658
  282.4 2.1 fusion.4
  284.5 3.1 %collective-permute-start.55 = (f32[16,768]{1,0:T(8,128)S(1)}, f32[16,768]{1,0:T(8,128)S(1)}, u32[]{:S(2)}, u32[]{:S(2)}) collective-permute-start(f32[16,768]{1,0:T(8,128)S(1)} %add.135), channel_id=1, source_target_pairs={{0,16},{1,17},{2,18},{3,19},{4,20},{5,21},{6,22},{7,23},{8,24},{9,... | collective-permute-start | bytes 147464 | tf_op jit(solution)/shard_map/ppermute | solution.py:658
  287.6 3.3 %add_add_fusion = f32[512,768]{1,0:T(8,128)} fusion(f32[512,768]{1,0:T(8,128)S(1)} %fusion.4, f32[512,768]{1,0:T(8,128)S(1)} %copy-done.9, f32[512,768]{1,0:T(8,128)S(1)} %fusion.6, bf16[512,768]{1,0:T(8,128)(2,1)S(1)} %copy-done.7, bf16[3072,768]{1,0:T(8,128)(2,1)} %get-tuple-element.203.refs_6_), kind=kOutput, calls=%fused_computation.1 | convolution fusion | flops 605159424 | bytes 8257536 | tf_op jit(solution)/shard_map/dot_general | solution.py:39
  291.5 5.0 %update.1 = (f32[1,1]{1,0:T(1,128)}, f32[12,768]{1,0:T(8,128)}, f32[96,768]{1,0:T(8,128)}, f32[96,768]{1,0:T(8,128)}, f32[96,768]{1,0:T(8,128)}, /*index=5*/f32[...) custom-call(f32[16,768]{1,0:T(8,128)} %add.136.total_ref, ...), custom_call_target="tpu_custom_call" | custom-call | tf_op jit(solution)/shard_map/update/pallas_call | solution.py:768
  (235 shorter events, 71.3 us)
Async XLA Ops:
  1.7 24.2 %collective-permute-start = (bf16[96,768]{1,0:T(8,128)(2,1)S(1)}, bf16[96,768]{1,0:T(8,128)(2,1)S(1)}, u32[]{:S(2)}, u32[]{:S(2)}) collective-permute-start(bf16[96,768]{1,0:T(8,128)(2,1)S(1)} %convert_element_type.127), channel_id=1, source_target_pairs={{0,8},{1,9},{2,10},{3,11},{4,12},{5,13},{6,14},{7,15},{8,0},{9,1},... | collective-permute-start | bytes 442376 | tf_op jit(solution)/shard_map/ppermute | solution.py:658
  4.8 21.1 %collective-permute-start.1 = (bf16[96,768]{1,0:T(8,128)(2,1)S(1)}, bf16[96,768]{1,0:T(8,128)(2,1)S(1)}, u32[]{:S(2)}, u32[]{:S(2)}) collective-permute-start(bf16[96,768]{1,0:T(8,128)(2,1)S(1)} %convert_element_type.127), channel_id=1, source_target_pairs={{0,16},{1,17},{2,18},{3,19},{4,20},{5,21},{6,22},{7,23},{8,24},{9,... | collective-permute-start | bytes 442376 | tf_op jit(solution)/shard_map/ppermute | solution.py:658
  7.4 18.5 %collective-permute-start.2 = (bf16[96,768]{1,0:T(8,128)(2,1)S(1)}, bf16[96,768]{1,0:T(8,128)(2,1)S(1)}, u32[]{:S(2)}, u32[]{:S(2)}) collective-permute-start(bf16[96,768]{1,0:T(8,128)(2,1)S(1)} %convert_element_type.127), channel_id=1, source_target_pairs={{0,24},{1,25},{2,26},{3,27},{4,28},{5,29},{6,30},{7,31},{8,16},{9,... | collective-permute-start | bytes 442376 | tf_op jit(solution)/shard_map/ppermute | solution.py:658
  8.5 17.5 %collective-permute-start.3 = (bf16[192,768]{1,0:T(8,128)(2,1)S(1)}, bf16[192,768]{1,0:T(8,128)(2,1)S(1)}, u32[]{:S(2)}, u32[]{:S(2)}) collective-permute-start(bf16[192,768]{1,0:T(8,128)(2,1)S(1)} %convert_element_type.128.refs_7_), channel_id=1, source_target_pairs={{0,4},{1,5},{2,6},{3,7},{4,0},{5,1},{6,2},{7,3},{8,12},{9,13},{10,... | collective-permute-start | bytes 884744 | tf_op jit(solution)/shard_map/ppermute | solution.py:658
  10.3 15.7 %collective-permute-start.4 = (bf16[192,768]{1,0:T(8,128)(2,1)S(1)}, bf16[192,768]{1,0:T(8,128)(2,1)S(1)}, u32[]{:S(2)}, u32[]{:S(2)}) collective-permute-start(bf16[192,768]{1,0:T(8,128)(2,1)S(1)} %convert_element_type.128.refs_7_), channel_id=1, source_target_pairs={{0,2},{1,3},{2,0},{3,1},{4,6},{5,7},{6,4},{7,5},{8,10},{9,11},{10,... | collective-permute-start | bytes 884744 | tf_op jit(solution)/shard_map/ppermute | solution.py:658
  26.0 27.6 %collective-permute-start.5 = (bf16[384,768]{1,0:T(8,128)(2,1)S(1)}, bf16[384,768]{1,0:T(8,128)(2,1)S(1)}, u32[]{:S(2)}, u32[]{:S(2)}) collective-permute-start(bf16[384,768]{1,0:T(8,128)(2,1)S(1)} %pad_maximum_fusion.2.refs_0_), channel_id=1, source_target_pairs={{0,4},{1,5},{2,6},{3,7},{4,0},{5,1},{6,2},{7,3},{8,12},{9,13},{10,... | collective-permute-start | bytes 1769480 | tf_op jit(solution)/shard_map/ppermute | solution.py:658
  26.6 27.0 %collective-permute-start.6 = (bf16[384,768]{1,0:T(8,128)(2,1)S(1)}, bf16[384,768]{1,0:T(8,128)(2,1)S(1)}, u32[]{:S(2)}, u32[]{:S(2)}) collective-permute-start(bf16[384,768]{1,0:T(8,128)(2,1)S(1)} %pad_maximum_fusion.2.refs_0_), channel_id=1, source_target_pairs={{0,2},{1,3},{2,0},{3,1},{4,6},{5,7},{6,4},{7,5},{8,10},{9,11},{10,... | collective-permute-start | bytes 1769480 | tf_op jit(solution)/shard_map/ppermute | solution.py:658
  26.9 23.4 %collective-permute-start.7 = (bf16[192,768]{1,0:T(8,128)(2,1)S(1)}, bf16[192,768]{1,0:T(8,128)(2,1)S(1)}, u32[]{:S(2)}, u32[]{:S(2)}) collective-permute-start(bf16[192,768]{1,0:T(8,128)(2,1)S(1)} %convert_element_type.128.refs_7_), channel_id=1, source_target_pairs={{0,8},{1,9},{2,10},{3,11},{4,12},{5,13},{6,14},{7,15},{8,0},{9,1},... | collective-permute-start | bytes 884744 | tf_op jit(solution)/shard_map/ppermute | solution.py:658
  27.8 24.0 %collective-permute-start.8 = (bf16[192,768]{1,0:T(8,128)(2,1)S(1)}, bf16[192,768]{1,0:T(8,128)(2,1)S(1)}, u32[]{:S(2)}, u32[]{:S(2)}) collective-permute-start(bf16[192,768]{1,0:T(8,128)(2,1)S(1)} %convert_element_type.128.refs_7_), channel_id=1, source_target_pairs={{0,16},{1,17},{2,18},{3,19},{4,20},{5,21},{6,22},{7,23},{8,24},{9,... | collective-permute-start | bytes 884744 | tf_op jit(solution)/shard_map/ppermute | solution.py:658
  31.3 21.2 %collective-permute-start.9 = (bf16[192,768]{1,0:T(8,128)(2,1)S(1)}, bf16[192,768]{1,0:T(8,128)(2,1)}, u32[]{:S(2)}, u32[]{:S(2)}) collective-permute-start(bf16[192,768]{1,0:T(8,128)(2,1)S(1)} %convert_element_type.128.refs_7_), channel_id=1, source_target_pairs={{0,24},{1,25},{2,26},{3,27},{4,28},{5,29},{6,30},{7,31},{8,16},{9,... | collective-permute-start | bytes 884744 | tf_op jit(solution)/shard_map/ppermute | solution.py:658
  59.6 26.8 %collective-permute-start.16 = (bf16[576,768]{1,0:T(8,128)(2,1)S(1)}, bf16[576,768]{1,0:T(8,128)(2,1)S(1)}, u32[]{:S(2)}, u32[]{:S(2)}) collective-permute-start(bf16[576,768]{1,0:T(8,128)(2,1)S(1)} %pad_maximum_fusion.1.refs_10_), channel_id=1, source_target_pairs={{0,4},{1,5},{2,6},{3,7},{4,0},{5,1},{6,2},{7,3},{8,12},{9,13},{10,... | collective-permute-start | bytes 2654216 | tf_op jit(solution)/shard_map/ppermute | solution.py:658
  60.1 26.3 %collective-permute-start.17 = (bf16[576,768]{1,0:T(8,128)(2,1)S(1)}, bf16[576,768]{1,0:T(8,128)(2,1)S(1)}, u32[]{:S(2)}, u32[]{:S(2)}) collective-permute-start(bf16[576,768]{1,0:T(8,128)(2,1)S(1)} %pad_maximum_fusion.1.refs_10_), channel_id=1, source_target_pairs={{0,2},{1,3},{2,0},{3,1},{4,6},{5,7},{6,4},{7,5},{8,10},{9,11},{10,... | collective-permute-start | bytes 2654216 | tf_op jit(solution)/shard_map/ppermute | solution.py:658
  68.8 17.6 %collective-permute-start.13 = (bf16[192,768]{1,0:T(8,128)(2,1)S(1)}, bf16[192,768]{1,0:T(8,128)(2,1)}, u32[]{:S(2)}, u32[]{:S(2)}) collective-permute-start(bf16[192,768]{1,0:T(8,128)(2,1)S(1)} %convert_element_type.128.refs_7_), channel_id=1, source_target_pairs={{0,1},{1,0},{2,3},{3,2},{4,5},{5,4},{6,7},{7,6},{8,9},{9,8},{10,11... | collective-permute-start | bytes 884744 | tf_op jit(solution)/shard_map/ppermute | solution.py:658
  70.6 15.9 %collective-permute-start.14 = (bf16[192,768]{1,0:T(8,128)(2,1)S(1)}, bf16[192,768]{1,0:T(8,128)(2,1)}, u32[]{:S(2)}, u32[]{:S(2)}) collective-permute-start(bf16[192,768]{1,0:T(8,128)(2,1)S(1)} %collective-permute-done.3.refs_8_), channel_id=1, source_target_pairs={{0,1},{1,0},{2,3},{3,2},{4,5},{5,4},{6,7},{7,6},{8,9},{9,8},{10,11... | collective-permute-start | bytes 884744 | tf_op jit(solution)/shard_map/ppermute | solution.py:658
  70.7 15.7 %collective-permute-start.15 = (bf16[192,768]{1,0:T(8,128)(2,1)}, bf16[192,768]{1,0:T(8,128)(2,1)}, u32[]{:S(2)}, u32[]{:S(2)}) collective-permute-start(bf16[192,768]{1,0:T(8,128)(2,1)} %copy-done.27), channel_id=1, source_target_pairs={{0,1},{1,0},{2,3},{3,2},{4,5},{5,4},{6,7},{7,6},{8,9},{9,8},{10,11... | collective-permute-start | bytes 884744 | tf_op jit(solution)/shard_map/ppermute | solution.py:658
  86.4 17.3 %collective-permute-start.22 = (bf16[576,768]{1,0:T(8,128)(2,1)S(1)}, bf16[576,768]{1,0:T(8,128)(2,1)}, u32[]{:S(2)}, u32[]{:S(2)}) collective-permute-start(bf16[576,768]{1,0:T(8,128)(2,1)S(1)} %pad_maximum_fusion.1.refs_10_), channel_id=1, source_target_pairs={{0,1},{1,0},{2,3},{3,2},{4,5},{5,4},{6,7},{7,6},{8,9},{9,8},{10,11... | collective-permute-start | bytes 2654216 | tf_op jit(solution)/shard_map/ppermute | solution.py:658
  86.5 18.6 %collective-permute-start.23 = (bf16[576,768]{1,0:T(8,128)(2,1)S(1)}, bf16[576,768]{1,0:T(8,128)(2,1)}, u32[]{:S(2)}, u32[]{:S(2)}) collective-permute-start(bf16[576,768]{1,0:T(8,128)(2,1)S(1)} %collective-permute-done.16.refs_11_), channel_id=1, source_target_pairs={{0,1},{1,0},{2,3},{3,2},{4,5},{5,4},{6,7},{7,6},{8,9},{9,8},{10,11... | collective-permute-start | bytes 2654216 | tf_op jit(solution)/shard_map/ppermute | solution.py:658
  87.0 18.0 %collective-permute-start.24 = (bf16[576,768]{1,0:T(8,128)(2,1)S(1)}, bf16[576,768]{1,0:T(8,128)(2,1)}, u32[]{:S(2)}, u32[]{:S(2)}) collective-permute-start(bf16[576,768]{1,0:T(8,128)(2,1)S(1)} %collective-permute-done.17.refs_12_), channel_id=1, source_target_pairs={{0,1},{1,0},{2,3},{3,2},{4,5},{5,4},{6,7},{7,6},{8,9},{9,8},{10,11... | collective-permute-start | bytes 2654216 | tf_op jit(solution)/shard_map/ppermute | solution.py:658
  88.8 15.9 %collective-permute-start.20 = (bf16[384,768]{1,0:T(8,128)(2,1)}, bf16[384,768]{1,0:T(8,128)(2,1)S(1)}, u32[]{:S(2)}, u32[]{:S(2)}) collective-permute-start(bf16[384,768]{1,0:T(8,128)(2,1)} %pad_maximum_fusion.3), channel_id=1, source_target_pairs={{0,2},{1,3},{2,0},{3,1},{4,6},{5,7},{6,4},{7,5},{8,10},{9,11},{10,... | collective-permute-start | bytes 1769480 | tf_op jit(solution)/shard_map/ppermute | solution.py:658
  89.4 15.7 %collective-permute-start.21 = (bf16[384,768]{1,0:T(8,128)(2,1)}, bf16[384,768]{1,0:T(8,128)(2,1)}, u32[]{:S(2)}, u32[]{:S(2)}) collective-permute-start(bf16[384,768]{1,0:T(8,128)(2,1)} %slice.124), channel_id=1, source_target_pairs={{0,4},{1,5},{2,6},{3,7},{4,0},{5,1},{6,2},{7,3},{8,12},{9,13},{10,... | collective-permute-start | bytes 1769480 | tf_op jit(solution)/shard_map/ppermute | solution.py:658
  162.1 29.1 %collective-permute-start.40 = (bf16[4,192,768]{2,1,0:T(8,128)(2,1)}, bf16[4,192,768]{2,1,0:T(8,128)(2,1)S(1)}, u32[]{:S(2)}, u32[]{:S(2)}) collective-permute-start(bf16[4,192,768]{2,1,0:T(8,128)(2,1)} %get-tuple-element.272), channel_id=1, source_target_pairs={{0,4},{1,5},{2,6},{3,7},{4,0},{5,1},{6,2},{7,3},{8,12},{9,13},{10,... | collective-permute-start | bytes 3538952 | tf_op jit(solution)/shard_map/ppermute | solution.py:658
  163.6 29.1 %collective-permute-start.39 = (bf16[4,192,768]{2,1,0:T(8,128)(2,1)}, bf16[4,192,768]{2,1,0:T(8,128)(2,1)S(1)}, u32[]{:S(2)}, u32[]{:S(2)}) collective-permute-start(bf16[4,192,768]{2,1,0:T(8,128)(2,1)} %get-tuple-element.271), channel_id=1, source_target_pairs={{0,2},{1,3},{2,0},{3,1},{4,6},{5,7},{6,4},{7,5},{8,10},{9,11},{10,... | collective-permute-start | bytes 3538952 | tf_op jit(solution)/shard_map/ppermute | solution.py:658
  173.5 43.8 %collective-permute-start.37 = (bf16[4,96,768]{2,1,0:T(8,128)(2,1)}, bf16[4,96,768]{2,1,0:T(8,128)(2,1)}, u32[]{:S(2)}, u32[]{:S(2)}) collective-permute-start(bf16[4,96,768]{2,1,0:T(8,128)(2,1)} %get-tuple-element.268), channel_id=1, source_target_pairs={{0,2},{1,3},{2,0},{3,1},{4,6},{5,7},{6,4},{7,5},{8,10},{9,11},{10,... | collective-permute-start | bytes 1769480 | tf_op jit(solution)/shard_map/ppermute | solution.py:658
  174.1 43.2 %collective-permute-start.38 = (bf16[4,96,768]{2,1,0:T(8,128)(2,1)}, bf16[4,96,768]{2,1,0:T(8,128)(2,1)}, u32[]{:S(2)}, u32[]{:S(2)}) collective-permute-start(bf16[4,96,768]{2,1,0:T(8,128)(2,1)} %get-tuple-element.269), channel_id=1, source_target_pairs={{0,4},{1,5},{2,6},{3,7},{4,0},{5,1},{6,2},{7,3},{8,12},{9,13},{10,... | collective-permute-start | bytes 1769480 | tf_op jit(solution)/shard_map/ppermute | solution.py:658
  193.9 23.5 %collective-permute-start.42 = (bf16[2,192,768]{2,1,0:T(8,128)(2,1)S(1)}, bf16[2,192,768]{2,1,0:T(8,128)(2,1)}, u32[]{:S(2)}, u32[]{:S(2)}) collective-permute-start(bf16[2,192,768]{2,1,0:T(8,128)(2,1)S(1)} %add_convert_fusion.1), channel_id=1, source_target_pairs={{0,2},{1,3},{2,0},{3,1},{4,6},{5,7},{6,4},{7,5},{8,10},{9,11},{10,... | collective-permute-start | bytes 1769480 | tf_op jit(solution)/shard_map/ppermute | solution.py:658
  196.4 20.9 %collective-permute-start.41 = (bf16[2,192,768]{2,1,0:T(8,128)(2,1)}, bf16[2,192,768]{2,1,0:T(8,128)(2,1)}, u32[]{:S(2)}, u32[]{:S(2)}) collective-permute-start(bf16[2,192,768]{2,1,0:T(8,128)(2,1)} %add_convert_fusion.2), channel_id=1, source_target_pairs={{0,4},{1,5},{2,6},{3,7},{4,0},{5,1},{6,2},{7,3},{8,12},{9,13},{10,... | collective-permute-start | bytes 1769480 | tf_op jit(solution)/shard_map/ppermute | solution.py:658
  219.6 22.9 %collective-permute-start.48 = (bf16[192,768]{1,0:T(8,128)(2,1)}, bf16[192,768]{1,0:T(8,128)(2,1)S(1)}, u32[]{:S(2)}, u32[]{:S(2)}) collective-permute-start(bf16[192,768]{1,0:T(8,128)(2,1)} %fusion.11), channel_id=1, source_target_pairs={{0,8},{1,9},{2,10},{3,11},{4,12},{5,13},{6,14},{7,15},{8,0},{9,1},... | collective-permute-start | bytes 884744 | tf_op jit(solution)/shard_map/ppermute | solution.py:658
  229.1 27.1 %collective-permute-start.49 = (bf16[192,768]{1,0:T(8,128)(2,1)}, bf16[192,768]{1,0:T(8,128)(2,1)S(1)}, u32[]{:S(2)}, u32[]{:S(2)}) collective-permute-start(bf16[192,768]{1,0:T(8,128)(2,1)} %get-tuple-element.334), channel_id=1, source_target_pairs={{0,16},{1,17},{2,18},{3,19},{4,20},{5,21},{6,22},{7,23},{8,24},{9,... | collective-permute-start | bytes 884744 | tf_op jit(solution)/shard_map/ppermute | solution.py:658
  230.0 26.2 %collective-permute-start.50 = (bf16[192,768]{1,0:T(8,128)(2,1)}, bf16[192,768]{1,0:T(8,128)(2,1)}, u32[]{:S(2)}, u32[]{:S(2)}) collective-permute-start(bf16[192,768]{1,0:T(8,128)(2,1)} %get-tuple-element.335), channel_id=1, source_target_pairs={{0,24},{1,25},{2,26},{3,27},{4,28},{5,29},{6,30},{7,31},{8,16},{9,... | collective-permute-start | bytes 884744 | tf_op jit(solution)/shard_map/ppermute | solution.py:658
  235.0 23.8 %collective-permute-start.45 = (bf16[96,768]{1,0:T(8,128)(2,1)}, bf16[96,768]{1,0:T(8,128)(2,1)}, u32[]{:S(2)}, u32[]{:S(2)}) collective-permute-start(bf16[96,768]{1,0:T(8,128)(2,1)} %fusion.15), channel_id=1, source_target_pairs={{0,8},{1,9},{2,10},{3,11},{4,12},{5,13},{6,14},{7,15},{8,0},{9,1},... | collective-permute-start | bytes 442376 | tf_op jit(solution)/shard_map/ppermute | solution.py:658
  236.8 28.9 %collective-permute-start.46 = (bf16[96,768]{1,0:T(8,128)(2,1)}, bf16[96,768]{1,0:T(8,128)(2,1)S(1)}, u32[]{:S(2)}, u32[]{:S(2)}) collective-permute-start(bf16[96,768]{1,0:T(8,128)(2,1)} %get-tuple-element.336), channel_id=1, source_target_pairs={{0,16},{1,17},{2,18},{3,19},{4,20},{5,21},{6,22},{7,23},{8,24},{9,... | collective-permute-start | bytes 442376 | tf_op jit(solution)/shard_map/ppermute | solution.py:658
  242.5 23.2 %collective-permute-start.47 = (bf16[96,768]{1,0:T(8,128)(2,1)}, bf16[96,768]{1,0:T(8,128)(2,1)S(1)}, u32[]{:S(2)}, u32[]{:S(2)}) collective-permute-start(bf16[96,768]{1,0:T(8,128)(2,1)} %get-tuple-element.337), channel_id=1, source_target_pairs={{0,24},{1,25},{2,26},{3,27},{4,28},{5,29},{6,30},{7,31},{8,16},{9,... | collective-permute-start | bytes 442376 | tf_op jit(solution)/shard_map/ppermute | solution.py:658
  (59 other events, 594.4 us)
